TPU v7x, 512 devices: a whole 4x4x16 slice. The times are simulated.
512 devices in a mesh: leaf: 32 (over x, y, core), row: 16 (over z).
Axes of the slice: x: 4, y: 4, z: 16, core: 2. Of those that a mesh axis runs over, the one named last changes fastest.
Arguments:
- rhs: bfloat16 [32, 16, 189, 512], P('leaf', 'row'), may hold values from -6 to 6
- inv_diag: bfloat16 [32, 16, 189, 1536], P('leaf', 'row'), may hold values from -0.15625 to 0.15625
- off_diag: bfloat16 [32, 16, 96, 12384], P('leaf', 'row'), may hold values from -0.0390625 to 0.0390625
- pair_mask: int32 [32, 16, 15], P('leaf', 'row'), may hold values 0 or 1
Outputs:
- solution: float32 [32, 16, 189, 512], P('leaf', 'row')
All inputs are finite; a program needn't handle non-finite values. No bound on the sum of `pair_mask` on one device may be relied on, other than what follows from the above.
Results may differ from a plain program's by a relative error of at most 0.0065.
Values may be sent and summed in bfloat16 or wider, within the bound.
No kernel may reach another device: no remote copies, remote signals or barrier semaphores. Data moves between devices by JAX's collectives and lax.ppermute only.
A program may use at most 64 MiB of HBM per device.

v0:
```python
import jax
import jax.numpy as jnp
from jax import lax
from jax.sharding import PartitionSpec as P


def partner_2(block, axis, bit):
    count = lax.axis_size(axis)
    route = []
    for low in range(count):
        high = low | 1 << bit
        if high != low and high < count:
            route += [(low, high), (high, low)]
    return lax.ppermute(block, axis, route)


def from_everyone(array, axis):
    copies = jnp.broadcast_to(array, (lax.axis_size(axis), *array.shape))
    return lax.all_to_all(copies, axis, split_axis=0, concat_axis=0, tiled=True)


def laid_out(pieces, dim):
    dims = list(pieces.shape[1:])
    dims[dim] *= pieces.shape[0]
    return jnp.moveaxis(pieces, 0, dim).reshape(dims)


def gathered_copies(array, axis, dim):
    pieces = from_everyone(array, axis)
    return laid_out(pieces, dim)


def column_start(ancestor, width_all):
    offset = 0
    for higher in range(1, ancestor):
        for within in range(higher):
            offset += width_all // 2**within
    return offset


def shards(rhs, inv_diag, off_diag, pair_mask):
    rows_n = lax.axis_size("row")
    leaves = lax.axis_size("leaf")
    levels_n = leaves.bit_length() - 1
    leaf_index = lax.axis_index("leaf")
    width_all = inv_diag.shape[3]
    right_all = rhs[0, 0]
    inverse_all = inv_diag[0, 0]
    panels = off_diag[0, 0]
    live_pairs = pair_mask[0, 0].astype(jnp.bfloat16)
    known_parts = []
    outputs = []
    offset = 0
    for ancestor in range(levels_n + 1):
        height = width_all // (2**ancestor * rows_n)
        own_rhs = right_all[offset : offset + height]
        own_inv = inverse_all[offset : offset + height]
        offset += height
        if ancestor > 0:
            stacked = jnp.concatenate(
                [
                    known_parts[source] * live_pairs[ancestor * (ancestor - 1) // 2 + source]
                    for source in range(ancestor)
                ],
                axis=0,
            )
            first_col = column_start(ancestor, width_all)
            span_cols = stacked.shape[0]
            update = jnp.dot(
                panels[:, first_col : first_col + span_cols],
                stacked,
                preferred_element_type=jnp.float32,
            )
        if ancestor > 0:
            current = update
            for bit_pos in reversed(range(ancestor)):
                half_rows = current.shape[0] // 2
                upper_half = leaf_index // 2**bit_pos % 2 == 1
                kept_rows = jnp.where(upper_half, current[half_rows:], current[:half_rows])
                sent_rows = jnp.where(upper_half, current[:half_rows], current[half_rows:])
                current = kept_rows + partner_2(
                    sent_rows.astype(jnp.bfloat16), "leaf", bit_pos
                ).astype(sent_rows.dtype)
            reduced = (own_rhs.astype(jnp.float32) - current).astype(jnp.bfloat16)
        else:
            reduced = own_rhs
        gathered = gathered_copies(reduced, "row", 0)
        for bit_pos in range(ancestor):
            partner = partner_2(gathered, "leaf", bit_pos)
            upper_half = leaf_index // 2**bit_pos % 2 == 1
            gathered = jnp.where(
                upper_half,
                jnp.concatenate([partner, gathered], axis=0),
                jnp.concatenate([gathered, partner], axis=0),
            )
        solved = jnp.dot(own_inv, gathered, preferred_element_type=jnp.float32)
        outputs.append(solved)
        if ancestor < levels_n:
            leaf_part = gathered_copies(solved.astype(jnp.bfloat16), "row", 0)
            known_parts.append(leaf_part)
    return jnp.concatenate(outputs, axis=0)[None, None]


def solution(mesh):
    in_specs = (
        P("leaf", "row", None, None),
        P("leaf", "row", None, None),
        P("leaf", "row", None, None),
        P("leaf", "row", None),
    )
    out_specs = P("leaf", "row", None, None)
    return jax.shard_map(shards, mesh=mesh, in_specs=in_specs, out_specs=out_specs, check_vma=False)
```

profile of v0, /device:TPU:1, one launch (start us, length us, event | category | flops | bytes accessed | tf_op | source)
XLA Modules:
  0.0 711.7 jit_solution(17276500015615745266)
XLA Ops:
  1.1 83.6 %all_to_all.55 = bf16[16,96,512]{2,1,0:T(8,128)(2,1)S(1)} all-to-all(bf16[16,96,512]{2,1,0:T(8,128)(2,1)S(1)} %broadcast_in_dim.36), channel_id=1, replica_groups=mesh['leaf'=32,'row'=16] {'row'}, dimensions={0} | all-to-all | bytes 3145728 | tf_op jit(solution)/shard_map/all_to_all | solution.py:19
  87.1 12.5 %all-to-all-start.1 = ((bf16[16,96,512]{2,1,0:T(8,128)(2,1)}), bf16[16,96,512]{2,1,0:T(8,128)(2,1)S(1)}, u32[]{:S(2)}, u32[]{:S(2)}) async-start(bf16[16,96,512]{2,1,0:T(8,128)(2,1)} %broadcast_in_dim.37), calls=%async_computation.1 | async-start | bytes 3145728 | tf_op jit(solution)/shard_map/all_to_all | solution.py:19
  100.4 68.3 %all-to-all-done.1 = bf16[16,96,512]{2,1,0:T(8,128)(2,1)S(1)} async-done(((bf16[16,96,512]{2,1,0:T(8,128)(2,1)}), bf16[16,96,512]{2,1,0:T(8,128)(2,1)S(1)}, u32[]{:S(2)}, u32[]{:S(2)}) %all-to-all-start.1) | async-done | bytes 1572896 | tf_op jit(solution)/shard_map/all_to_all | solution.py:19
  168.6 5.4 broadcast_multiply_fusion
  175.5 8.1 %collective-permute-start = (bf16[48,512]{1,0:T(8,128)(2,1)S(1)}, bf16[48,512]{1,0:T(8,128)(2,1)S(1)}, u32[]{:S(2)}, u32[]{:S(2)}) collective-permute-start(bf16[48,512]{1,0:T(8,128)(2,1)S(1)} %select_convert_fusion.4), channel_id=1, source_target_pairs={{0,16},{16,0},{32,48},{48,32},{64,80},{80,64},{96,112},{112,96},{1... | collective-permute-start | bytes 147464 | tf_op jit(solution)/shard_map/ppermute | solution.py:14
  184.5 41.6 %all_to_all.56 = bf16[16,48,512]{2,1,0:T(8,128)(2,1)S(1)} all-to-all(bf16[16,48,512]{2,1,0:T(8,128)(2,1)S(1)} %broadcast_in_dim.38), channel_id=1, replica_groups=mesh['leaf'=32,'row'=16] {'row'}, dimensions={0} | all-to-all | bytes 1572864 | tf_op jit(solution)/shard_map/all_to_all | solution.py:19
  226.1 8.1 %collective-permute-start.1 = (bf16[768,512]{1,0:T(8,128)(2,1)S(1)}, bf16[768,512]{1,0:T(8,128)(2,1)S(1)}, u32[]{:S(2)}, u32[]{:S(2)}) collective-permute-start(bf16[768,512]{1,0:T(8,128)(2,1)S(1)} %bitcast.114), channel_id=1, source_target_pairs={{0,16},{16,0},{32,48},{48,32},{64,80},{80,64},{96,112},{112,96},{1... | collective-permute-start | bytes 2359304 | tf_op jit(solution)/shard_map/ppermute | solution.py:14
  236.2 2.1 fusion.100
  239.2 5.1 all-to-all-start.3
  244.4 34.2 %all-to-all-done.3 = bf16[16,48,512]{2,1,0:T(8,128)(2,1)S(1)} async-done(((bf16[16,48,512]{2,1,0:T(8,128)(2,1)}), bf16[16,48,512]{2,1,0:T(8,128)(2,1)S(1)}, u32[]{:S(2)}, u32[]{:S(2)}) %all-to-all-start.3) | async-done | bytes 786464 | tf_op jit(solution)/shard_map/all_to_all | solution.py:19
  278.6 3.9 broadcast_multiply_fusion.5
  284.0 3.2 collective-permute-start.2
  288.9 8.9 %collective-permute-start.3 = (bf16[24,512]{1,0:T(8,128)(2,1)S(1)}, bf16[24,512]{1,0:T(8,128)(2,1)S(1)}, u32[]{:S(2)}, u32[]{:S(2)}) collective-permute-start(bf16[24,512]{1,0:T(8,128)(2,1)S(1)} %select_convert_fusion.8), channel_id=1, source_target_pairs={{0,16},{16,0},{32,48},{48,32},{64,80},{80,64},{96,112},{112,96},{1... | collective-permute-start | bytes 73736 | tf_op jit(solution)/shard_map/ppermute | solution.py:14
  298.7 24.4 %all_to_all.57 = bf16[16,24,512]{2,1,0:T(8,128)(2,1)S(1)} all-to-all(bf16[16,24,512]{2,1,0:T(8,128)(2,1)S(1)} %broadcast_in_dim.40), channel_id=1, replica_groups=mesh['leaf'=32,'row'=16] {'row'}, dimensions={0} | all-to-all | bytes 786432 | tf_op jit(solution)/shard_map/all_to_all | solution.py:19
  323.1 9.4 %collective-permute-start.4 = (bf16[384,512]{1,0:T(8,128)(2,1)S(1)}, bf16[384,512]{1,0:T(8,128)(2,1)S(1)}, u32[]{:S(2)}, u32[]{:S(2)}) collective-permute-start(bf16[384,512]{1,0:T(8,128)(2,1)S(1)} %bitcast.106), channel_id=1, source_target_pairs={{0,16},{16,0},{32,48},{48,32},{64,80},{80,64},{96,112},{112,96},{1... | collective-permute-start | bytes 1179656 | tf_op jit(solution)/shard_map/ppermute | solution.py:14
  334.2 3.2 collective-permute-start.5
  337.4 17.4 %collective-permute-done.5 = bf16[768,512]{1,0:T(8,128)(2,1)S(1)} collective-permute-done((bf16[768,512]{1,0:T(8,128)(2,1)S(1)}, bf16[768,512]{1,0:T(8,128)(2,1)S(1)}, u32[]{:S(2)}, u32[]{:S(2)}) %collective-permute-start.5) | collective-permute-done | bytes 786464 | tf_op jit(solution)/shard_map/ppermute | solution.py:14
  357.1 5.5 all-to-all-start.5
  362.6 16.8 %all-to-all-done.5 = bf16[16,24,512]{2,1,0:T(8,128)(2,1)S(1)} async-done(((bf16[16,24,512]{2,1,0:T(8,128)(2,1)}), bf16[16,24,512]{2,1,0:T(8,128)(2,1)S(1)}, u32[]{:S(2)}, u32[]{:S(2)}) %all-to-all-start.5) | async-done | bytes 393248 | tf_op jit(solution)/shard_map/all_to_all | solution.py:19
  379.4 2.8 broadcast_multiply_fusion.9
  384.1 4.8 collective-permute-start.6
  390.5 3.2 collective-permute-start.7
  395.1 11.5 %collective-permute-start.8 = (bf16[12,512]{1,0:T(8,128)(2,1)S(1)}, bf16[12,512]{1,0:T(8,128)(2,1)S(1)}, u32[]{:S(2)}, u32[]{:S(2)}) collective-permute-start(bf16[12,512]{1,0:T(8,128)(2,1)S(1)} %select_convert_fusion.11), channel_id=1, source_target_pairs={{0,16},{16,0},{32,48},{48,32},{64,80},{80,64},{96,112},{112,96},{1... | collective-permute-start | bytes 36872 | tf_op jit(solution)/shard_map/ppermute | solution.py:14
  407.5 20.2 %all_to_all.58 = bf16[16,12,512]{2,1,0:T(8,128)(2,1)S(1)} all-to-all(bf16[16,12,512]{2,1,0:T(8,128)(2,1)S(1)} %broadcast_in_dim.42), channel_id=1, replica_groups=mesh['leaf'=32,'row'=16] {'row'}, dimensions={0} | all-to-all | bytes 393216 | tf_op jit(solution)/shard_map/all_to_all | solution.py:19
  427.7 7.0 collective-permute-start.9
  435.9 3.2 collective-permute-start.10
  439.1 9.0 %collective-permute-done.10 = bf16[384,512]{1,0:T(8,128)(2,1)S(1)} collective-permute-done((bf16[384,512]{1,0:T(8,128)(2,1)S(1)}, bf16[384,512]{1,0:T(8,128)(2,1)S(1)}, u32[]{:S(2)}, u32[]{:S(2)}) %collective-permute-start.10) | collective-permute-done | bytes 393248 | tf_op jit(solution)/shard_map/ppermute | solution.py:14
  448.4 4.8 collective-permute-start.11
  453.2 16.4 %collective-permute-done.11 = bf16[768,512]{1,0:T(8,128)(2,1)S(1)} collective-permute-done((bf16[768,512]{1,0:T(8,128)(2,1)S(1)}, bf16[768,512]{1,0:T(8,128)(2,1)S(1)}, u32[]{:S(2)}, u32[]{:S(2)}) %collective-permute-start.11) | collective-permute-done | bytes 786464 | tf_op jit(solution)/shard_map/ppermute | solution.py:14
  471.8 5.7 all-to-all-start.7
  477.5 12.7 %all-to-all-done.7 = bf16[16,12,512]{2,1,0:T(8,128)(2,1)S(1)} async-done(((bf16[16,12,512]{2,1,0:T(8,128)(2,1)}), bf16[16,12,512]{2,1,0:T(8,128)(2,1)S(1)}, u32[]{:S(2)}, u32[]{:S(2)}) %all-to-all-start.7) | async-done | bytes 196640 | tf_op jit(solution)/shard_map/all_to_all | solution.py:19
  490.2 2.0 broadcast_multiply_fusion.12
  492.3 2.0 fusion.59
  494.4 3.1 collective-permute-start.12
  499.2 4.8 collective-permute-start.13
  505.4 3.2 collective-permute-start.14
  509.9 12.3 %collective-permute-start.15 = (bf16[6,512]{1,0:T(8,128)(2,1)S(1)}, bf16[6,512]{1,0:T(8,128)(2,1)S(1)}, u32[]{:S(2)}, u32[]{:S(2)}) collective-permute-start(bf16[6,512]{1,0:T(8,128)(2,1)S(1)} %select_convert_fusion.13), channel_id=1, source_target_pairs={{0,16},{16,0},{32,48},{48,32},{64,80},{80,64},{96,112},{112,96},{1... | collective-permute-start | bytes 18440 | tf_op jit(solution)/shard_map/ppermute | solution.py:14
  523.0 17.1 %all_to_all.59 = bf16[16,6,512]{2,1,0:T(8,128)(2,1)S(1)} all-to-all(bf16[16,6,512]{2,1,0:T(8,128)(2,1)S(1)} %broadcast_in_dim.44), channel_id=1, replica_groups=mesh['leaf'=32,'row'=16] {'row'}, dimensions={0} | all-to-all | bytes 196608 | tf_op jit(solution)/shard_map/all_to_all | solution.py:19
  540.1 5.2 collective-permute-start.16
  546.3 3.3 collective-permute-start.17
  549.6 4.6 collective-permute-done.17
  554.4 4.8 collective-permute-start.18
  559.2 8.0 %collective-permute-done.18 = bf16[384,512]{1,0:T(8,128)(2,1)S(1)} collective-permute-done((bf16[384,512]{1,0:T(8,128)(2,1)S(1)}, bf16[384,512]{1,0:T(8,128)(2,1)S(1)}, u32[]{:S(2)}, u32[]{:S(2)}) %collective-permute-start.18) | collective-permute-done | bytes 393248 | tf_op jit(solution)/shard_map/ppermute | solution.py:14
  568.4 3.1 collective-permute-start.19
  573.1 14.6 %collective-permute-done.19 = bf16[768,512]{1,0:T(8,128)(2,1)} collective-permute-done((bf16[768,512]{1,0:T(8,128)(2,1)}, bf16[768,512]{1,0:T(8,128)(2,1)}, u32[]{:S(2)}, u32[]{:S(2)}) %collective-permute-start.19) | collective-permute-done | bytes 786464 | tf_op jit(solution)/shard_map/ppermute | solution.py:14
  587.7 2.3 fusion.103
  590.7 4.2 all-to-all-start.9
  597.1 9.7 %all-to-all-done.9 = bf16[16,6,512]{2,1,0:T(8,128)(2,1)} async-done(((bf16[16,6,512]{2,1,0:T(8,128)(2,1)}), bf16[16,6,512]{2,1,0:T(8,128)(2,1)}, u32[]{:S(2)}, u32[]{:S(2)}) %all-to-all-start.9) | async-done | bytes 98336 | tf_op jit(solution)/shard_map/all_to_all | solution.py:19
  610.2 4.6 collective-permute-start.20
  616.6 3.1 collective-permute-start.21
  619.7 1.9 collective-permute-done.21
  621.6 4.8 collective-permute-start.22
  627.6 3.3 collective-permute-start.23
  632.1 10.4 %collective-permute-start.24 = (bf16[3,512]{1,0:T(4,128)(2,1)S(1)}, bf16[3,512]{1,0:T(4,128)(2,1)S(1)}, u32[]{:S(2)}, u32[]{:S(2)}) collective-permute-start(bf16[3,512]{1,0:T(4,128)(2,1)S(1)} %select_convert_fusion.14), channel_id=1, source_target_pairs={{0,16},{16,0},{32,48},{48,32},{64,80},{80,64},{96,112},{112,96},{1... | collective-permute-start | bytes 9224 | tf_op jit(solution)/shard_map/ppermute | solution.py:14
  644.0 15.1 %all_to_all.60 = bf16[16,3,512]{2,1,0:T(4,128)(2,1)S(1)} all-to-all(bf16[16,3,512]{2,1,0:T(4,128)(2,1)S(1)} %broadcast_in_dim.46), channel_id=1, replica_groups=mesh['leaf'=32,'row'=16] {'row'}, dimensions={0} | all-to-all | bytes 98304 | tf_op jit(solution)/shard_map/all_to_all | solution.py:19
  659.1 3.9 collective-permute-start.25
  663.9 3.3 collective-permute-start.26
  667.3 2.5 collective-permute-done.26
  669.9 4.8 collective-permute-start.27
  674.7 3.8 collective-permute-done.27
  678.6 3.1 collective-permute-start.28
  681.8 7.4 %collective-permute-done.28 = bf16[384,512]{1,0:T(8,128)(2,1)S(1)} collective-permute-done((bf16[384,512]{1,0:T(8,128)(2,1)S(1)}, bf16[384,512]{1,0:T(8,128)(2,1)S(1)}, u32[]{:S(2)}, u32[]{:S(2)}) %collective-permute-start.28) | collective-permute-done | bytes 393248 | tf_op jit(solution)/shard_map/ppermute | solution.py:14
  689.5 4.9 collective-permute-start.29
  694.4 14.8 %collective-permute-done.29 = bf16[768,512]{1,0:T(8,128)(2,1)S(1)} collective-permute-done((bf16[768,512]{1,0:T(8,128)(2,1)S(1)}, bf16[768,512]{1,0:T(8,128)(2,1)S(1)}, u32[]{:S(2)}, u32[]{:S(2)}) %collective-permute-start.29) | collective-permute-done | bytes 786464 | tf_op jit(solution)/shard_map/ppermute | solution.py:14
  (109 shorter events, 51.4 us)
Async XLA Ops:
  1.1 83.6 %copy-start.4 = (bf16[1,1,189,1536]{3,2,1,0:T(8,128)(2,1)S(1)}, bf16[1,1,189,1536]{3,2,1,0:T(8,128)(2,1)}, u32[]{:S(2)}) copy-start(bf16[1,1,189,1536]{3,2,1,0:T(8,128)(2,1)} %param.5) | copy-start | bytes 1741828
  87.1 12.5 %copy-start.6 = (s32[1,1,15]{2,1,0:T(1,128)S(1)}, s32[1,1,15]{2,1,0:T(1,128)}, u32[]{:S(2)}) copy-start(s32[1,1,15]{2,1,0:T(1,128)} %param.7) | copy-start | bytes 184
  87.1 81.5 %all-to-all-start.1 = ((bf16[16,96,512]{2,1,0:T(8,128)(2,1)}), bf16[16,96,512]{2,1,0:T(8,128)(2,1)S(1)}, u32[]{:S(2)}, u32[]{:S(2)}) async-start(bf16[16,96,512]{2,1,0:T(8,128)(2,1)} %broadcast_in_dim.37), calls=%async_computation.1 | async-start | bytes 3145728 | tf_op jit(solution)/shard_map/all_to_all | solution.py:19
  174.1 10.4 %copy-start.3 = (bf16[1,1,189,512]{3,2,1,0:T(8,128)(2,1)S(1)}, bf16[1,1,189,512]{3,2,1,0:T(8,128)(2,1)}, u32[]{:S(2)}) copy-start(bf16[1,1,189,512]{3,2,1,0:T(8,128)(2,1)} %param.4) | copy-start | bytes 580612
  175.5 8.9 %collective-permute-start = (bf16[48,512]{1,0:T(8,128)(2,1)S(1)}, bf16[48,512]{1,0:T(8,128)(2,1)S(1)}, u32[]{:S(2)}, u32[]{:S(2)}) collective-permute-start(bf16[48,512]{1,0:T(8,128)(2,1)S(1)} %select_convert_fusion.4), channel_id=1, source_target_pairs={{0,16},{16,0},{32,48},{48,32},{64,80},{80,64},{96,112},{112,96},{1... | collective-permute-start | bytes 147464 | tf_op jit(solution)/shard_map/ppermute | solution.py:14
  226.1 10.0 %collective-permute-start.1 = (bf16[768,512]{1,0:T(8,128)(2,1)S(1)}, bf16[768,512]{1,0:T(8,128)(2,1)S(1)}, u32[]{:S(2)}, u32[]{:S(2)}) collective-permute-start(bf16[768,512]{1,0:T(8,128)(2,1)S(1)} %bitcast.114), channel_id=1, source_target_pairs={{0,16},{16,0},{32,48},{48,32},{64,80},{80,64},{96,112},{112,96},{1... | collective-permute-start | bytes 2359304 | tf_op jit(solution)/shard_map/ppermute | solution.py:14
  239.2 39.3 %all-to-all-start.3 = ((bf16[16,48,512]{2,1,0:T(8,128)(2,1)}), bf16[16,48,512]{2,1,0:T(8,128)(2,1)S(1)}, u32[]{:S(2)}, u32[]{:S(2)}) async-start(bf16[16,48,512]{2,1,0:T(8,128)(2,1)} %broadcast_in_dim.39), calls=%async_computation.3 | async-start | bytes 1572864 | tf_op jit(solution)/shard_map/all_to_all | solution.py:19
  284.0 4.8 collective-permute-start.2
  288.9 9.8 %collective-permute-start.3 = (bf16[24,512]{1,0:T(8,128)(2,1)S(1)}, bf16[24,512]{1,0:T(8,128)(2,1)S(1)}, u32[]{:S(2)}, u32[]{:S(2)}) collective-permute-start(bf16[24,512]{1,0:T(8,128)(2,1)S(1)} %select_convert_fusion.8), channel_id=1, source_target_pairs={{0,16},{16,0},{32,48},{48,32},{64,80},{80,64},{96,112},{112,96},{1... | collective-permute-start | bytes 73736 | tf_op jit(solution)/shard_map/ppermute | solution.py:14
  323.1 10.7 %collective-permute-start.4 = (bf16[384,512]{1,0:T(8,128)(2,1)S(1)}, bf16[384,512]{1,0:T(8,128)(2,1)S(1)}, u32[]{:S(2)}, u32[]{:S(2)}) collective-permute-start(bf16[384,512]{1,0:T(8,128)(2,1)S(1)} %bitcast.106), channel_id=1, source_target_pairs={{0,16},{16,0},{32,48},{48,32},{64,80},{80,64},{96,112},{112,96},{1... | collective-permute-start | bytes 1179656 | tf_op jit(solution)/shard_map/ppermute | solution.py:14
  334.2 20.6 %collective-permute-start.5 = (bf16[768,512]{1,0:T(8,128)(2,1)S(1)}, bf16[768,512]{1,0:T(8,128)(2,1)S(1)}, u32[]{:S(2)}, u32[]{:S(2)}) collective-permute-start(bf16[768,512]{1,0:T(8,128)(2,1)S(1)} %maximum_select_fusion.20), channel_id=1, source_target_pairs={{0,32},{32,0},{16,48},{48,16},{64,96},{96,64},{80,112},{112,80},{1... | collective-permute-start | bytes 2359304 | tf_op jit(solution)/shard_map/ppermute | solution.py:14
  356.3 25.9 %copy-start.1 = (bf16[16,96,512]{2,1,0:T(8,128)(2,1)S(1)}, bf16[16,96,512]{2,1,0:T(8,128)(2,1)}, u32[]{:S(2)}) copy-start(bf16[16,96,512]{2,1,0:T(8,128)(2,1)} %get-tuple-element.7) | copy-start | bytes 4718596
  357.1 22.3 %all-to-all-start.5 = ((bf16[16,24,512]{2,1,0:T(8,128)(2,1)}), bf16[16,24,512]{2,1,0:T(8,128)(2,1)S(1)}, u32[]{:S(2)}, u32[]{:S(2)}) async-start(bf16[16,24,512]{2,1,0:T(8,128)(2,1)} %broadcast_in_dim.41), calls=%async_computation.5 | async-start | bytes 786432 | tf_op jit(solution)/shard_map/all_to_all | solution.py:19
  384.1 6.3 collective-permute-start.6
  390.5 4.6 collective-permute-start.7
  395.1 12.3 %collective-permute-start.8 = (bf16[12,512]{1,0:T(8,128)(2,1)S(1)}, bf16[12,512]{1,0:T(8,128)(2,1)S(1)}, u32[]{:S(2)}, u32[]{:S(2)}) collective-permute-start(bf16[12,512]{1,0:T(8,128)(2,1)S(1)} %select_convert_fusion.11), channel_id=1, source_target_pairs={{0,16},{16,0},{32,48},{48,32},{64,80},{80,64},{96,112},{112,96},{1... | collective-permute-start | bytes 36872 | tf_op jit(solution)/shard_map/ppermute | solution.py:14
  427.7 8.1 %collective-permute-start.9 = (bf16[192,512]{1,0:T(8,128)(2,1)S(1)}, bf16[192,512]{1,0:T(8,128)(2,1)S(1)}, u32[]{:S(2)}, u32[]{:S(2)}) collective-permute-start(bf16[192,512]{1,0:T(8,128)(2,1)S(1)} %reshape.109), channel_id=1, source_target_pairs={{0,16},{16,0},{32,48},{48,32},{64,80},{80,64},{96,112},{112,96},{1... | collective-permute-start | bytes 589832 | tf_op jit(solution)/shard_map/ppermute | solution.py:14
  435.9 12.2 %collective-permute-start.10 = (bf16[384,512]{1,0:T(8,128)(2,1)S(1)}, bf16[384,512]{1,0:T(8,128)(2,1)S(1)}, u32[]{:S(2)}, u32[]{:S(2)}) collective-permute-start(bf16[384,512]{1,0:T(8,128)(2,1)S(1)} %maximum_select_fusion.24), channel_id=1, source_target_pairs={{0,32},{32,0},{16,48},{48,16},{64,96},{96,64},{80,112},{112,80},{1... | collective-permute-start | bytes 1179656 | tf_op jit(solution)/shard_map/ppermute | solution.py:14
  448.4 21.3 %collective-permute-start.11 = (bf16[768,512]{1,0:T(8,128)(2,1)S(1)}, bf16[768,512]{1,0:T(8,128)(2,1)S(1)}, u32[]{:S(2)}, u32[]{:S(2)}) collective-permute-start(bf16[768,512]{1,0:T(8,128)(2,1)S(1)} %maximum_select_fusion.21), channel_id=1, source_target_pairs={{0,64},{64,0},{16,80},{80,16},{32,96},{96,32},{48,112},{112,48},{1... | collective-permute-start | bytes 2359304 | tf_op jit(solution)/shard_map/ppermute | solution.py:14
  471.1 21.3 %copy-start = (bf16[16,96,512]{2,1,0:T(8,128)(2,1)S(1)}, bf16[16,96,512]{2,1,0:T(8,128)(2,1)}, u32[]{:S(2)}) copy-start(bf16[16,96,512]{2,1,0:T(8,128)(2,1)} %get-tuple-element.6) | copy-start | bytes 4718596
  471.8 18.4 %all-to-all-start.7 = ((bf16[16,12,512]{2,1,0:T(8,128)(2,1)}), bf16[16,12,512]{2,1,0:T(8,128)(2,1)S(1)}, u32[]{:S(2)}, u32[]{:S(2)}) async-start(bf16[16,12,512]{2,1,0:T(8,128)(2,1)} %broadcast_in_dim.43), calls=%async_computation.7 | async-start | bytes 524288 | tf_op jit(solution)/shard_map/all_to_all | solution.py:19
  494.4 4.8 collective-permute-start.12
  499.2 6.1 collective-permute-start.13
  505.4 4.5 collective-permute-start.14
  509.9 13.1 %collective-permute-start.15 = (bf16[6,512]{1,0:T(8,128)(2,1)S(1)}, bf16[6,512]{1,0:T(8,128)(2,1)S(1)}, u32[]{:S(2)}, u32[]{:S(2)}) collective-permute-start(bf16[6,512]{1,0:T(8,128)(2,1)S(1)} %select_convert_fusion.13), channel_id=1, source_target_pairs={{0,16},{16,0},{32,48},{48,32},{64,80},{80,64},{96,112},{112,96},{1... | collective-permute-start | bytes 18440 | tf_op jit(solution)/shard_map/ppermute | solution.py:14
  540.1 6.1 collective-permute-start.16
  546.3 8.0 %collective-permute-start.17 = (bf16[192,512]{1,0:T(8,128)(2,1)S(1)}, bf16[192,512]{1,0:T(8,128)(2,1)S(1)}, u32[]{:S(2)}, u32[]{:S(2)}) collective-permute-start(bf16[192,512]{1,0:T(8,128)(2,1)S(1)} %maximum_select_fusion.27), channel_id=1, source_target_pairs={{0,32},{32,0},{16,48},{48,16},{64,96},{96,64},{80,112},{112,80},{1... | collective-permute-start | bytes 589832 | tf_op jit(solution)/shard_map/ppermute | solution.py:14
  554.4 12.9 %collective-permute-start.18 = (bf16[384,512]{1,0:T(8,128)(2,1)S(1)}, bf16[384,512]{1,0:T(8,128)(2,1)S(1)}, u32[]{:S(2)}, u32[]{:S(2)}) collective-permute-start(bf16[384,512]{1,0:T(8,128)(2,1)S(1)} %maximum_select_fusion.25), channel_id=1, source_target_pairs={{0,64},{64,0},{16,80},{80,16},{32,96},{96,32},{48,112},{112,48},{1... | collective-permute-start | bytes 1179656 | tf_op jit(solution)/shard_map/ppermute | solution.py:14
  568.4 19.2 %collective-permute-start.19 = (bf16[768,512]{1,0:T(8,128)(2,1)}, bf16[768,512]{1,0:T(8,128)(2,1)}, u32[]{:S(2)}, u32[]{:S(2)}) collective-permute-start(bf16[768,512]{1,0:T(8,128)(2,1)} %maximum_select_fusion.22), channel_id=1, source_target_pairs={{0,128},{128,0},{16,144},{144,16},{32,160},{160,32},{48,176},{176,... | collective-permute-start | bytes 2359304 | tf_op jit(solution)/shard_map/ppermute | solution.py:14
  590.7 16.1 %all-to-all-start.9 = ((bf16[16,6,512]{2,1,0:T(8,128)(2,1)}), bf16[16,6,512]{2,1,0:T(8,128)(2,1)}, u32[]{:S(2)}, u32[]{:S(2)}) async-start(bf16[16,6,512]{2,1,0:T(8,128)(2,1)} %broadcast_in_dim.45), calls=%async_computation.9 | async-start | bytes 262144 | tf_op jit(solution)/shard_map/all_to_all | solution.py:19
  610.2 6.3 collective-permute-start.20
  616.6 5.0 collective-permute-start.21
  621.6 6.0 collective-permute-start.22
  627.6 4.4 collective-permute-start.23
  632.1 11.2 %collective-permute-start.24 = (bf16[3,512]{1,0:T(4,128)(2,1)S(1)}, bf16[3,512]{1,0:T(4,128)(2,1)S(1)}, u32[]{:S(2)}, u32[]{:S(2)}) collective-permute-start(bf16[3,512]{1,0:T(4,128)(2,1)S(1)} %select_convert_fusion.14), channel_id=1, source_target_pairs={{0,16},{16,0},{32,48},{48,32},{64,80},{80,64},{96,112},{112,96},{1... | collective-permute-start | bytes 9224 | tf_op jit(solution)/shard_map/ppermute | solution.py:14
  659.1 4.8 collective-permute-start.25
  663.9 5.9 collective-permute-start.26
  669.9 8.7 %collective-permute-start.27 = (bf16[192,512]{1,0:T(8,128)(2,1)S(1)}, bf16[192,512]{1,0:T(8,128)(2,1)S(1)}, u32[]{:S(2)}, u32[]{:S(2)}) collective-permute-start(bf16[192,512]{1,0:T(8,128)(2,1)S(1)} %maximum_select_fusion.28), channel_id=1, source_target_pairs={{0,64},{64,0},{16,80},{80,16},{32,96},{96,32},{48,112},{112,48},{1... | collective-permute-start | bytes 589832 | tf_op jit(solution)/shard_map/ppermute | solution.py:14
  678.6 10.5 %collective-permute-start.28 = (bf16[384,512]{1,0:T(8,128)(2,1)S(1)}, bf16[384,512]{1,0:T(8,128)(2,1)S(1)}, u32[]{:S(2)}, u32[]{:S(2)}) collective-permute-start(bf16[384,512]{1,0:T(8,128)(2,1)S(1)} %maximum_select_fusion.26), channel_id=1, source_target_pairs={{0,128},{128,0},{16,144},{144,16},{32,160},{160,32},{48,176},{176,... | collective-permute-start | bytes 1179656 | tf_op jit(solution)/shard_map/ppermute | solution.py:14
  689.5 21.0 %copy-start.2 = (f32[96,512]{1,0:T(8,128)S(1)}, f32[96,512]{1,0:T(8,128)}, u32[]{:S(2)}) copy-start(f32[96,512]{1,0:T(8,128)} %get-tuple-element.35) | copy-start | bytes 589828
  689.5 21.0 %copy-start.5 = (f32[48,512]{1,0:T(8,128)S(1)}, f32[48,512]{1,0:T(8,128)}, u32[]{:S(2)}) copy-start(f32[48,512]{1,0:T(8,128)} %get-tuple-element.37) | copy-start | bytes 294916
  689.5 19.7 %collective-permute-start.29 = (bf16[768,512]{1,0:T(8,128)(2,1)S(1)}, bf16[768,512]{1,0:T(8,128)(2,1)S(1)}, u32[]{:S(2)}, u32[]{:S(2)}) collective-permute-start(bf16[768,512]{1,0:T(8,128)(2,1)S(1)} %maximum_select_fusion.23), channel_id=1, source_target_pairs={{0,256},{256,0},{16,272},{272,16},{32,288},{288,32},{48,304},{304,... | collective-permute-start | bytes 2359304 | tf_op jit(solution)/shard_map/ppermute | solution.py:14
where the time goes:
time: 717 us; the launch traced here: 712 us
  waiting for transfers between devices  265 us (37%)
  blocking collectives  202 us (28%)
  starting transfers between devices  195 us (27%)
  other arithmetic  19.4 us (3%)
  matrix products  18.2 us (3%)
  local copies, waits for them, and re-layouts  11.7 us (2%)
    all_to_all x6, blocking collectives, from_everyone(): return lax.all_to_all(copies, axis, split_axis=0, concat_axis=0, tiled=True)  202 us
    ppermute x30, starting transfers between devices, partner_2(): return lax.ppermute(block, axis, route)  162 us
    all_to_all x5, waiting for transfers between devices, from_everyone(): return lax.all_to_all(copies, axis, split_axis=0, concat_axis=0, tiled=True)  142 us
    ppermute x30, waiting for transfers between devices, partner_2(): return lax.ppermute(block, axis, route)  123 us
    all_to_all x5, starting transfers between devices, from_everyone(): return lax.all_to_all(copies, axis, split_axis=0, concat_axis=0, tiled=True)  32.9 us
    mul x5, other arithmetic, shards(): known_parts[source] * live_pairs[ancestor * (ancestor - 1) // 2 + source]  15.8 us
  transfers between devices with their start and end apart: 35, of which 35 were waited for; matrix products, arithmetic and copies ran while one was open for 1% of the time, Pallas kernels for 0%

commit v1 on v0

v1 whole, which is shorter than its diff:
```python
import jax
import jax.numpy as jnp
from jax import lax
from jax.sharding import PartitionSpec as P

F32 = jnp.float32
BF16 = jnp.bfloat16


def column_start(ancestor, source, width_all):
    offset = 0
    for higher in range(1, ancestor):
        for within in range(higher):
            offset += width_all // 2**within
    for within in range(source):
        offset += width_all // 2**within
    return offset


def dot(a, b):
    return jnp.dot(a, b, preferred_element_type=F32)


def dot_t(a, b):
    return lax.dot_general(a, b, (((1,), (b.ndim - 1,)), ((), ())), preferred_element_type=F32)


def core_swap(block):
    count = lax.axis_size("leaf")
    return lax.ppermute(block, "leaf", [(i, i ^ 1) for i in range(count)])


def leaf_groups(size):
    count = lax.axis_size("leaf")
    return [[first + i for i in range(size)] for first in range(0, count, size)]


def leaf_scatter(pieces):
    size = pieces.shape[0]
    return lax.all_to_all(pieces, "leaf", 0, 0, tiled=True, axis_index_groups=leaf_groups(size))


def leaf_everyone(block, size):
    return leaf_scatter(jnp.broadcast_to(block, (size, *block.shape)))


def shards(rhs, inv_diag, off_diag, pair_mask):
    rows_n = lax.axis_size("row")
    leaves = lax.axis_size("leaf")
    levels = leaves.bit_length() - 1
    width = inv_diag.shape[3]
    cols = rhs.shape[3]
    strip = width // rows_n
    half = cols // 2
    sub = half // rows_n
    leaf = lax.axis_index("leaf")
    core = leaf % 2
    first_core = core == 0
    b_all = rhs[0, 0]
    d_all = inv_diag[0, 0]
    panels = off_diag[0, 0]
    live = pair_mask[0, 0]
    heights = [strip >> m for m in range(levels + 1)]
    starts = [sum(heights[:m]) for m in range(levels + 1)]

    def panel(m, l):
        first = column_start(m, l, width)
        return panels[:, first : first + (width >> l)]

    def alive(m, l, dtype):
        return live[m * (m - 1) // 2 + l].astype(dtype)

    def masked(m, l):
        return panel(m, l) * alive(m, l, BF16)

    d_own0 = d_all[: heights[0]]
    d_full0 = lax.all_gather(d_own0, "row", axis=0, tiled=True)
    b0 = b_all[: heights[0]]
    z0 = jnp.concatenate(
        [
            lax.all_gather(b0[:, :half], "row", axis=0, tiled=True),
            lax.all_gather(b0[:, half:], "row", axis=0, tiled=True),
        ],
        axis=1,
    )

    d_own1 = d_all[starts[1] : starts[2]]
    mid = width // 2
    own1 = jnp.concatenate(
        [masked(m, 1) for m in range(2, levels + 1)] + [d_own1[:, :mid], d_own1[:, mid:]], axis=0
    )
    other1 = core_swap(own1)
    p_rows = strip * (levels - 1)
    p_own1 = own1[:p_rows]
    p_other1 = other1[:p_rows]
    d_other1 = jnp.concatenate(
        [other1[p_rows : p_rows + heights[1]], other1[p_rows + heights[1] :]], axis=1
    )

    upper_pairs = sorted(
        ((m, l) for l in range(2, levels) for m in range(l + 1, levels + 1)), key=lambda p: (p[1], p[0])
    )
    d_up = d_all[starts[2] :]
    d_rows = d_up.shape[0]
    d_pad = strip // 2
    d_up = jnp.concatenate([d_up, jnp.zeros((d_pad - d_rows, width), BF16)], axis=0)
    packed = jnp.concatenate(
        [jnp.concatenate([d_up[:, :mid], d_up[:, mid:]], axis=0)] + [masked(m, l) for m, l in upper_pairs], axis=1
    )
    packed, d_full0 = lax.optimization_barrier((packed, d_full0))
    everyone = lax.all_gather(packed, "row", axis=0, tiled=False)

    yb0 = dot(d_full0, z0).astype(BF16)
    out0 = dot(d_own0, z0)
    parts = []
    for m in range(1, levels + 1):
        placed = lax.dynamic_update_slice(
            jnp.zeros((strip, cols), BF16),
            b_all[starts[m] : starts[m] + heights[m]],
            (leaf % 2**m * heights[m], 0),
        )
        parts.append(placed.astype(F32) - dot(panel(m, 0), yb0) * alive(m, 0, F32))
    part = jnp.concatenate(parts, axis=0)
    kept = jnp.where(first_core, part[:, :half], part[:, half:])
    sent = jnp.where(first_core, part[:, half:], part[:, :half]).astype(BF16)
    part = kept + core_swap(sent).astype(F32)

    def natural1(block):
        pieces = lax.all_gather(block, "row", axis=0, tiled=False)
        return pieces.reshape(rows_n, 2, heights[1], half).transpose(1, 0, 2, 3).reshape(2, mid, half)

    z1 = natural1(part[:strip].astype(BF16)).reshape(width, half)
    y_own1 = dot(d_own1, z1)
    y_other1 = dot(d_other1, z1)
    yb1 = jnp.where(
        first_core,
        jnp.concatenate([y_own1, y_other1], axis=0),
        jnp.concatenate([y_other1, y_own1], axis=0),
    ).astype(BF16)
    y_got1 = core_swap(y_other1)
    out1 = jnp.where(
        first_core,
        jnp.concatenate([y_own1, y_got1], axis=1),
        jnp.concatenate([y_got1, y_own1], axis=1),
    )
    yn1 = natural1(yb1)
    here = jnp.where(first_core, yn1[0], yn1[1])
    there = jnp.where(first_core, yn1[1], yn1[0])
    part = part[strip:] - (dot(p_own1, here) + dot(p_other1, there))

    turned = part.T.astype(BF16).reshape(rows_n, sub, p_rows)
    turned = lax.all_to_all(turned, "row", 0, 0, tiled=True)

    def turned_of(m):
        return turned[:, :, (m - 2) * strip : (m - 1) * strip]

    def d_leaf(m):
        low = starts[m] - starts[2]
        left = everyone[:, low : low + heights[m], :mid]
        right = everyone[:, d_pad + low : d_pad + low + heights[m], :mid]
        return jnp.concatenate([left, right], axis=2).reshape(rows_n * heights[m], width)

    p_leaf = {}
    at = mid
    for m, l in upper_pairs:
        p_leaf[m, l] = everyone[:, :, at : at + (width >> l)]
        at += width >> l

    def natural(z, m):
        z = z.reshape(rows_n, 2 * sub, 2**m, heights[m])
        return z.transpose(1, 2, 0, 3).reshape(2 * sub, width)

    solved = []
    sums = {}
    for m in range(2, levels + 1):
        if m == 2:
            pieces = leaf_everyone(turned_of(2), 4).astype(F32)
            pieces = pieces.reshape(2, 2, rows_n, sub, strip).sum(axis=0).astype(BF16)
            z = pieces.transpose(1, 0, 2, 3).reshape(rows_n, 2 * sub, strip)
        else:
            size = 2**m
            mine = jnp.where(
                (jnp.arange(2) == core)[None, :, None, None], turned_of(m)[:, None], jnp.zeros((), BF16)
            ).reshape(rows_n, 2 * sub, strip)
            v = (mine.astype(F32) - sums[m]).astype(BF16)
            if size <= rows_n:
                v = v.reshape(size, rows_n // size, 2 * sub, strip)
                z = leaf_scatter(v).astype(F32).sum(axis=0).astype(BF16)
                z = leaf_everyone(z, size).reshape(rows_n, 2 * sub, strip)
            else:
                cut = size // rows_n
                v = v.reshape(rows_n, 2 * sub, cut, strip // cut).transpose(0, 2, 1, 3)
                v = v.reshape(size, 2 * sub, strip // cut)
                z = leaf_scatter(v).astype(F32).sum(axis=0).astype(BF16)
                z = leaf_everyone(z, size).reshape(rows_n, cut, 2 * sub, strip // cut)
                z = z.transpose(0, 2, 1, 3).reshape(rows_n, 2 * sub, strip)
        y = dot_t(natural(z, m), d_leaf(m))
        yb = y.astype(BF16)
        solved.append(yb.reshape(2 * sub, rows_n, heights[m]))
        for higher in range(m + 1, levels + 1):
            term = dot_t(yb, p_leaf[higher, m]).transpose(1, 0, 2)
            sums[higher] = term if m == 2 else sums[higher] + term

    done = jnp.concatenate(solved, axis=2).transpose(1, 0, 2)
    done = lax.all_to_all(done, "row", 0, 0, tiled=True)
    done = done.reshape(rows_n, 2, sub, d_rows).transpose(3, 1, 0, 2).reshape(d_rows, cols)
    return jnp.concatenate([out0, out1, done.astype(F32)], axis=0)[None, None]


def solution(mesh):
    in_specs = (
        P("leaf", "row", None, None),
        P("leaf", "row", None, None),
        P("leaf", "row", None, None),
        P("leaf", "row", None),
    )
    out_specs = P("leaf", "row", None, None)
    return jax.shard_map(shards, mesh=mesh, in_specs=in_specs, out_specs=out_specs, check_vma=False)
```

time: 717 us -> 422 us (0.59)
  waiting for transfers between devices: 265 us -> 109 us
  starting transfers between devices: 195 us -> 73.9 us
  blocking collectives: 202 us -> 144 us
  local copies, waits for them, and re-layouts: 11.7 us -> 30 us
  between operations: 0.84 us -> 17.6 us
    all_to_all x6 -> x1, blocking collectives: 202 us -> 20.8 us  [shards(): turned = lax.all_to_all(turned, 'row', 0, 0, tiled=True)]
    ppermute x30 -> x3, starting transfers between devices: 162 us -> 22.5 us  [core_swap(): return lax.ppermute(block, 'leaf', [(i, i ^ 1) for i in range(count)])]
    all_gather x0 -> x4, blocking collectives: none -> 123 us  [the longest x2 49.4 us: natural1(): pieces = lax.all_gather(block, 'row', axis=0, tiled=False)]
    ppermute x30 -> x3, waiting for transfers between devices: 123 us -> 1.09 us  [core_swap(): return lax.ppermute(block, 'leaf', [(i, i ^ 1) for i in range(count)])]
    all_to_all x5 -> x8, waiting for transfers between devices: 142 us -> 40.8 us  [the longest x7 30.6 us: leaf_scatter(): lax.all_to_all(pieces, 'leaf', 0, 0, tiled=True, axis_index_groups=leaf_g...]
    all_gather x0 -> x2, waiting for transfers between devices: none -> 67.4 us  [the longest x1 67.4 us: shards(): d_full0 = lax.all_gather(d_own0, 'row', axis=0, tiled=True)]
    all_to_all x5 -> x8, starting transfers between devices: 32.9 us -> 51.3 us  [the longest x7 46.5 us: leaf_scatter(): lax.all_to_all(pieces, 'leaf', 0, 0, tiled=True, axis_index_groups=leaf_g...]
    unnamed x0 -> x4, other arithmetic: none -> 9.2 us
  transfers between devices with their start and end apart: 35 -> 13, of which waited for: 35 -> 10; matrix products, arithmetic and copies ran while one was open for 1% -> 17% of each run, Pallas kernels for 0% -> 0%
where the time goes in v1:
time: 422 us; the launch traced here: 421 us
  blocking collectives  144 us (34%)
  waiting for transfers between devices  109 us (26%)
  starting transfers between devices  73.9 us (18%)
  local copies, waits for them, and re-layouts  30 us (7%)
  matrix products  23.1 us (5%)
  other arithmetic  23 us (5%)
  between operations  17.6 us (4%)
    all_gather x1, waiting for transfers between devices, shards(): d_full0 = lax.all_gather(d_own0, 'row', axis=0, tiled=True)  67.4 us
    all_gather x2, blocking collectives, natural1(): pieces = lax.all_gather(block, 'row', axis=0, tiled=False)  49.4 us
    all_to_all x7, starting transfers between devices, leaf_scatter(): lax.all_to_all(pieces, 'leaf', 0, 0, tiled=True, axis_index_groups=leaf_g...  46.5 us
    all_gather x1, blocking collectives, shards(): lax.all_gather(b0[:, :half], 'row', axis=0, tiled=True)  37 us
    all_gather x1, blocking collectives, shards(): lax.all_gather(b0[:, half:], 'row', axis=0, tiled=True)  36.5 us
    all_to_all x7, waiting for transfers between devices, leaf_scatter(): lax.all_to_all(pieces, 'leaf', 0, 0, tiled=True, axis_index_groups=leaf_g...  30.6 us
    ppermute x3, starting transfers between devices, core_swap(): return lax.ppermute(block, 'leaf', [(i, i ^ 1) for i in range(count)])  22.5 us
    all_to_all x1, blocking collectives, shards(): turned = lax.all_to_all(turned, 'row', 0, 0, tiled=True)  20.8 us
  transfers between devices with their start and end apart: 13, of which 10 were waited for; matrix products, arithmetic and copies ran while one was open for 17% of the time, Pallas kernels for 0%

profile of v1, /device:TPU:1, one launch (start us, length us, event | category | flops | bytes accessed | tf_op | source)
XLA Modules:
  0.0 420.5 jit_solution(10371558072732546112)
XLA Ops:
  6.5 1.7 slice.287
  9.7 0.9 slice_bitcast_fusion.1
  10.6 1.3 slice_multiply_fusion.9
  11.9 2.3 slice_multiply_fusion.7
  14.2 3.0 slice_multiply_fusion.4
  17.2 0.9 concatenate.78
  18.1 67.4 %all-gather.6.cloned.1.call-done = bf16[1,1,1536,1536]{3,2,1,0:T(8,128)(2,1)} async-done(((bf16[1,1,96,1536]{3,2,1,0:T(8,128)(2,1)}), bf16[1,1,1536,1536]{3,2,1,0:T(8,128)(2,1)}) %all-gather.6.cloned.1.call-update) | async-done | bytes 4718608 | tf_op jit(solution)/shard_map/all_gather | solution.py:77
  85.5 2.2 constant_dynamic-update-slice_fusion.5
  87.7 2.2 constant_dynamic-update-slice_fusion.4
  89.9 2.4 constant_dynamic-update-slice_fusion.3
  92.3 2.4 constant_dynamic-update-slice_fusion.2
  96.0 10.9 %collective-permute-start.1 = (bf16[480,768]{1,0:T(8,128)(2,1)}, bf16[480,768]{1,0:T(8,128)(2,1)S(1)}, u32[]{:S(2)}, u32[]{:S(2)}) collective-permute-start(bf16[480,768]{1,0:T(8,128)(2,1)} %slice_dynamic-update-slice_fusion), channel_id=1, source_target_pairs={{0,16},{16,0},{32,48},{48,32},{64,80},{80,64},{96,112},{112,96},{1... | collective-permute-start | bytes 2211848 | tf_op jit(solution)/shard_map/ppermute | solution.py:30
  111.7 37.0 %all_gather.25 = bf16[1536,256]{1,0:T(8,128)(2,1)S(1)} all-gather(bf16[96,256]{1,0:T(8,128)(2,1)S(1)} %get-tuple-element.43), channel_id=1, replica_groups=mesh['leaf'=32,'row'=16] {'row'}, dimensions={0}, use_global_device_ids=true | all-gather | bytes 835584 | tf_op jit(solution)/shard_map/all_gather | solution.py:81
  148.8 36.5 %all_gather.26 = bf16[1536,256]{1,0:T(8,128)(2,1)S(1)} all-gather(bf16[96,256]{1,0:T(8,128)(2,1)S(1)} %get-tuple-element.42), channel_id=1, replica_groups=mesh['leaf'=32,'row'=16] {'row'}, dimensions={0}, use_global_device_ids=true | all-gather | bytes 835584 | tf_op jit(solution)/shard_map/all_gather | solution.py:82
  185.4 2.6 convolution_convert_fusion
  190.1 9.7 %collective-permute-start = (bf16[480,256]{1,0:T(8,128)(2,1)S(1)}, bf16[480,256]{1,0:T(8,128)(2,1)S(1)}, u32[]{:S(2)}, u32[]{:S(2)}) collective-permute-start(bf16[480,256]{1,0:T(8,128)(2,1)S(1)} %select_convert_fusion), channel_id=1, source_target_pairs={{0,16},{16,0},{32,48},{48,32},{64,80},{80,64},{96,112},{112,96},{1... | collective-permute-start | bytes 737288 | tf_op jit(solution)/shard_map/ppermute | solution.py:30
  199.9 1.1 collective-permute-done
  201.0 25.1 %all-gather.1 = bf16[1536,256]{1,0:T(8,128)(2,1)S(1)} all-gather(bf16[96,256]{1,0:T(8,128)(2,1)S(1)} %slice.485), channel_id=3, replica_groups=mesh['leaf'=32,'row'=16] {'row'}, dimensions={0}, use_global_device_ids=true | all-gather | bytes 835584 | tf_op jit(solution)/shard_map/all_gather | solution.py:129
  226.2 0.9 fusion.57
  227.3 0.9 fusion.61
  228.2 24.3 %all_gather.30 = bf16[16,96,256]{2,1,0:T(8,128)(2,1)S(1)} all-gather(bf16[1,96,256]{2,1,0:T(8,128)(2,1)S(1)} %fusion.61), channel_id=1, replica_groups=mesh['leaf'=32,'row'=16] {'row'}, dimensions={0}, use_global_device_ids=true | all-gather | bytes 835584 | tf_op jit(solution)/shard_map/all_gather | solution.py:129
  253.4 20.8 %all_to_all.45 = bf16[16,16,384]{2,1,0:T(8,128)(2,1)S(1)} all-to-all(bf16[16,16,384]{2,1,0:T(8,128)(2,1)S(1)} %bitcast.226), channel_id=1, replica_groups=mesh['leaf'=32,'row'=16] {'row'}, dimensions={0} | all-to-all | bytes 393216 | tf_op jit(solution)/shard_map/all_to_all | solution.py:152
  274.4 0.7 broadcast_in_dim.70
  275.1 18.8 %all-to-all-start.1 = ((bf16[4,16,16,96]{3,2,1,0:T(8,128)(2,1)}), bf16[4,16,16,96]{3,2,1,0:T(8,128)(2,1)S(1)}, u32[]{:S(2)}, u32[]{:S(2)}) async-start(bf16[4,16,16,96]{3,2,1,0:T(8,128)(2,1)} %broadcast_in_dim.70), calls=%async_computation.1 | async-start | bytes 524288 | tf_op jit(solution)/shard_map/all_to_all | solution.py:40
  294.1 1.9 collective-permute-start.2
  296.1 0.8 bitcast_select_fusion.1
  296.9 2.1 all-to-all-done.1
  300.7 1.3 fusion.75
  302.0 2.0 fusion.74
  304.5 2.7 fusion.2
  307.2 2.6 fusion
  309.8 2.6 fusion.33
  312.4 5.2 %all-to-all-start.2 = ((bf16[8,2,32,96]{3,2,1,0:T(8,128)(2,1)}), bf16[8,2,32,96]{3,2,1,0:T(8,128)(2,1)S(1)}, u32[]{:S(2)}, u32[]{:S(2)}) async-start(bf16[8,2,32,96]{3,2,1,0:T(8,128)(2,1)} %bitcast.55), calls=%async_computation.2 | async-start | bytes 262144 | tf_op jit(solution)/shard_map/all_to_all | solution.py:40
  317.6 1.1 pad_maximum_fusion.1
  318.7 4.2 all-to-all-done.2
  323.6 4.7 %all-to-all-start.3 = ((bf16[8,2,32,96]{3,2,1,0:T(8,128)(2,1)}), bf16[8,2,32,96]{3,2,1,0:T(8,128)(2,1)}, u32[]{:S(2)}, u32[]{:S(2)}) async-start(bf16[8,2,32,96]{3,2,1,0:T(8,128)(2,1)} %broadcast_in_dim.77), calls=%async_computation.3 | async-start | bytes 262144 | tf_op jit(solution)/shard_map/all_to_all | solution.py:40
  328.3 2.0 fusion.73
  330.5 3.2 all-to-all-done.3
  333.7 1.9 copy.78
  335.6 1.1 copy.79
  336.7 1.0 reshape.219
  337.7 1.3 convolution_convert_fusion.2
  339.0 2.3 fusion.36
  341.3 4.3 %all-to-all-start.4 = ((bf16[16,1,32,96]{3,2,1,0:T(8,128)(2,1)}), bf16[16,1,32,96]{3,2,1,0:T(8,128)(2,1)S(1)}, u32[]{:S(2)}, u32[]{:S(2)}) async-start(bf16[16,1,32,96]{3,2,1,0:T(8,128)(2,1)} %fusion.36), calls=%async_computation.4 | async-start | bytes 262144 | tf_op jit(solution)/shard_map/all_to_all | solution.py:40
  345.6 1.1 pad_maximum_fusion.2
  346.8 4.9 %all-to-all-done.4 = bf16[16,1,32,96]{3,2,1,0:T(8,128)(2,1)S(1)} async-done(((bf16[16,1,32,96]{3,2,1,0:T(8,128)(2,1)}), bf16[16,1,32,96]{3,2,1,0:T(8,128)(2,1)S(1)}, u32[]{:S(2)}, u32[]{:S(2)}) %all-to-all-start.4) | async-done | bytes 98336 | tf_op jit(solution)/shard_map/all_to_all | solution.py:40
  352.4 4.0 all-to-all-start.5
  356.4 2.4 convolution_add_fusion.2
  358.8 3.8 all-to-all-done.5
  363.6 1.5 fusion.16
  365.2 1.0 reshape.243
  366.2 5.6 %all-to-all-start.6 = ((bf16[32,2,768]{2,1,0:T(2,128)(2,1)}), bf16[32,2,768]{2,1,0:T(2,128)(2,1)S(1)}, u32[]{:S(2)}, u32[]{:S(2)}) async-start(bf16[32,2,768]{2,1,0:T(2,128)(2,1)} %reshape.243), calls=%async_computation.6 | async-start | bytes 196608 | tf_op jit(solution)/shard_map/all_to_all | solution.py:40
  371.9 1.1 fusion.72
  373.0 6.3 %all-to-all-done.6 = bf16[32,2,768]{2,1,0:T(2,128)(2,1)S(1)} async-done(((bf16[32,2,768]{2,1,0:T(2,128)(2,1)}), bf16[32,2,768]{2,1,0:T(2,128)(2,1)S(1)}, u32[]{:S(2)}, u32[]{:S(2)}) %all-to-all-start.6) | async-done | bytes 98336 | tf_op jit(solution)/shard_map/all_to_all | solution.py:40
  379.7 1.0 reshape.245
  380.7 3.9 all-to-all-start.7
  385.2 0.8 reshape.241
  386.0 6.1 %all-to-all-done.7 = bf16[32,2,768]{2,1,0:T(2,128)(2,1)S(1)} async-done(((bf16[32,2,768]{2,1,0:T(2,128)(2,1)}), bf16[32,2,768]{2,1,0:T(2,128)(2,1)S(1)}, u32[]{:S(2)}, u32[]{:S(2)}) %all-to-all-start.7) | async-done | bytes 98336 | tf_op jit(solution)/shard_map/all_to_all | solution.py:40
  393.8 1.1 maximum_bitcast_fusion.1
  394.9 0.8 reshape.247
  395.8 4.8 %all-to-all-start.8 = ((bf16[16,2,720]{2,1,0:T(2,128)(2,1)}), bf16[16,2,720]{2,1,0:T(2,128)(2,1)S(1)}, u32[]{:S(2)}, u32[]{:S(2)}) async-start(bf16[16,2,720]{2,1,0:T(2,128)(2,1)} %reshape.247), calls=%async_computation.8 | async-start | bytes 98304 | tf_op jit(solution)/shard_map/all_to_all | solution.py:205
  401.0 0.9 maximum_select_fusion
  401.9 10.3 %all-to-all-done.8 = bf16[16,2,720]{2,1,0:T(2,128)(2,1)S(1)} async-done(((bf16[16,2,720]{2,1,0:T(2,128)(2,1)}), bf16[16,2,720]{2,1,0:T(2,128)(2,1)S(1)}, u32[]{:S(2)}, u32[]{:S(2)}) %all-to-all-start.8) | async-done | bytes 46112 | tf_op jit(solution)/shard_map/all_to_all | solution.py:205
  412.6 1.1 copy.95
  (120 shorter events, 16.2 us)
Async XLA Ops:
  6.5 78.9 %all-gather.6.cloned.1.call-start = ((), (), s32[]{:S(2)}) async-start(), calls=%async_computation.9 | async-start | bytes 5013504 | tf_op jit(solution)/shard_map/all_gather | solution.py:77
  8.3 292.4 %all-gather.8.cloned.1.call-start = ((), (), s32[]{:S(2)}) async-start(), calls=%async_computation.10 | async-start | bytes 7938048 | tf_op jit(solution)/shard_map/all_gather | solution.py:111
  17.2 77.5 %copy-start.1 = (bf16[1,1,189,1536]{3,2,1,0:T(8,128)(2,1)S(1)}, bf16[1,1,189,1536]{3,2,1,0:T(8,128)(2,1)}, u32[]{:S(2)}) copy-start(bf16[1,1,189,1536]{3,2,1,0:T(8,128)(2,1)} %param.5) | copy-start | bytes 1741828
  18.1 88.8 %copy-start.13 = (s32[1,1,15]{2,1,0:T(1,128)S(1)}, s32[1,1,15]{2,1,0:T(1,128)}, u32[]{:S(2)}) copy-start(s32[1,1,15]{2,1,0:T(1,128)} %param.7) | copy-start | bytes 184
  18.1 92.8 %copy-start.9 = (bf16[1,1,189,512]{3,2,1,0:T(8,128)(2,1)S(1)}, bf16[1,1,189,512]{3,2,1,0:T(8,128)(2,1)}, u32[]{:S(2)}) copy-start(bf16[1,1,189,512]{3,2,1,0:T(8,128)(2,1)} %param.4) | copy-start | bytes 580612
  96.0 103.9 %collective-permute-start.1 = (bf16[480,768]{1,0:T(8,128)(2,1)}, bf16[480,768]{1,0:T(8,128)(2,1)S(1)}, u32[]{:S(2)}, u32[]{:S(2)}) collective-permute-start(bf16[480,768]{1,0:T(8,128)(2,1)} %slice_dynamic-update-slice_fusion), channel_id=1, source_target_pairs={{0,16},{16,0},{32,48},{48,32},{64,80},{80,64},{96,112},{112,96},{1... | collective-permute-start | bytes 2211848 | tf_op jit(solution)/shard_map/ppermute | solution.py:30
  111.7 73.6 %copy-start.14 = (bf16[1,1,1536,1536]{3,2,1,0:T(8,128)(2,1)S(1)}, bf16[1,1,1536,1536]{3,2,1,0:T(8,128)(2,1)}, u32[]{:S(2)}) copy-start(bf16[1,1,1536,1536]{3,2,1,0:T(8,128)(2,1)} %all-gather.6.cloned.1.call-done) | copy-start | bytes 14155780
  185.4 2.6 copy-start
  190.1 10.9 %collective-permute-start = (bf16[480,256]{1,0:T(8,128)(2,1)S(1)}, bf16[480,256]{1,0:T(8,128)(2,1)S(1)}, u32[]{:S(2)}, u32[]{:S(2)}) collective-permute-start(bf16[480,256]{1,0:T(8,128)(2,1)S(1)} %select_convert_fusion), channel_id=1, source_target_pairs={{0,16},{16,0},{32,48},{48,32},{64,80},{80,64},{96,112},{112,96},{1... | collective-permute-start | bytes 737288 | tf_op jit(solution)/shard_map/ppermute | solution.py:30
  227.1 25.5 %copy-start.10 = (bf16[96,768]{1,0:T(8,128)(2,1)S(1)}, bf16[96,768]{1,0:T(8,128)(2,1)}, u32[]{:S(2)}) copy-start(bf16[96,768]{1,0:T(8,128)(2,1)} %get-tuple-element.14) | copy-start | bytes 442372
  227.1 25.5 %copy-start.11 = (bf16[96,768]{1,0:T(8,128)(2,1)S(1)}, bf16[96,768]{1,0:T(8,128)(2,1)}, u32[]{:S(2)}) copy-start(bf16[96,768]{1,0:T(8,128)(2,1)} %get-tuple-element.12) | copy-start | bytes 442372
  227.1 25.5 %copy-start.12 = (bf16[96,768]{1,0:T(8,128)(2,1)S(1)}, bf16[96,768]{1,0:T(8,128)(2,1)}, u32[]{:S(2)}) copy-start(bf16[96,768]{1,0:T(8,128)(2,1)} %get-tuple-element.10) | copy-start | bytes 442372
  227.3 25.6 %copy-start.7 = (f32[256,48]{0,1:T(8,128)}, f32[256,48]{0,1:T(8,128)S(1)}, u32[]{:S(2)}) copy-start(f32[256,48]{0,1:T(8,128)S(1)} %fusion.70) | copy-start | bytes 147460
  275.1 23.9 %all-to-all-start.1 = ((bf16[4,16,16,96]{3,2,1,0:T(8,128)(2,1)}), bf16[4,16,16,96]{3,2,1,0:T(8,128)(2,1)S(1)}, u32[]{:S(2)}, u32[]{:S(2)}) async-start(bf16[4,16,16,96]{3,2,1,0:T(8,128)(2,1)} %broadcast_in_dim.70), calls=%async_computation.1 | async-start | bytes 524288 | tf_op jit(solution)/shard_map/all_to_all | solution.py:40
  294.1 106.8 %collective-permute-start.2 = (f32[48,256]{1,0:T(8,128)}, f32[48,256]{1,0:T(8,128)}, u32[]{:S(2)}, u32[]{:S(2)}) collective-permute-start(f32[48,256]{1,0:T(8,128)} %fusion.57), channel_id=1, source_target_pairs={{0,16},{16,0},{32,48},{48,32},{64,80},{80,64},{96,112},{112,96},{1... | collective-permute-start | bytes 147464 | tf_op jit(solution)/shard_map/ppermute | solution.py:30
  304.5 7.9 %copy-start.3 = (bf16[32,384]{1,0:T(8,128)(2,1)}, bf16[32,384]{1,0:T(8,128)(2,1)S(1)}, u32[]{:S(2)}) copy-start(bf16[32,384]{1,0:T(8,128)(2,1)S(1)} %convolution_convert_fusion.1) | copy-start | bytes 73732
  312.4 10.5 %all-to-all-start.2 = ((bf16[8,2,32,96]{3,2,1,0:T(8,128)(2,1)}), bf16[8,2,32,96]{3,2,1,0:T(8,128)(2,1)S(1)}, u32[]{:S(2)}, u32[]{:S(2)}) async-start(bf16[8,2,32,96]{3,2,1,0:T(8,128)(2,1)} %bitcast.55), calls=%async_computation.2 | async-start | bytes 262144 | tf_op jit(solution)/shard_map/all_to_all | solution.py:40
  323.6 10.1 %all-to-all-start.3 = ((bf16[8,2,32,96]{3,2,1,0:T(8,128)(2,1)}), bf16[8,2,32,96]{3,2,1,0:T(8,128)(2,1)}, u32[]{:S(2)}, u32[]{:S(2)}) async-start(bf16[8,2,32,96]{3,2,1,0:T(8,128)(2,1)} %broadcast_in_dim.77), calls=%async_computation.3 | async-start | bytes 262144 | tf_op jit(solution)/shard_map/all_to_all | solution.py:40
  330.5 8.5 %copy-start.6 = (bf16[16,32,96]{2,1,0:T(8,128)(2,1)S(1)}, bf16[16,32,96]{2,1,0:T(8,128)(2,1)}, u32[]{:S(2)}) copy-start(bf16[16,32,96]{2,1,0:T(8,128)(2,1)} %get-tuple-element.44) | copy-start | bytes 294916
  339.0 17.4 %copy-start.2 = (f32[32,16,96]{2,0,1:T(8,128)S(1)}, f32[32,16,96]{2,0,1:T(8,128)}, u32[]{:S(2)}) copy-start(f32[32,16,96]{2,0,1:T(8,128)} %fusion) | copy-start | bytes 589828
  341.3 10.4 %all-to-all-start.4 = ((bf16[16,1,32,96]{3,2,1,0:T(8,128)(2,1)}), bf16[16,1,32,96]{3,2,1,0:T(8,128)(2,1)S(1)}, u32[]{:S(2)}, u32[]{:S(2)}) async-start(bf16[16,1,32,96]{3,2,1,0:T(8,128)(2,1)} %fusion.36), calls=%async_computation.4 | async-start | bytes 262144 | tf_op jit(solution)/shard_map/all_to_all | solution.py:40
  352.4 10.2 %all-to-all-start.5 = ((bf16[16,1,32,96]{3,2,1,0:T(8,128)(2,1)}), bf16[16,1,32,96]{3,2,1,0:T(8,128)(2,1)S(1)}, u32[]{:S(2)}, u32[]{:S(2)}) async-start(bf16[16,1,32,96]{3,2,1,0:T(8,128)(2,1)} %broadcast_in_dim.80), calls=%async_computation.5 | async-start | bytes 262144 | tf_op jit(solution)/shard_map/all_to_all | solution.py:40
  358.8 4.7 %copy-start.5 = (bf16[16,32,96]{2,1,0:T(8,128)(2,1)S(1)}, bf16[16,32,96]{2,1,0:T(8,128)(2,1)}, u32[]{:S(2)}) copy-start(bf16[16,32,96]{2,1,0:T(8,128)(2,1)} %get-tuple-element.45) | copy-start | bytes 294916
  365.2 19.5 %copy-start.4 = (bf16[32,384]{1,0:T(8,128)(2,1)S(1)}, bf16[32,384]{1,0:T(8,128)(2,1)}, u32[]{:S(2)}) copy-start(bf16[32,384]{1,0:T(8,128)(2,1)} %copy-done.3) | copy-start | bytes 73732
  366.2 13.1 %all-to-all-start.6 = ((bf16[32,2,768]{2,1,0:T(2,128)(2,1)}), bf16[32,2,768]{2,1,0:T(2,128)(2,1)S(1)}, u32[]{:S(2)}, u32[]{:S(2)}) async-start(bf16[32,2,768]{2,1,0:T(2,128)(2,1)} %reshape.243), calls=%async_computation.6 | async-start | bytes 196608 | tf_op jit(solution)/shard_map/all_to_all | solution.py:40
  380.7 11.5 %all-to-all-start.7 = ((bf16[32,2,768]{2,1,0:T(2,128)(2,1)}), bf16[32,2,768]{2,1,0:T(2,128)(2,1)S(1)}, u32[]{:S(2)}, u32[]{:S(2)}) async-start(bf16[32,2,768]{2,1,0:T(2,128)(2,1)} %reshape.245), calls=%async_computation.7 | async-start | bytes 196608 | tf_op jit(solution)/shard_map/all_to_all | solution.py:40
  393.8 7.2 %copy-start.8 = (f32[256,48]{0,1:T(8,128)S(1)}, f32[256,48]{0,1:T(8,128)}, u32[]{:S(2)}) copy-start(f32[256,48]{0,1:T(8,128)} %copy-done.7) | copy-start | bytes 147460
  395.8 16.4 %all-to-all-start.8 = ((bf16[16,2,720]{2,1,0:T(2,128)(2,1)}), bf16[16,2,720]{2,1,0:T(2,128)(2,1)S(1)}, u32[]{:S(2)}, u32[]{:S(2)}) async-start(bf16[16,2,720]{2,1,0:T(2,128)(2,1)} %reshape.247), calls=%async_computation.8 | async-start | bytes 98304 | tf_op jit(solution)/shard_map/all_to_all | solution.py:205
Sparse Core Ops, SparseCore 0:
  9.4 76.0 all-gather.5
  87.5 117.3 all-gather.7

commit v2 on v1

--- a/solution.py
+++ b/solution.py
@@ -76,27 +76,10 @@
     d_own0 = d_all[: heights[0]]
     d_full0 = lax.all_gather(d_own0, "row", axis=0, tiled=True)
     b0 = b_all[: heights[0]]
-    z0 = jnp.concatenate(
-        [
-            lax.all_gather(b0[:, :half], "row", axis=0, tiled=True),
-            lax.all_gather(b0[:, half:], "row", axis=0, tiled=True),
-        ],
-        axis=1,
-    )
+    z0_left = lax.all_gather(b0[:, :half], "row", axis=0, tiled=True)
+    z0_right = lax.all_gather(b0[:, half:], "row", axis=0, tiled=True)
 
-    d_own1 = d_all[starts[1] : starts[2]]
     mid = width // 2
-    own1 = jnp.concatenate(
-        [masked(m, 1) for m in range(2, levels + 1)] + [d_own1[:, :mid], d_own1[:, mid:]], axis=0
-    )
-    other1 = core_swap(own1)
-    p_rows = strip * (levels - 1)
-    p_own1 = own1[:p_rows]
-    p_other1 = other1[:p_rows]
-    d_other1 = jnp.concatenate(
-        [other1[p_rows : p_rows + heights[1]], other1[p_rows + heights[1] :]], axis=1
-    )
-
     upper_pairs = sorted(
         ((m, l) for l in range(2, levels) for m in range(l + 1, levels + 1)), key=lambda p: (p[1], p[0])
     )
@@ -107,9 +90,10 @@
     packed = jnp.concatenate(
         [jnp.concatenate([d_up[:, :mid], d_up[:, mid:]], axis=0)] + [masked(m, l) for m, l in upper_pairs], axis=1
     )
-    packed, d_full0 = lax.optimization_barrier((packed, d_full0))
+    packed, z0_left = lax.optimization_barrier((packed, z0_left))
     everyone = lax.all_gather(packed, "row", axis=0, tiled=False)
 
+    z0 = jnp.concatenate([z0_left, z0_right], axis=1)
     yb0 = dot(d_full0, z0).astype(BF16)
     out0 = dot(d_own0, z0)
     parts = []
@@ -120,33 +104,29 @@
             (leaf % 2**m * heights[m], 0),
         )
         parts.append(placed.astype(F32) - dot(panel(m, 0), yb0) * alive(m, 0, F32))
-    part = jnp.concatenate(parts, axis=0)
-    kept = jnp.where(first_core, part[:, :half], part[:, half:])
-    sent = jnp.where(first_core, part[:, half:], part[:, :half]).astype(BF16)
-    part = kept + core_swap(sent).astype(F32)
+    def core_sum(part):
+        kept = jnp.where(first_core, part[:, :half], part[:, half:])
+        sent = jnp.where(first_core, part[:, half:], part[:, :half]).astype(BF16)
+        return kept + core_swap(sent).astype(F32)
 
-    def natural1(block):
-        pieces = lax.all_gather(block, "row", axis=0, tiled=False)
-        return pieces.reshape(rows_n, 2, heights[1], half).transpose(1, 0, 2, 3).reshape(2, mid, half)
-
-    z1 = natural1(part[:strip].astype(BF16)).reshape(width, half)
-    y_own1 = dot(d_own1, z1)
-    y_other1 = dot(d_other1, z1)
-    yb1 = jnp.where(
-        first_core,
-        jnp.concatenate([y_own1, y_other1], axis=0),
-        jnp.concatenate([y_other1, y_own1], axis=0),
-    ).astype(BF16)
-    y_got1 = core_swap(y_other1)
+    d_own1 = d_all[starts[1] : starts[2]]
+    z1 = core_sum(parts[0]).astype(BF16)
+    z1 = lax.all_gather(z1, "row", axis=0, tiled=False)
+    z1 = z1.reshape(rows_n, 2, heights[1], half).transpose(1, 0, 2, 3).reshape(width, half)
+    z1_got = core_swap(z1)
+    y_kept1 = dot(d_own1, z1)
+    y_got1 = dot(d_own1, z1_got)
     out1 = jnp.where(
         first_core,
-        jnp.concatenate([y_own1, y_got1], axis=1),
-        jnp.concatenate([y_got1, y_own1], axis=1),
+        jnp.concatenate([y_kept1, y_got1], axis=1),
+        jnp.concatenate([y_got1, y_kept1], axis=1),
     )
-    yn1 = natural1(yb1)
-    here = jnp.where(first_core, yn1[0], yn1[1])
-    there = jnp.where(first_core, yn1[1], yn1[0])
-    part = part[strip:] - (dot(p_own1, here) + dot(p_other1, there))
+    yb1 = lax.all_gather(out1.astype(BF16), "row", axis=0, tiled=True)
+    parts = [
+        parts[m - 1] - dot(panel(m, 1), yb1) * alive(m, 1, F32) for m in range(2, levels + 1)
+    ]
+    part = core_sum(jnp.concatenate(parts, axis=0))
+    p_rows = strip * (levels - 1)
 
     turned = part.T.astype(BF16).reshape(rows_n, sub, p_rows)
     turned = lax.all_to_all(turned, "row", 0, 0, tiled=True)

time: 422 us -> 368 us (0.87)
  waiting for transfers between devices: 109 us -> 45.2 us
  blocking collectives: 144 us -> 170 us
  other arithmetic: 23 us -> 12.6 us
  starting transfers between devices: 73.9 us -> 64.2 us
    all_gather x1, waiting for transfers between devices: 67.4 us -> 0.02 us  [shards(): d_full0 = lax.all_gather(d_own0, 'row', axis=0, tiled=True)]
    all_gather x4, blocking collectives: 123 us -> 149 us  [the longest x1 42.1 us: shards(): z0_left = lax.all_gather(b0[:, :half], 'row', axis=0, tiled=True)]
    all_to_all x7, starting transfers between devices: 46.5 us -> 35.6 us  [leaf_scatter(): lax.all_to_all(pieces, 'leaf', 0, 0, tiled=True, axis_index_groups=leaf_g...]
    unnamed x4 -> x0, other arithmetic: 9.2 us -> none
    dot_general x11 -> x13, matrix products: 6.76 us -> 10.2 us  [dot(): return jnp.dot(a, b, preferred_element_type=F32)]
  transfers between devices with their start and end apart: 13 -> 13, of which waited for: 10 -> 10; matrix products, arithmetic and copies ran while one was open for 17% -> 10% of each run, Pallas kernels for 0% -> 0%
where the time goes in v2:
time: 368 us; the launch traced here: 367 us
  blocking collectives  170 us (46%)
  starting transfers between devices  64.2 us (17%)
  waiting for transfers between devices  45.2 us (12%)
  local copies, waits for them, and re-layouts  28.6 us (8%)
  matrix products  26.5 us (7%)
  between operations  19.8 us (5%)
  other arithmetic  12.6 us (3%)
    all_gather x1, blocking collectives, shards(): z0_left = lax.all_gather(b0[:, :half], 'row', axis=0, tiled=True)  42.1 us
    all_gather x1, blocking collectives, shards(): yb1 = lax.all_gather(out1.astype(BF16), 'row', axis=0, tiled=True)  38.3 us
    all_gather x1, blocking collectives, shards(): z1 = lax.all_gather(z1, 'row', axis=0, tiled=False)  36 us
    all_to_all x7, starting transfers between devices, leaf_scatter(): lax.all_to_all(pieces, 'leaf', 0, 0, tiled=True, axis_index_groups=leaf_g...  35.6 us
    all_gather x1, blocking collectives, shards(): z0_right = lax.all_gather(b0[:, half:], 'row', axis=0, tiled=True)  32.7 us
    all_to_all x7, waiting for transfers between devices, leaf_scatter(): lax.all_to_all(pieces, 'leaf', 0, 0, tiled=True, axis_index_groups=leaf_g...  32.5 us
    ppermute x3, starting transfers between devices, core_swap(): return lax.ppermute(block, 'leaf', [(i, i ^ 1) for i in range(count)])  22.8 us
    all_to_all x1, blocking collectives, shards(): turned = lax.all_to_all(turned, 'row', 0, 0, tiled=True)  20.8 us
  transfers between devices with their start and end apart: 13, of which 10 were waited for; matrix products, arithmetic and copies ran while one was open for 10% of the time, Pallas kernels for 0%

profile of v2, /device:TPU:1, one launch (start us, length us, event | category | flops | bytes accessed | tf_op | source)
XLA Modules:
  0.0 366.8 jit_solution(553565897219668362)
XLA Ops:
  6.5 1.7 slice.273
  8.3 0.7 convert.15
  9.0 0.7 fusion.79
  9.7 0.9 slice_bitcast_fusion
  10.6 1.4 slice_multiply_fusion.5
  12.1 2.2 slice_multiply_fusion.3
  14.2 2.9 slice_multiply_fusion
  17.1 0.9 concatenate.44
  18.0 42.1 %all_gather.24 = bf16[1536,256]{1,0:T(8,128)(2,1)S(1)} all-gather(bf16[96,256]{1,0:T(8,128)(2,1)S(1)} %get-tuple-element.33), channel_id=1, replica_groups=mesh['leaf'=32,'row'=16] {'row'}, dimensions={0}, use_global_device_ids=true | all-gather | bytes 835584 | tf_op jit(solution)/shard_map/all_gather | solution.py:79
  60.2 0.7 fusion.78
  67.3 32.7 %all_gather.25 = bf16[1536,256]{1,0:T(8,128)(2,1)S(1)} all-gather(bf16[96,256]{1,0:T(8,128)(2,1)S(1)} %get-tuple-element.32), channel_id=1, replica_groups=mesh['leaf'=32,'row'=16] {'row'}, dimensions={0}, use_global_device_ids=true | all-gather | bytes 835584 | tf_op jit(solution)/shard_map/all_gather | solution.py:80
  100.1 5.1 %fusion.2 = bf16[512,1536]{1,0:T(8,128)(2,1)S(1)} fusion(bf16[1536,512]{1,0:T(8,128)(2,1)S(1)} %constant_dynamic-update-slice_fusion, bf16[1,1,1536,1536]{3,2,1,0:T(8,128)(2,1)} %all-gather.6.cloned.1.call-done), kind=kOutput, calls=%fused_computation.2 | convolution fusion | flops 2416705536 | bytes 7864320 | tf_op jit(solution)/shard_map/dot_general | solution.py:21
  105.9 11.0 %collective-permute-start = (bf16[96,256]{1,0:T(8,128)(2,1)S(1)}, bf16[96,256]{1,0:T(8,128)(2,1)S(1)}, u32[]{:S(2)}, u32[]{:S(2)}) collective-permute-start(bf16[96,256]{1,0:T(8,128)(2,1)S(1)} %select_convert_fusion.1), channel_id=1, source_target_pairs={{0,16},{16,0},{32,48},{48,32},{64,80},{80,64},{96,112},{112,96},{1... | collective-permute-start | bytes 147464 | tf_op jit(solution)/shard_map/ppermute | solution.py:30
  118.2 36.0 %all-gather.1 = bf16[1536,256]{1,0:T(8,128)(2,1)S(1)} all-gather(bf16[96,256]{1,0:T(8,128)(2,1)S(1)} %add_convert_fusion.1), channel_id=3, replica_groups=mesh['leaf'=32,'row'=16] {'row'}, dimensions={0}, use_global_device_ids=true | all-gather | bytes 835584 | tf_op jit(solution)/shard_map/all_gather | solution.py:114
  154.3 5.2 %collective-permute-start.1 = (bf16[1536,256]{1,0:T(8,128)(2,1)S(1)}, bf16[1536,256]{1,0:T(8,128)(2,1)S(1)}, u32[]{:S(2)}, u32[]{:S(2)}) collective-permute-start(bf16[1536,256]{1,0:T(8,128)(2,1)S(1)} %bitcast.210), channel_id=1, source_target_pairs={{0,16},{16,0},{32,48},{48,32},{64,80},{80,64},{96,112},{112,96},{1... | collective-permute-start | bytes 2359304 | tf_op jit(solution)/shard_map/ppermute | solution.py:30
  160.1 0.6 fusion.39
  161.7 0.7 fusion.70
  162.3 38.3 %all_gather.29 = bf16[768,512]{1,0:T(8,128)(2,1)S(1)} all-gather(bf16[48,512]{1,0:T(8,128)(2,1)S(1)} %get-tuple-element.9), channel_id=1, replica_groups=mesh['leaf'=32,'row'=16] {'row'}, dimensions={0}, use_global_device_ids=true | all-gather | bytes 835584 | tf_op jit(solution)/shard_map/all_gather | solution.py:124
  201.9 6.6 %collective-permute-start.2 = (bf16[384,256]{1,0:T(8,128)(2,1)S(1)}, bf16[384,256]{1,0:T(8,128)(2,1)S(1)}, u32[]{:S(2)}, u32[]{:S(2)}) collective-permute-start(bf16[384,256]{1,0:T(8,128)(2,1)S(1)} %select_convert_fusion), channel_id=1, source_target_pairs={{0,16},{16,0},{32,48},{48,32},{64,80},{80,64},{96,112},{112,96},{1... | collective-permute-start | bytes 589832 | tf_op jit(solution)/shard_map/ppermute | solution.py:30
  208.5 1.0 collective-permute-done.2
  209.8 20.8 %all_to_all.45 = bf16[16,16,384]{2,1,0:T(8,128)(2,1)S(1)} all-to-all(bf16[16,16,384]{2,1,0:T(8,128)(2,1)S(1)} %bitcast.232), channel_id=1, replica_groups=mesh['leaf'=32,'row'=16] {'row'}, dimensions={0} | all-to-all | bytes 393216 | tf_op jit(solution)/shard_map/all_to_all | solution.py:132
  230.7 0.7 broadcast_in_dim.70
  231.4 6.9 %all-to-all-start.1 = ((bf16[4,16,16,96]{3,2,1,0:T(8,128)(2,1)}), bf16[4,16,16,96]{3,2,1,0:T(8,128)(2,1)S(1)}, u32[]{:S(2)}, u32[]{:S(2)}) async-start(bf16[4,16,16,96]{3,2,1,0:T(8,128)(2,1)} %broadcast_in_dim.70), calls=%async_computation.1 | async-start | bytes 524288 | tf_op jit(solution)/shard_map/all_to_all | solution.py:40
  238.4 0.8 bitcast_select_fusion.1
  239.3 4.0 %all-to-all-done.1 = bf16[4,16,16,96]{3,2,1,0:T(8,128)(2,1)S(1)} async-done(((bf16[4,16,16,96]{3,2,1,0:T(8,128)(2,1)}), bf16[4,16,16,96]{3,2,1,0:T(8,128)(2,1)S(1)}, u32[]{:S(2)}, u32[]{:S(2)}) %all-to-all-start.1) | async-done | bytes 196640 | tf_op jit(solution)/shard_map/all_to_all | solution.py:40
  244.2 0.7 reshape.148
  245.0 1.3 fusion.74
  246.3 2.0 fusion.73
  248.8 2.7 fusion.7
  251.5 2.6 fusion.5
  254.1 2.6 fusion.41
  256.7 5.9 %all-to-all-start.2 = ((bf16[8,2,32,96]{3,2,1,0:T(8,128)(2,1)}), bf16[8,2,32,96]{3,2,1,0:T(8,128)(2,1)S(1)}, u32[]{:S(2)}, u32[]{:S(2)}) async-start(bf16[8,2,32,96]{3,2,1,0:T(8,128)(2,1)} %bitcast.52), calls=%async_computation.2 | async-start | bytes 262144 | tf_op jit(solution)/shard_map/all_to_all | solution.py:40
  262.7 1.1 pad_maximum_fusion.2
  263.7 4.2 %all-to-all-done.2 = bf16[8,2,32,96]{3,2,1,0:T(8,128)(2,1)S(1)} async-done(((bf16[8,2,32,96]{3,2,1,0:T(8,128)(2,1)}), bf16[8,2,32,96]{3,2,1,0:T(8,128)(2,1)S(1)}, u32[]{:S(2)}, u32[]{:S(2)}) %all-to-all-start.2) | async-done | bytes 98336 | tf_op jit(solution)/shard_map/all_to_all | solution.py:40
  267.9 0.7 broadcast_in_dim.77
  268.6 4.7 %all-to-all-start.3 = ((bf16[8,2,32,96]{3,2,1,0:T(8,128)(2,1)}), bf16[8,2,32,96]{3,2,1,0:T(8,128)(2,1)}, u32[]{:S(2)}, u32[]{:S(2)}) async-start(bf16[8,2,32,96]{3,2,1,0:T(8,128)(2,1)} %broadcast_in_dim.77), calls=%async_computation.3 | async-start | bytes 262144 | tf_op jit(solution)/shard_map/all_to_all | solution.py:40
  273.3 2.0 fusion.72
  275.5 3.2 all-to-all-done.3
  278.7 1.8 copy.68
  280.6 1.1 copy.69
  281.7 1.0 reshape.152
  282.7 1.3 convolution_convert_fusion.1
  284.0 2.2 fusion.44
  286.3 4.7 %all-to-all-start.4 = ((bf16[16,1,32,96]{3,2,1,0:T(8,128)(2,1)}), bf16[16,1,32,96]{3,2,1,0:T(8,128)(2,1)S(1)}, u32[]{:S(2)}, u32[]{:S(2)}) async-start(bf16[16,1,32,96]{3,2,1,0:T(8,128)(2,1)} %fusion.44), calls=%async_computation.4 | async-start | bytes 262144 | tf_op jit(solution)/shard_map/all_to_all | solution.py:40
  290.9 1.1 pad_maximum_fusion.3
  292.1 4.9 %all-to-all-done.4 = bf16[16,1,32,96]{3,2,1,0:T(8,128)(2,1)S(1)} async-done(((bf16[16,1,32,96]{3,2,1,0:T(8,128)(2,1)}), bf16[16,1,32,96]{3,2,1,0:T(8,128)(2,1)S(1)}, u32[]{:S(2)}, u32[]{:S(2)}) %all-to-all-start.4) | async-done | bytes 98336 | tf_op jit(solution)/shard_map/all_to_all | solution.py:40
  297.1 0.7 broadcast_in_dim.80
  297.7 4.0 %all-to-all-start.5 = ((bf16[16,1,32,96]{3,2,1,0:T(8,128)(2,1)}), bf16[16,1,32,96]{3,2,1,0:T(8,128)(2,1)S(1)}, u32[]{:S(2)}, u32[]{:S(2)}) async-start(bf16[16,1,32,96]{3,2,1,0:T(8,128)(2,1)} %broadcast_in_dim.80), calls=%async_computation.5 | async-start | bytes 262144 | tf_op jit(solution)/shard_map/all_to_all | solution.py:40
  301.7 2.4 convolution_add_fusion.1
  304.1 3.8 %all-to-all-done.5 = bf16[16,1,32,96]{3,2,1,0:T(8,128)(2,1)S(1)} async-done(((bf16[16,1,32,96]{3,2,1,0:T(8,128)(2,1)}), bf16[16,1,32,96]{3,2,1,0:T(8,128)(2,1)S(1)}, u32[]{:S(2)}, u32[]{:S(2)}) %all-to-all-start.5) | async-done | bytes 98336 | tf_op jit(solution)/shard_map/all_to_all | solution.py:40
  308.9 1.5 fusion.21
  310.6 1.0 reshape.176
  311.6 5.6 %all-to-all-start.6 = ((bf16[32,2,768]{2,1,0:T(2,128)(2,1)}), bf16[32,2,768]{2,1,0:T(2,128)(2,1)S(1)}, u32[]{:S(2)}, u32[]{:S(2)}) async-start(bf16[32,2,768]{2,1,0:T(2,128)(2,1)} %reshape.176), calls=%async_computation.6 | async-start | bytes 196608 | tf_op jit(solution)/shard_map/all_to_all | solution.py:40
  317.2 1.1 fusion.71
  318.3 6.3 %all-to-all-done.6 = bf16[32,2,768]{2,1,0:T(2,128)(2,1)S(1)} async-done(((bf16[32,2,768]{2,1,0:T(2,128)(2,1)}), bf16[32,2,768]{2,1,0:T(2,128)(2,1)S(1)}, u32[]{:S(2)}, u32[]{:S(2)}) %all-to-all-start.6) | async-done | bytes 98336 | tf_op jit(solution)/shard_map/all_to_all | solution.py:40
  325.0 1.0 reshape.178
  326.0 3.9 %all-to-all-start.7 = ((bf16[32,2,768]{2,1,0:T(2,128)(2,1)}), bf16[32,2,768]{2,1,0:T(2,128)(2,1)S(1)}, u32[]{:S(2)}, u32[]{:S(2)}) async-start(bf16[32,2,768]{2,1,0:T(2,128)(2,1)} %reshape.178), calls=%async_computation.7 | async-start | bytes 196608 | tf_op jit(solution)/shard_map/all_to_all | solution.py:40
  330.5 0.8 reshape.174
  331.3 6.1 %all-to-all-done.7 = bf16[32,2,768]{2,1,0:T(2,128)(2,1)S(1)} async-done(((bf16[32,2,768]{2,1,0:T(2,128)(2,1)}), bf16[32,2,768]{2,1,0:T(2,128)(2,1)S(1)}, u32[]{:S(2)}, u32[]{:S(2)}) %all-to-all-start.7) | async-done | bytes 98336 | tf_op jit(solution)/shard_map/all_to_all | solution.py:40
  339.1 1.1 maximum_bitcast_fusion.1
  340.3 0.8 reshape.180
  341.1 5.7 %all-to-all-start.8 = ((bf16[16,2,720]{2,1,0:T(2,128)(2,1)}), bf16[16,2,720]{2,1,0:T(2,128)(2,1)S(1)}, u32[]{:S(2)}, u32[]{:S(2)}) async-start(bf16[16,2,720]{2,1,0:T(2,128)(2,1)} %reshape.180), calls=%async_computation.8 | async-start | bytes 98304 | tf_op jit(solution)/shard_map/all_to_all | solution.py:185
  347.2 11.2 %all-to-all-done.8 = bf16[16,2,720]{2,1,0:T(2,128)(2,1)S(1)} async-done(((bf16[16,2,720]{2,1,0:T(2,128)(2,1)}), bf16[16,2,720]{2,1,0:T(2,128)(2,1)S(1)}, u32[]{:S(2)}, u32[]{:S(2)}) %all-to-all-start.8) | async-done | bytes 46112 | tf_op jit(solution)/shard_map/all_to_all | solution.py:185
  358.8 1.1 copy.85
  (104 shorter events, 12.4 us)
Async XLA Ops:
  6.5 11.5 %copy-start.8 = (bf16[1,1,189,512]{3,2,1,0:T(8,128)(2,1)S(1)}, bf16[1,1,189,512]{3,2,1,0:T(8,128)(2,1)}, u32[]{:S(2)}) copy-start(bf16[1,1,189,512]{3,2,1,0:T(8,128)(2,1)} %param.4) | copy-start | bytes 580612
  6.5 93.6 %all-gather.6.cloned.1.call-start = ((), (), s32[]{:S(2)}) async-start(), calls=%async_computation.9 | async-start | bytes 5013504 | tf_op jit(solution)/shard_map/all_gather | solution.py:77
  8.3 51.9 %copy-start.9 = (s32[1,1,15]{2,1,0:T(1,128)S(1)}, s32[1,1,15]{2,1,0:T(1,128)}, u32[]{:S(2)}) copy-start(s32[1,1,15]{2,1,0:T(1,128)} %param.7) | copy-start | bytes 184
  8.3 236.7 %all-gather.8.cloned.1.call-start = ((), (), s32[]{:S(2)}) async-start(), calls=%async_computation.10 | async-start | bytes 7938048 | tf_op jit(solution)/shard_map/all_gather | solution.py:94
  100.1 5.2 %copy-start = (bf16[1,1,96,12384]{3,2,1,0:T(8,128)(2,1)S(1)}, bf16[1,1,96,12384]{3,2,1,0:T(8,128)(2,1)}, u32[]{:S(2)}) copy-start(bf16[1,1,96,12384]{3,2,1,0:T(8,128)(2,1)} %param.6) | copy-start | bytes 7133188
  105.9 12.2 %collective-permute-start = (bf16[96,256]{1,0:T(8,128)(2,1)S(1)}, bf16[96,256]{1,0:T(8,128)(2,1)S(1)}, u32[]{:S(2)}, u32[]{:S(2)}) collective-permute-start(bf16[96,256]{1,0:T(8,128)(2,1)S(1)} %select_convert_fusion.1), channel_id=1, source_target_pairs={{0,16},{16,0},{32,48},{48,32},{64,80},{80,64},{96,112},{112,96},{1... | collective-permute-start | bytes 147464 | tf_op jit(solution)/shard_map/ppermute | solution.py:30
  154.3 6.5 %copy-start.1 = (bf16[1,1,189,1536]{3,2,1,0:T(8,128)(2,1)S(1)}, bf16[1,1,189,1536]{3,2,1,0:T(8,128)(2,1)}, u32[]{:S(2)}) copy-start(bf16[1,1,189,1536]{3,2,1,0:T(8,128)(2,1)} %param.5) | copy-start | bytes 1741828
  154.3 7.1 %collective-permute-start.1 = (bf16[1536,256]{1,0:T(8,128)(2,1)S(1)}, bf16[1536,256]{1,0:T(8,128)(2,1)S(1)}, u32[]{:S(2)}, u32[]{:S(2)}) collective-permute-start(bf16[1536,256]{1,0:T(8,128)(2,1)S(1)} %bitcast.210), channel_id=1, source_target_pairs={{0,16},{16,0},{32,48},{48,32},{64,80},{80,64},{96,112},{112,96},{1... | collective-permute-start | bytes 2359304 | tf_op jit(solution)/shard_map/ppermute | solution.py:30
  201.9 7.7 %collective-permute-start.2 = (bf16[384,256]{1,0:T(8,128)(2,1)S(1)}, bf16[384,256]{1,0:T(8,128)(2,1)S(1)}, u32[]{:S(2)}, u32[]{:S(2)}) collective-permute-start(bf16[384,256]{1,0:T(8,128)(2,1)S(1)} %select_convert_fusion), channel_id=1, source_target_pairs={{0,16},{16,0},{32,48},{48,32},{64,80},{80,64},{96,112},{112,96},{1... | collective-permute-start | bytes 589832 | tf_op jit(solution)/shard_map/ppermute | solution.py:30
  231.4 11.9 %all-to-all-start.1 = ((bf16[4,16,16,96]{3,2,1,0:T(8,128)(2,1)}), bf16[4,16,16,96]{3,2,1,0:T(8,128)(2,1)S(1)}, u32[]{:S(2)}, u32[]{:S(2)}) async-start(bf16[4,16,16,96]{3,2,1,0:T(8,128)(2,1)} %broadcast_in_dim.70), calls=%async_computation.1 | async-start | bytes 524288 | tf_op jit(solution)/shard_map/all_to_all | solution.py:40
  248.8 13.8 %copy-start.3 = (bf16[32,384]{1,0:T(8,128)(2,1)}, bf16[32,384]{1,0:T(8,128)(2,1)S(1)}, u32[]{:S(2)}) copy-start(bf16[32,384]{1,0:T(8,128)(2,1)S(1)} %convolution_convert_fusion) | copy-start | bytes 73732
  256.7 11.2 %all-to-all-start.2 = ((bf16[8,2,32,96]{3,2,1,0:T(8,128)(2,1)}), bf16[8,2,32,96]{3,2,1,0:T(8,128)(2,1)S(1)}, u32[]{:S(2)}, u32[]{:S(2)}) async-start(bf16[8,2,32,96]{3,2,1,0:T(8,128)(2,1)} %bitcast.52), calls=%async_computation.2 | async-start | bytes 262144 | tf_op jit(solution)/shard_map/all_to_all | solution.py:40
  268.6 10.1 %all-to-all-start.3 = ((bf16[8,2,32,96]{3,2,1,0:T(8,128)(2,1)}), bf16[8,2,32,96]{3,2,1,0:T(8,128)(2,1)}, u32[]{:S(2)}, u32[]{:S(2)}) async-start(bf16[8,2,32,96]{3,2,1,0:T(8,128)(2,1)} %broadcast_in_dim.77), calls=%async_computation.3 | async-start | bytes 262144 | tf_op jit(solution)/shard_map/all_to_all | solution.py:40
  275.5 8.5 %copy-start.6 = (bf16[16,32,96]{2,1,0:T(8,128)(2,1)S(1)}, bf16[16,32,96]{2,1,0:T(8,128)(2,1)}, u32[]{:S(2)}) copy-start(bf16[16,32,96]{2,1,0:T(8,128)(2,1)} %get-tuple-element.34) | copy-start | bytes 294916
  282.7 19.0 %copy-start.2 = (f32[32,16,96]{2,0,1:T(8,128)S(1)}, f32[32,16,96]{2,0,1:T(8,128)}, u32[]{:S(2)}) copy-start(f32[32,16,96]{2,0,1:T(8,128)} %fusion.5) | copy-start | bytes 589828
  286.3 10.8 %all-to-all-start.4 = ((bf16[16,1,32,96]{3,2,1,0:T(8,128)(2,1)}), bf16[16,1,32,96]{3,2,1,0:T(8,128)(2,1)S(1)}, u32[]{:S(2)}, u32[]{:S(2)}) async-start(bf16[16,1,32,96]{3,2,1,0:T(8,128)(2,1)} %fusion.44), calls=%async_computation.4 | async-start | bytes 262144 | tf_op jit(solution)/shard_map/all_to_all | solution.py:40
  297.1 11.8 %copy-start.5 = (bf16[16,32,96]{2,1,0:T(8,128)(2,1)S(1)}, bf16[16,32,96]{2,1,0:T(8,128)(2,1)}, u32[]{:S(2)}) copy-start(bf16[16,32,96]{2,1,0:T(8,128)(2,1)} %get-tuple-element.35) | copy-start | bytes 294916
  297.7 10.2 %all-to-all-start.5 = ((bf16[16,1,32,96]{3,2,1,0:T(8,128)(2,1)}), bf16[16,1,32,96]{3,2,1,0:T(8,128)(2,1)S(1)}, u32[]{:S(2)}, u32[]{:S(2)}) async-start(bf16[16,1,32,96]{3,2,1,0:T(8,128)(2,1)} %broadcast_in_dim.80), calls=%async_computation.5 | async-start | bytes 262144 | tf_op jit(solution)/shard_map/all_to_all | solution.py:40
  308.9 21.1 %copy-start.4 = (bf16[32,384]{1,0:T(8,128)(2,1)S(1)}, bf16[32,384]{1,0:T(8,128)(2,1)}, u32[]{:S(2)}) copy-start(bf16[32,384]{1,0:T(8,128)(2,1)} %copy-done.3) | copy-start | bytes 73732
  311.6 13.1 %all-to-all-start.6 = ((bf16[32,2,768]{2,1,0:T(2,128)(2,1)}), bf16[32,2,768]{2,1,0:T(2,128)(2,1)S(1)}, u32[]{:S(2)}, u32[]{:S(2)}) async-start(bf16[32,2,768]{2,1,0:T(2,128)(2,1)} %reshape.176), calls=%async_computation.6 | async-start | bytes 196608 | tf_op jit(solution)/shard_map/all_to_all | solution.py:40
  326.0 11.5 %all-to-all-start.7 = ((bf16[32,2,768]{2,1,0:T(2,128)(2,1)}), bf16[32,2,768]{2,1,0:T(2,128)(2,1)S(1)}, u32[]{:S(2)}, u32[]{:S(2)}) async-start(bf16[32,2,768]{2,1,0:T(2,128)(2,1)} %reshape.178), calls=%async_computation.7 | async-start | bytes 196608 | tf_op jit(solution)/shard_map/all_to_all | solution.py:40
  339.1 19.7 %copy-start.7 = (f32[48,512]{1,0:T(8,128)S(1)}, f32[48,512]{1,0:T(8,128)}, u32[]{:S(2)}) copy-start(f32[48,512]{1,0:T(8,128)} %get-tuple-element.10) | copy-start | bytes 294916
  341.1 17.3 %all-to-all-start.8 = ((bf16[16,2,720]{2,1,0:T(2,128)(2,1)}), bf16[16,2,720]{2,1,0:T(2,128)(2,1)S(1)}, u32[]{:S(2)}, u32[]{:S(2)}) async-start(bf16[16,2,720]{2,1,0:T(2,128)(2,1)} %reshape.180), calls=%async_computation.8 | async-start | bytes 98304 | tf_op jit(solution)/shard_map/all_to_all | solution.py:185
Sparse Core Ops, SparseCore 0:
  9.4 86.2 all-gather.5
  97.8 114.9 all-gather.7

commit v3 on v2

v3 whole, which is shorter than its diff:
```python
import jax
import jax.numpy as jnp
import numpy as np
from jax import lax
from jax.sharding import PartitionSpec as P

F32 = jnp.float32
BF16 = jnp.bfloat16


def column_start(ancestor, source, width_all):
    offset = 0
    for higher in range(1, ancestor):
        for within in range(higher):
            offset += width_all // 2**within
    for within in range(source):
        offset += width_all // 2**within
    return offset


def dot(a, b):
    return jnp.dot(a, b, preferred_element_type=F32)


def dot_t(a, b):
    return lax.dot_general(a, b, (((1,), (b.ndim - 1,)), ((), ())), preferred_element_type=F32)


def core_swap(block):
    count = lax.axis_size("leaf")
    return lax.ppermute(block, "leaf", [(i, i ^ 1) for i in range(count)])


def leaf_groups(size):
    count = lax.axis_size("leaf")
    return [[first + i for i in range(size)] for first in range(0, count, size)]


def leaf_scatter(pieces):
    size = pieces.shape[0]
    return lax.all_to_all(pieces, "leaf", 0, 0, tiled=True, axis_index_groups=leaf_groups(size))


def leaf_everyone(block, size):
    return leaf_scatter(jnp.broadcast_to(block, (size, *block.shape)))


def shards(rhs, inv_diag, off_diag, pair_mask):
    rows_n = lax.axis_size("row")
    leaves = lax.axis_size("leaf")
    levels = leaves.bit_length() - 1
    width = inv_diag.shape[3]
    cols = rhs.shape[3]
    strip = width // rows_n
    half = cols // 2
    sub = half // rows_n
    leaf = lax.axis_index("leaf")
    core = leaf & 1
    first_core = core == 0
    b_all = rhs[0, 0]
    d_all = inv_diag[0, 0]
    panels = off_diag[0, 0]
    live = pair_mask[0, 0]
    heights = [strip >> m for m in range(levels + 1)]
    starts = [sum(heights[:m]) for m in range(levels + 1)]

    def panel(m, l):
        first = column_start(m, l, width)
        return panels[:, first : first + (width >> l)]

    def alive(m, l, dtype):
        return live[m * (m - 1) // 2 + l].astype(dtype)

    def by_core(one, two):
        return jnp.where(first_core, one, two)

    d_own0 = d_all[: heights[0]]
    d_full0 = lax.all_gather(d_own0, "row", axis=0, tiled=True)
    b0 = b_all[: heights[0]]
    z0_left = lax.all_gather(b0[:, :half], "row", axis=0, tiled=True)
    z0_right = lax.all_gather(b0[:, half:], "row", axis=0, tiled=True)

    upper_pairs = sorted(
        ((m, l) for l in range(2, levels) for m in range(l + 1, levels + 1)), key=lambda p: (p[1], p[0])
    )
    p_cols = sum(width >> l for _, l in upper_pairs)
    pieces = [
        jnp.concatenate([panel(m, l) * alive(m, l, BF16) for m, l in upper_pairs], axis=1)
    ]
    d_first = {}
    at = strip
    for m in range(2, levels + 1):
        d_first[m] = at
        room = -heights[m] % 8
        rows = d_all[starts[m] : starts[m] + heights[m]]
        pieces.append(jnp.pad(rows, ((0, room), (0, p_cols - width))))
        at += heights[m] + room
    packed = jnp.concatenate(pieces, axis=0)
    packed, z0_left = lax.optimization_barrier((packed, z0_left))
    everyone = lax.all_gather(packed, "row", axis=0, tiled=False)

    tall = strip * levels
    base = np.concatenate([strip * (m - 1) + np.arange(heights[m]) for m in range(1, levels + 1)])
    bits = np.concatenate([np.full(heights[m], 2**m - 1) for m in range(1, levels + 1)])
    step = np.concatenate([np.full(heights[m], heights[m]) for m in range(1, levels + 1)])
    place = jnp.asarray(base, jnp.int32) + (leaf & jnp.asarray(bits, jnp.int32)) * jnp.asarray(step, jnp.int32)
    spread = (lax.broadcasted_iota(jnp.int32, (tall, base.size), 0) == place[None]).astype(BF16)
    b_up = b_all[strip:]
    b_up = by_core(b_up, jnp.concatenate([b_up[:, half:], b_up[:, :half]], axis=1))
    placed = dot(spread, b_up)

    z0_sent = by_core(z0_right, z0_left)
    z0_kept = by_core(z0_left, z0_right)
    live1 = alive(1, 0, F32)
    yb_sent = dot(d_full0, z0_sent).astype(BF16)
    sent = placed[:strip, half:] - dot(panel(1, 0), yb_sent) * live1
    got = core_swap(sent.astype(BF16))
    yb_kept = dot(d_full0, z0_kept).astype(BF16)
    kept = placed[:strip, :half] - dot(panel(1, 0), yb_kept) * live1
    yb0 = jnp.concatenate([yb_kept, yb_sent], axis=1)
    parts = [
        placed[strip * (m - 1) : strip * m] - dot(panel(m, 0), yb0) * alive(m, 0, F32)
        for m in range(2, levels + 1)
    ]

    d_own1 = d_all[starts[1] : starts[2]]
    z1 = (kept + got.astype(F32)).astype(BF16)
    z1 = lax.all_gather(z1, "row", axis=0, tiled=False)
    z1 = z1.reshape(rows_n, 2, heights[1], half).transpose(1, 0, 2, 3).reshape(width, half)
    z1_got = core_swap(z1)
    y_kept1 = dot(d_own1, z1)
    y_sent1 = dot(d_own1, z1_got)
    yb1 = jnp.concatenate([y_kept1, y_sent1], axis=1).astype(BF16)
    yb1, parts = lax.optimization_barrier((yb1, parts))
    yb1 = lax.all_gather(yb1, "row", axis=0, tiled=True)
    out0_kept = dot(d_own0, z0_kept)
    out0_sent = dot(d_own0, z0_sent)
    part = jnp.concatenate(
        [parts[m - 2] - dot(panel(m, 1), yb1) * alive(m, 1, F32) for m in range(2, levels + 1)], axis=0
    )
    part = part[:, :half] + core_swap(part[:, half:].astype(BF16)).astype(F32)
    p_rows = strip * (levels - 1)

    turned = part.T.astype(BF16).reshape(rows_n, sub, p_rows)
    turned = lax.all_to_all(turned, "row", 0, 0, tiled=True)

    def turned_of(m):
        return turned[:, :, (m - 2) * strip : (m - 1) * strip]

    def d_leaf(m):
        rows = everyone[:, d_first[m] : d_first[m] + heights[m], :width]
        return rows.reshape(rows_n * heights[m], width)

    p_leaf = {}
    at = 0
    for m, l in upper_pairs:
        p_leaf[m, l] = everyone[:, :strip, at : at + (width >> l)]
        at += width >> l

    def natural(z, m):
        z = z.reshape(rows_n, 2 * sub, 2**m, heights[m])
        return z.transpose(1, 2, 0, 3).reshape(2 * sub, width)

    solved = []
    sums = {}
    for m in range(2, levels + 1):
        if m == 2:
            pieces = leaf_everyone(turned_of(2), 4).astype(F32)
            pieces = pieces.reshape(2, 2, rows_n, sub, strip).sum(axis=0).astype(BF16)
            z = pieces.transpose(1, 0, 2, 3).reshape(rows_n, 2 * sub, strip)
        else:
            size = 2**m
            mine = jnp.where(
                (jnp.arange(2) == core)[None, :, None, None], turned_of(m)[:, None], jnp.zeros((), BF16)
            ).reshape(rows_n, 2 * sub, strip)
            v = (mine.astype(F32) - sums[m]).astype(BF16)
            v = v.reshape(size, rows_n * 2 * sub // size, strip)
            z = leaf_scatter(v).astype(F32).sum(axis=0).astype(BF16)
            z = leaf_everyone(z, size).reshape(rows_n, 2 * sub, strip)
        y = dot_t(natural(z, m), d_leaf(m))
        yb = y.astype(BF16)
        solved.append(yb.reshape(2 * sub, rows_n, heights[m]))
        for higher in range(m + 1, levels + 1):
            term = dot_t(yb, p_leaf[higher, m]).transpose(1, 0, 2)
            sums[higher] = term if m == 2 else sums[higher] + term

    d_rows = sum(heights[2:])
    done = jnp.concatenate(solved, axis=2).transpose(1, 0, 2)
    done = lax.all_to_all(done, "row", 0, 0, tiled=True)
    done = done.reshape(rows_n, 2, sub, d_rows).transpose(3, 1, 0, 2).reshape(d_rows, cols)
    head_kept = jnp.concatenate([out0_kept, y_kept1], axis=0)
    head_sent = jnp.concatenate([out0_sent, y_sent1], axis=0)
    head = by_core(
        jnp.concatenate([head_kept, head_sent], axis=1), jnp.concatenate([head_sent, head_kept], axis=1)
    )
    return jnp.concatenate([head, done.astype(F32)], axis=0)[None, None]


def solution(mesh):
    in_specs = (
        P("leaf", "row", None, None),
        P("leaf", "row", None, None),
        P("leaf", "row", None, None),
        P("leaf", "row", None),
    )
    out_specs = P("leaf", "row", None, None)
    return jax.shard_map(shards, mesh=mesh, in_specs=in_specs, out_specs=out_specs, check_vma=False)
```

time: 368 us -> 359 us (0.976)
  blocking collectives: 170 us -> 198 us
  waiting for transfers between devices: 45.2 us -> 29.8 us
  starting transfers between devices: 64.2 us -> 50.1 us
  other arithmetic: 12.6 us -> 8.68 us
    all_to_all x0 -> x2, blocking collectives: none -> 24.1 us  [leaf_scatter(): lax.all_to_all(pieces, 'leaf', 0, 0, tiled=True, axis_index_groups=leaf_g...]
    all_to_all x7 -> x5, waiting for transfers between devices: 32.5 us -> 17.4 us  [leaf_scatter(): lax.all_to_all(pieces, 'leaf', 0, 0, tiled=True, axis_index_groups=leaf_g...]
    all_to_all x7 -> x5, starting transfers between devices: 35.6 us -> 23 us  [leaf_scatter(): lax.all_to_all(pieces, 'leaf', 0, 0, tiled=True, axis_index_groups=leaf_g...]
    dot_general x10, matrix products: 16.3 us -> 12.5 us  [dot_t(): lax.dot_general(a, b, (((1,), (b.ndim - 1,)), ((), ())), preferred_elemen...]
    dot_general x13 -> x17, matrix products: 10.2 us -> 13.2 us  [dot(): return jnp.dot(a, b, preferred_element_type=F32)]
    slice x9 -> x11, local copies, waits for them, and re-layouts: 7.4 us -> 7.94 us  [the longest x4 4.63 us: d_leaf(): rows = everyone[:, d_first[m]:d_first[m] + heights[m], :width]]
  transfers between devices with their start and end apart: 13 -> 11, of which waited for: 10 -> 7; matrix products, arithmetic and copies ran while one was open for 10% -> 11% of each run, Pallas kernels for 0% -> 0%
where the time goes in v3:
time: 359 us; the launch traced here: 357 us
  blocking collectives  198 us (55%)
  starting transfers between devices  50.1 us (14%)
  waiting for transfers between devices  29.8 us (8%)
  matrix products  25.6 us (7%)
  local copies, waits for them, and re-layouts  25.3 us (7%)
  between operations  19.6 us (5%)
  other arithmetic  8.68 us (2%)
    all_gather x1, blocking collectives, shards(): z0_left = lax.all_gather(b0[:, :half], 'row', axis=0, tiled=True)  45.1 us
    all_gather x1, blocking collectives, shards(): yb1 = lax.all_gather(yb1, 'row', axis=0, tiled=True)  38.4 us
    all_gather x1, blocking collectives, shards(): z1 = lax.all_gather(z1, 'row', axis=0, tiled=False)  38.3 us
    all_gather x1, blocking collectives, shards(): z0_right = lax.all_gather(b0[:, half:], 'row', axis=0, tiled=True)  33.6 us
    all_to_all x2, blocking collectives, leaf_scatter(): lax.all_to_all(pieces, 'leaf', 0, 0, tiled=True, axis_index_groups=leaf_g...  24.1 us
    all_to_all x5, starting transfers between devices, leaf_scatter(): lax.all_to_all(pieces, 'leaf', 0, 0, tiled=True, axis_index_groups=leaf_g...  23 us
    ppermute x3, starting transfers between devices, core_swap(): return lax.ppermute(block, 'leaf', [(i, i ^ 1) for i in range(count)])  21.3 us
    all_to_all x1, blocking collectives, shards(): turned = lax.all_to_all(turned, 'row', 0, 0, tiled=True)  18.7 us
  transfers between devices with their start and end apart: 11, of which 7 were waited for; matrix products, arithmetic and copies ran while one was open for 11% of the time, Pallas kernels for 0%

profile of v3, /device:TPU:1, one launch (start us, length us, event | category | flops | bytes accessed | tf_op | source)
XLA Modules:
  0.0 357.2 jit_solution(548420940309869740)
XLA Ops:
  6.5 1.7 slice.263
  8.4 0.7 convert.24
  9.0 0.7 fusion.93
  9.7 1.3 slice_multiply_fusion.5
  11.0 2.2 slice_multiply_fusion.3
  13.2 2.9 slice_multiply_fusion
  16.2 0.9 slice_bitcast_fusion.2
  17.2 0.8 slice_bitcast_fusion.3
  18.0 0.8 slice_bitcast_fusion.4
  18.8 0.8 slice_bitcast_fusion.5
  19.6 45.1 %all_gather.24 = bf16[1536,256]{1,0:T(8,128)(2,1)} all-gather(bf16[96,256]{1,0:T(8,128)(2,1)S(1)} %get-tuple-element.31), channel_id=1, replica_groups=mesh['leaf'=32,'row'=16] {'row'}, dimensions={0}, use_global_device_ids=true | all-gather | bytes 835584 | tf_op jit(solution)/shard_map/all_gather | solution.py:80
  64.7 0.7 fusion.92
  71.3 33.6 %all_gather.25 = bf16[1536,256]{1,0:T(8,128)(2,1)} all-gather(bf16[96,256]{1,0:T(8,128)(2,1)S(1)} %get-tuple-element.30), channel_id=1, replica_groups=mesh['leaf'=32,'row'=16] {'row'}, dimensions={0}, use_global_device_ids=true | all-gather | bytes 835584 | tf_op jit(solution)/shard_map/all_gather | solution.py:81
  104.9 4.2 %fusion.7 = bf16[256,1536]{1,0:T(8,128)(2,1)S(1)} fusion(bf16[1,1,1536,1536]{3,2,1,0:T(8,128)(2,1)} %all-gather.6.cloned.1.call-done, bf16[1536,256]{1,0:T(8,128)(2,1)} %all_gather.25, bf16[1536,256]{1,0:T(8,128)(2,1)} %all_gather.24, pred[]{:T(512)S(6)} %eq.25), kind=kOutput, calls=%fused_computation.5 | convolution fusion | flops 1208745984 | bytes 7077889 | tf_op jit(solution)/shard_map/dot_general | solution.py:22
  109.5 10.5 %collective-permute-start = (bf16[96,256]{1,0:T(8,128)(2,1)S(1)}, bf16[96,256]{1,0:T(8,128)(2,1)S(1)}, u32[]{:S(2)}, u32[]{:S(2)}) collective-permute-start(bf16[96,256]{1,0:T(8,128)(2,1)S(1)} %fusion.51), channel_id=1, source_target_pairs={{0,16},{16,0},{32,48},{48,32},{64,80},{80,64},{96,112},{112,96},{1... | collective-permute-start | bytes 147464 | tf_op jit(solution)/shard_map/ppermute | solution.py:31
  120.1 1.4 fusion.4
  121.5 0.6 fusion.42
  122.5 38.3 %all-gather.1 = bf16[1536,256]{1,0:T(8,128)(2,1)S(1)} all-gather(bf16[96,256]{1,0:T(8,128)(2,1)S(1)} %add_convert_fusion), channel_id=3, replica_groups=mesh['leaf'=32,'row'=16] {'row'}, dimensions={0}, use_global_device_ids=true | all-gather | bytes 835584 | tf_op jit(solution)/shard_map/all_gather | solution.py:128
  160.9 5.3 %collective-permute-start.1 = (bf16[1536,256]{1,0:T(8,128)(2,1)S(1)}, bf16[1536,256]{1,0:T(8,128)(2,1)S(1)}, u32[]{:S(2)}, u32[]{:S(2)}) collective-permute-start(bf16[1536,256]{1,0:T(8,128)(2,1)S(1)} %bitcast.217), channel_id=1, source_target_pairs={{0,16},{16,0},{32,48},{48,32},{64,80},{80,64},{96,112},{112,96},{1... | collective-permute-start | bytes 2359304 | tf_op jit(solution)/shard_map/ppermute | solution.py:31
  166.8 0.6 fusion.38
  168.5 0.9 fusion.95
  169.4 0.9 fusion.94
  170.3 38.4 %all_gather.29 = bf16[768,512]{1,0:T(8,128)(2,1)S(1)} all-gather(bf16[48,512]{1,0:T(8,128)(2,1)S(1)} %pad_maximum_fusion.2), channel_id=1, replica_groups=mesh['leaf'=32,'row'=16] {'row'}, dimensions={0}, use_global_device_ids=true | all-gather | bytes 835584 | tf_op jit(solution)/shard_map/all_gather | solution.py:135
  209.9 5.4 %collective-permute-start.2 = (bf16[384,256]{1,0:T(8,128)(2,1)S(1)}, bf16[384,256]{1,0:T(8,128)(2,1)S(1)}, u32[]{:S(2)}, u32[]{:S(2)}) collective-permute-start(bf16[384,256]{1,0:T(8,128)(2,1)S(1)} %slice.437), channel_id=1, source_target_pairs={{0,16},{16,0},{32,48},{48,32},{64,80},{80,64},{96,112},{112,96},{1... | collective-permute-start | bytes 589832 | tf_op jit(solution)/shard_map/ppermute | solution.py:31
  215.3 1.0 collective-permute-done.2
  216.6 18.7 %all_to_all.45 = bf16[16,16,384]{2,1,0:T(8,128)(2,1)S(1)} all-to-all(bf16[16,16,384]{2,1,0:T(8,128)(2,1)S(1)} %bitcast.246), channel_id=1, replica_groups=mesh['leaf'=32,'row'=16] {'row'}, dimensions={0} | all-to-all | bytes 393216 | tf_op jit(solution)/shard_map/all_to_all | solution.py:145
  235.4 0.7 broadcast_in_dim.70
  236.2 6.9 %all-to-all-start.1 = ((bf16[4,16,16,96]{3,2,1,0:T(8,128)(2,1)}), bf16[4,16,16,96]{3,2,1,0:T(8,128)(2,1)S(1)}, u32[]{:S(2)}, u32[]{:S(2)}) async-start(bf16[4,16,16,96]{3,2,1,0:T(8,128)(2,1)} %broadcast_in_dim.70), calls=%async_computation.1 | async-start | bytes 524288 | tf_op jit(solution)/shard_map/all_to_all | solution.py:41
  243.3 4.8 %all-to-all-done.1 = bf16[4,16,16,96]{3,2,1,0:T(8,128)(2,1)S(1)} async-done(((bf16[4,16,16,96]{3,2,1,0:T(8,128)(2,1)}), bf16[4,16,16,96]{3,2,1,0:T(8,128)(2,1)S(1)}, u32[]{:S(2)}, u32[]{:S(2)}) %all-to-all-start.1) | async-done | bytes 196640 | tf_op jit(solution)/shard_map/all_to_all | solution.py:41
  248.4 0.6 copy.51
  249.0 0.7 reshape.141
  249.7 1.4 slice.339
  251.6 2.0 fusion.44
  253.5 10.8 %all_to_all.46 = bf16[8,64,96]{2,1,0:T(8,128)(2,1)S(1)} all-to-all(bf16[8,64,96]{2,1,0:T(8,128)(2,1)S(1)} %bitcast.248), channel_id=1, replica_groups={{0,16,32,48,64,80,96,112},{128,144,160,176,192,208,224,240},{256,272,28..., dimensions={0} | all-to-all | bytes 196608 | tf_op jit(solution)/shard_map/all_to_all | solution.py:41
  264.4 0.7 broadcast_in_dim.77
  265.0 4.1 %all-to-all-start.3 = ((bf16[8,64,96]{2,1,0:T(8,128)(2,1)}), bf16[8,64,96]{2,1,0:T(8,128)(2,1)S(1)}, u32[]{:S(2)}, u32[]{:S(2)}) async-start(bf16[8,64,96]{2,1,0:T(8,128)(2,1)} %broadcast_in_dim.77), calls=%async_computation.3 | async-start | bytes 262144 | tf_op jit(solution)/shard_map/all_to_all | solution.py:41
  269.2 1.9 fusion.12
  271.1 1.2 slice.342
  272.5 2.0 all-to-all-done.3
  275.4 2.2 fusion.43
  277.6 4.2 %all-to-all-start.4 = ((bf16[16,32,96]{2,1,0:T(8,128)(2,1)}), bf16[16,32,96]{2,1,0:T(8,128)(2,1)S(1)}, u32[]{:S(2)}, u32[]{:S(2)}) async-start(bf16[16,32,96]{2,1,0:T(8,128)(2,1)} %fusion.43), calls=%async_computation.4 | async-start | bytes 262144 | tf_op jit(solution)/shard_map/all_to_all | solution.py:41
  281.8 1.9 fusion.10
  283.7 1.0 slice.346
  284.9 3.1 all-to-all-done.4
  288.0 0.7 broadcast_in_dim.80
  288.7 4.0 %all-to-all-start.5 = ((bf16[16,32,96]{2,1,0:T(8,128)(2,1)}), bf16[16,32,96]{2,1,0:T(8,128)(2,1)S(1)}, u32[]{:S(2)}, u32[]{:S(2)}) async-start(bf16[16,32,96]{2,1,0:T(8,128)(2,1)} %broadcast_in_dim.80), calls=%async_computation.5 | async-start | bytes 262144 | tf_op jit(solution)/shard_map/all_to_all | solution.py:41
  292.7 1.7 convolution_add_fusion.1
  294.5 4.4 %all-to-all-done.5 = bf16[16,32,96]{2,1,0:T(8,128)(2,1)S(1)} async-done(((bf16[16,32,96]{2,1,0:T(8,128)(2,1)}), bf16[16,32,96]{2,1,0:T(8,128)(2,1)S(1)}, u32[]{:S(2)}, u32[]{:S(2)}) %all-to-all-start.5) | async-done | bytes 98336 | tf_op jit(solution)/shard_map/all_to_all | solution.py:41
  299.9 1.4 fusion.26
  301.3 13.3 %all_to_all.47 = bf16[32,16,96]{2,1,0:T(8,128)(2,1)S(1)} all-to-all(bf16[32,16,96]{2,1,0:T(8,128)(2,1)S(1)} %bitcast.247), channel_id=1, replica_groups={{0,16,32,48,64,80,96,112,128,144,160,176,192,208,224,240,256,272,288,30..., dimensions={0} | all-to-all | bytes 196608 | tf_op jit(solution)/shard_map/all_to_all | solution.py:41
  314.6 0.7 broadcast_in_dim.83
  315.3 3.9 %all-to-all-start.7 = ((bf16[32,16,96]{2,1,0:T(8,128)(2,1)}), bf16[32,16,96]{2,1,0:T(8,128)(2,1)S(1)}, u32[]{:S(2)}, u32[]{:S(2)}) async-start(bf16[32,16,96]{2,1,0:T(8,128)(2,1)} %broadcast_in_dim.83), calls=%async_computation.7 | async-start | bytes 262144 | tf_op jit(solution)/shard_map/all_to_all | solution.py:41
  319.3 0.9 convolution_bitcast_fusion
  320.2 1.0 slice.351
  321.2 0.9 reshape.143
  322.2 0.8 reshape.165
  323.0 0.8 reshape.166
  323.9 3.2 all-to-all-done.7
  327.0 1.1 copy.58
  329.6 1.1 maximum_bitcast_fusion.1
  330.7 0.8 reshape.168
  331.5 5.7 %all-to-all-start.8 = ((bf16[16,2,720]{2,1,0:T(2,128)(2,1)}), bf16[16,2,720]{2,1,0:T(2,128)(2,1)S(1)}, u32[]{:S(2)}, u32[]{:S(2)}) async-start(bf16[16,2,720]{2,1,0:T(2,128)(2,1)} %reshape.168), calls=%async_computation.8 | async-start | bytes 98304 | tf_op jit(solution)/shard_map/all_to_all | solution.py:189
  337.6 11.2 %all-to-all-done.8 = bf16[16,2,720]{2,1,0:T(2,128)(2,1)S(1)} async-done(((bf16[16,2,720]{2,1,0:T(2,128)(2,1)}), bf16[16,2,720]{2,1,0:T(2,128)(2,1)S(1)}, u32[]{:S(2)}, u32[]{:S(2)}) %all-to-all-start.8) | async-done | bytes 46112 | tf_op jit(solution)/shard_map/all_to_all | solution.py:189
  349.2 1.1 copy.67
  (109 shorter events, 10.2 us)
Async XLA Ops:
  6.5 13.0 %copy-start.10 = (bf16[1,1,189,512]{3,2,1,0:T(8,128)(2,1)S(1)}, bf16[1,1,189,512]{3,2,1,0:T(8,128)(2,1)}, u32[]{:S(2)}) copy-start(bf16[1,1,189,512]{3,2,1,0:T(8,128)(2,1)} %param.7) | copy-start | bytes 580612
  6.5 98.3 %all-gather.6.cloned.1.call-start = ((), (), s32[]{:S(2)}) async-start(), calls=%async_computation.9 | async-start | bytes 5013504 | tf_op jit(solution)/shard_map/all_gather | solution.py:78
  8.3 56.4 %copy-start.14 = (s32[1,1,15]{2,1,0:T(1,128)S(1)}, s32[1,1,15]{2,1,0:T(1,128)}, u32[]{:S(2)}) copy-start(s32[1,1,15]{2,1,0:T(1,128)} %param.10) | copy-start | bytes 184
  8.3 62.6 %copy-start.15 = (s32[93]{0:T(128)S(1)}, s32[93]{0:T(128)}, u32[]{:S(2)}) copy-start(s32[93]{0:T(128)} %constant.24.clone) | copy-start | bytes 1120
  8.3 62.6 %copy-start.16 = (s32[93]{0:T(128)S(1)}, s32[93]{0:T(128)}, u32[]{:S(2)}) copy-start(s32[93]{0:T(128)} %constant.25.clone) | copy-start | bytes 1120
  8.3 62.6 %copy-start.17 = (s32[93]{0:T(128)S(1)}, s32[93]{0:T(128)}, u32[]{:S(2)}) copy-start(s32[93]{0:T(128)} %constant.26.clone) | copy-start | bytes 1120
  8.3 241.4 %all-gather.8.cloned.1.call-start = ((), (), s32[]{:S(2)}) async-start(), calls=%async_computation.10 | async-start | bytes 8599552 | tf_op jit(solution)/shard_map/all_gather | solution.py:100
  19.6 45.1 %copy-start = (bf16[152,1632]{1,0:T(8,128)(2,1)}, bf16[152,1632]{1,0:T(8,128)(2,1)S(1)}, u32[]{:S(2)}) copy-start(bf16[152,1632]{1,0:T(8,128)(2,1)S(1)} %pad_dynamic-update-slice_fusion.2) | copy-start | bytes 1488388
  104.9 4.2 %copy-start.1 = (bf16[1,1,96,12384]{3,2,1,0:T(8,128)(2,1)S(1)}, bf16[1,1,96,12384]{3,2,1,0:T(8,128)(2,1)}, u32[]{:S(2)}) copy-start(bf16[1,1,96,12384]{3,2,1,0:T(8,128)(2,1)} %param.9) | copy-start | bytes 7133188
  104.9 15.1 %copy-start.4 = (bf16[1536,256]{1,0:T(8,128)(2,1)S(1)}, bf16[1536,256]{1,0:T(8,128)(2,1)}, u32[]{:S(2)}) copy-start(bf16[1536,256]{1,0:T(8,128)(2,1)} %all_gather.24) | copy-start | bytes 2359300
  104.9 15.2 %copy-start.6 = (bf16[1536,256]{1,0:T(8,128)(2,1)S(1)}, bf16[1536,256]{1,0:T(8,128)(2,1)}, u32[]{:S(2)}) copy-start(bf16[1536,256]{1,0:T(8,128)(2,1)} %all_gather.25) | copy-start | bytes 2359300
  104.9 15.2 %copy-start.18 = (bf16[1,1,1536,1536]{3,2,1,0:T(8,128)(2,1)S(1)}, bf16[1,1,1536,1536]{3,2,1,0:T(8,128)(2,1)}, u32[]{:S(2)}) copy-start(bf16[1,1,1536,1536]{3,2,1,0:T(8,128)(2,1)} %all-gather.6.cloned.1.call-done) | copy-start | bytes 14155780
  109.5 12.7 %collective-permute-start = (bf16[96,256]{1,0:T(8,128)(2,1)S(1)}, bf16[96,256]{1,0:T(8,128)(2,1)S(1)}, u32[]{:S(2)}, u32[]{:S(2)}) collective-permute-start(bf16[96,256]{1,0:T(8,128)(2,1)S(1)} %fusion.51), channel_id=1, source_target_pairs={{0,16},{16,0},{32,48},{48,32},{64,80},{80,64},{96,112},{112,96},{1... | collective-permute-start | bytes 147464 | tf_op jit(solution)/shard_map/ppermute | solution.py:31
  160.9 8.5 %collective-permute-start.1 = (bf16[1536,256]{1,0:T(8,128)(2,1)S(1)}, bf16[1536,256]{1,0:T(8,128)(2,1)S(1)}, u32[]{:S(2)}, u32[]{:S(2)}) collective-permute-start(bf16[1536,256]{1,0:T(8,128)(2,1)S(1)} %bitcast.217), channel_id=1, source_target_pairs={{0,16},{16,0},{32,48},{48,32},{64,80},{80,64},{96,112},{112,96},{1... | collective-permute-start | bytes 2359304 | tf_op jit(solution)/shard_map/ppermute | solution.py:31
  167.4 1.1 copy-start.2
  209.9 6.5 %collective-permute-start.2 = (bf16[384,256]{1,0:T(8,128)(2,1)S(1)}, bf16[384,256]{1,0:T(8,128)(2,1)S(1)}, u32[]{:S(2)}, u32[]{:S(2)}) collective-permute-start(bf16[384,256]{1,0:T(8,128)(2,1)S(1)} %slice.437), channel_id=1, source_target_pairs={{0,16},{16,0},{32,48},{48,32},{64,80},{80,64},{96,112},{112,96},{1... | collective-permute-start | bytes 589832 | tf_op jit(solution)/shard_map/ppermute | solution.py:31
  236.2 11.9 %all-to-all-start.1 = ((bf16[4,16,16,96]{3,2,1,0:T(8,128)(2,1)}), bf16[4,16,16,96]{3,2,1,0:T(8,128)(2,1)S(1)}, u32[]{:S(2)}, u32[]{:S(2)}) async-start(bf16[4,16,16,96]{3,2,1,0:T(8,128)(2,1)} %broadcast_in_dim.70), calls=%async_computation.1 | async-start | bytes 524288 | tf_op jit(solution)/shard_map/all_to_all | solution.py:41
  265.0 9.4 %all-to-all-start.3 = ((bf16[8,64,96]{2,1,0:T(8,128)(2,1)}), bf16[8,64,96]{2,1,0:T(8,128)(2,1)S(1)}, u32[]{:S(2)}, u32[]{:S(2)}) async-start(bf16[8,64,96]{2,1,0:T(8,128)(2,1)} %broadcast_in_dim.77), calls=%async_computation.3 | async-start | bytes 262144 | tf_op jit(solution)/shard_map/all_to_all | solution.py:41
  277.6 10.4 %all-to-all-start.4 = ((bf16[16,32,96]{2,1,0:T(8,128)(2,1)}), bf16[16,32,96]{2,1,0:T(8,128)(2,1)S(1)}, u32[]{:S(2)}, u32[]{:S(2)}) async-start(bf16[16,32,96]{2,1,0:T(8,128)(2,1)} %fusion.43), calls=%async_computation.4 | async-start | bytes 262144 | tf_op jit(solution)/shard_map/all_to_all | solution.py:41
  288.7 10.2 %all-to-all-start.5 = ((bf16[16,32,96]{2,1,0:T(8,128)(2,1)}), bf16[16,32,96]{2,1,0:T(8,128)(2,1)S(1)}, u32[]{:S(2)}, u32[]{:S(2)}) async-start(bf16[16,32,96]{2,1,0:T(8,128)(2,1)} %broadcast_in_dim.80), calls=%async_computation.5 | async-start | bytes 262144 | tf_op jit(solution)/shard_map/all_to_all | solution.py:41
  294.4 24.8 %copy-start.3 = (bf16[1,1,189,1536]{3,2,1,0:T(8,128)(2,1)S(1)}, bf16[1,1,189,1536]{3,2,1,0:T(8,128)(2,1)}, u32[]{:S(2)}) copy-start(bf16[1,1,189,1536]{3,2,1,0:T(8,128)(2,1)} %param.8) | copy-start | bytes 1741828
  294.4 24.8 %copy-start.5 = (bf16[1536,256]{1,0:T(8,128)(2,1)S(1)}, bf16[1536,256]{1,0:T(8,128)(2,1)}, u32[]{:S(2)}) copy-start(bf16[1536,256]{1,0:T(8,128)(2,1)} %all_gather.24) | copy-start | bytes 2359300
  299.6 19.7 %copy-start.7 = (bf16[1536,256]{1,0:T(8,128)(2,1)S(1)}, bf16[1536,256]{1,0:T(8,128)(2,1)}, u32[]{:S(2)}) copy-start(bf16[1536,256]{1,0:T(8,128)(2,1)} %all_gather.25) | copy-start | bytes 2359300
  315.3 11.7 %all-to-all-start.7 = ((bf16[32,16,96]{2,1,0:T(8,128)(2,1)}), bf16[32,16,96]{2,1,0:T(8,128)(2,1)S(1)}, u32[]{:S(2)}, u32[]{:S(2)}) async-start(bf16[32,16,96]{2,1,0:T(8,128)(2,1)} %broadcast_in_dim.83), calls=%async_computation.7 | async-start | bytes 262144 | tf_op jit(solution)/shard_map/all_to_all | solution.py:41
  328.5 1.1 copy-start.8
  328.5 1.1 copy-start.9
  328.8 8.7 %copy-start.11 = (f32[48,256]{1,0:T(8,128)S(1)}, f32[48,256]{1,0:T(8,128)}, u32[]{:S(2)}) copy-start(f32[48,256]{1,0:T(8,128)} %get-tuple-element.53) | copy-start | bytes 147460
  329.1 8.4 %copy-start.12 = (f32[48,256]{1,0:T(8,128)S(1)}, f32[48,256]{1,0:T(8,128)}, u32[]{:S(2)}) copy-start(f32[48,256]{1,0:T(8,128)} %get-tuple-element.51) | copy-start | bytes 147460
  329.1 8.4 %copy-start.13 = (f32[96,256]{1,0:T(8,128)S(1)}, f32[96,256]{1,0:T(8,128)}, u32[]{:S(2)}) copy-start(f32[96,256]{1,0:T(8,128)} %convolution_bitcast_fusion) | copy-start | bytes 294916
  331.5 17.3 %all-to-all-start.8 = ((bf16[16,2,720]{2,1,0:T(2,128)(2,1)}), bf16[16,2,720]{2,1,0:T(2,128)(2,1)S(1)}, u32[]{:S(2)}, u32[]{:S(2)}) async-start(bf16[16,2,720]{2,1,0:T(2,128)(2,1)} %reshape.168), calls=%async_computation.8 | async-start | bytes 98304 | tf_op jit(solution)/shard_map/all_to_all | solution.py:189
Sparse Core Ops, SparseCore 0:
  9.4 86.3 all-gather.5
  97.9 121.4 all-gather.7

commit v4 on v3

--- a/solution.py
+++ b/solution.py
@@ -2,6 +2,8 @@
 import jax.numpy as jnp
 import numpy as np
 from jax import lax
+from jax.experimental import pallas as pl
+from jax.experimental.pallas import tpu as pltpu
 from jax.sharding import PartitionSpec as P
 
 F32 = jnp.float32
@@ -43,6 +45,50 @@
 
 def leaf_everyone(block, size):
     return leaf_scatter(jnp.broadcast_to(block, (size, *block.shape)))
+
+
+def pack_upper(off_diag, inv_diag, live, pairs, d_start):
+    strip, width = off_diag.shape[2], inv_diag.shape[3]
+    d_rows = inv_diag.shape[2] - d_start
+    first = min(column_start(m, l, width) for m, l in pairs) // 128 * 128
+    span = off_diag.shape[3] - first
+    total = sum(width >> l for _, l in pairs)
+
+    def body(live_ref, off_ref, inv_ref, out_ref, p_ref, d_ref, sems):
+        p_copy = pltpu.make_async_copy(off_ref.at[0, 0, :, pl.ds(first, span)], p_ref, sems.at[0])
+        d_copy = pltpu.make_async_copy(inv_ref.at[0, 0, pl.ds(d_start, d_rows), :], d_ref, sems.at[1])
+        p_copy.start()
+        d_copy.start()
+        d_copy.wait()
+        out_ref[strip:, :] = jnp.zeros((out_ref.shape[0] - strip, total), BF16)
+        out_ref[strip : strip + d_rows, :width] = d_ref[...]
+        p_copy.wait()
+        at = 0
+        for m, l in pairs:
+            low = column_start(m, l, width) - first
+            wide = width >> l
+            alive = live_ref[m * (m - 1) // 2 + l].astype(F32)
+            block = p_ref[:, low : low + wide].astype(F32) * alive
+            out_ref[:strip, at : at + wide] = block.astype(BF16)
+            at += wide
+
+    tall = (strip + d_rows + 15) // 16 * 16
+    return pl.pallas_call(
+        body,
+        out_shape=jax.ShapeDtypeStruct((tall, total), BF16),
+        in_specs=[
+            pl.BlockSpec(memory_space=pltpu.SMEM),
+            pl.BlockSpec(memory_space=pl.ANY),
+            pl.BlockSpec(memory_space=pl.ANY),
+        ],
+        out_specs=pl.BlockSpec(memory_space=pltpu.VMEM),
+        scratch_shapes=[
+            pltpu.VMEM((strip, span), BF16),
+            pltpu.VMEM((d_rows, width), BF16),
+            pltpu.SemaphoreType.DMA((2,)),
+        ],
+        name="pack_upper",
+    )(live, off_diag, inv_diag)
 
 
 def shards(rhs, inv_diag, off_diag, pair_mask):
@@ -68,8 +114,11 @@
         first = column_start(m, l, width)
         return panels[:, first : first + (width >> l)]
 
-    def alive(m, l, dtype):
-        return live[m * (m - 1) // 2 + l].astype(dtype)
+    def mask_rows(l):
+        ancestors = range(l + 1, levels + 1)
+        index = jnp.asarray(np.repeat([m * (m - 1) // 2 + l for m in ancestors], strip), jnp.int32)
+        hit = index[:, None] == lax.broadcasted_iota(jnp.int32, (1, live.shape[0]), 1)
+        return jnp.where(hit, live[None], 0).sum(axis=1, keepdims=True).astype(F32)
 
     def by_core(one, two):
         return jnp.where(first_core, one, two)
@@ -83,19 +132,8 @@
     upper_pairs = sorted(
         ((m, l) for l in range(2, levels) for m in range(l + 1, levels + 1)), key=lambda p: (p[1], p[0])
     )
-    p_cols = sum(width >> l for _, l in upper_pairs)
-    pieces = [
-        jnp.concatenate([panel(m, l) * alive(m, l, BF16) for m, l in upper_pairs], axis=1)
-    ]
-    d_first = {}
-    at = strip
-    for m in range(2, levels + 1):
-        d_first[m] = at
-        room = -heights[m] % 8
-        rows = d_all[starts[m] : starts[m] + heights[m]]
-        pieces.append(jnp.pad(rows, ((0, room), (0, p_cols - width))))
-        at += heights[m] + room
-    packed = jnp.concatenate(pieces, axis=0)
+    d_first = {m: strip + starts[m] - starts[2] for m in range(2, levels + 1)}
+    packed = pack_upper(off_diag, inv_diag, live, upper_pairs, starts[2])
     packed, z0_left = lax.optimization_barrier((packed, z0_left))
     everyone = lax.all_gather(packed, "row", axis=0, tiled=False)
 
@@ -111,7 +149,8 @@
 
     z0_sent = by_core(z0_right, z0_left)
     z0_kept = by_core(z0_left, z0_right)
-    live1 = alive(1, 0, F32)
+    mask0, mask1 = lax.optimization_barrier((mask_rows(0), mask_rows(1)))
+    live1 = mask0[:strip]
     yb_sent = dot(d_full0, z0_sent).astype(BF16)
     sent = placed[:strip, half:] - dot(panel(1, 0), yb_sent) * live1
     got = core_swap(sent.astype(BF16))
@@ -119,7 +158,7 @@
     kept = placed[:strip, :half] - dot(panel(1, 0), yb_kept) * live1
     yb0 = jnp.concatenate([yb_kept, yb_sent], axis=1)
     parts = [
-        placed[strip * (m - 1) : strip * m] - dot(panel(m, 0), yb0) * alive(m, 0, F32)
+        placed[strip * (m - 1) : strip * m] - dot(panel(m, 0), yb0) * mask0[strip * (m - 1) : strip * m]
         for m in range(2, levels + 1)
     ]
 
@@ -136,7 +175,11 @@
     out0_kept = dot(d_own0, z0_kept)
     out0_sent = dot(d_own0, z0_sent)
     part = jnp.concatenate(
-        [parts[m - 2] - dot(panel(m, 1), yb1) * alive(m, 1, F32) for m in range(2, levels + 1)], axis=0
+        [
+            parts[m - 2] - dot(panel(m, 1), yb1) * mask1[strip * (m - 2) : strip * (m - 1)]
+            for m in range(2, levels + 1)
+        ],
+        axis=0,
     )
     part = part[:, :half] + core_swap(part[:, half:].astype(BF16)).astype(F32)
     p_rows = strip * (levels - 1)

time: 359 us -> 349 us (0.972)
  other arithmetic: 8.68 us -> 1.78 us
  between operations: 19.6 us -> 14.1 us
  waiting for transfers between devices: 29.8 us -> 35 us
  local copies, waits for them, and re-layouts: 25.3 us -> 21 us
    mul x3 -> x0, other arithmetic: 6.42 us -> none  [shards(): panel(m, l) * alive(m, l, BF16)]
    all_gather x1, blocking collectives: 45.1 us -> 39.4 us  [shards(): z0_left = lax.all_gather(b0[:, :half], 'row', axis=0, tiled=True)]
    all_gather x1, waiting for transfers between devices: 0.01 us -> 5.46 us  [shards(): d_full0 = lax.all_gather(d_own0, 'row', axis=0, tiled=True)]
    slice x6 -> x0, local copies, waits for them, and re-layouts: 4.59 us -> none  [the longest x4 3.26 us: shards(): rows = d_all[starts[m]:starts[m] + heights[m]]]
    all_gather x1, blocking collectives: 33.6 us -> 37.3 us  [shards(): z0_right = lax.all_gather(b0[:, half:], 'row', axis=0, tiled=True)]
  transfers between devices with their start and end apart: 11 -> 11, of which waited for: 7 -> 8; matrix products, arithmetic and copies ran while one was open for 11% -> 9% of each run, Pallas kernels for 0% -> 1%
where the time goes in v4:
time: 349 us; the launch traced here: 348 us
  blocking collectives  195 us (56%)
  starting transfers between devices  49.1 us (14%)
  waiting for transfers between devices  35 us (10%)
  matrix products  29 us (8%)
  local copies, waits for them, and re-layouts  21 us (6%)
  between operations  14.1 us (4%)
    all_gather x1, blocking collectives, shards(): z0_left = lax.all_gather(b0[:, :half], 'row', axis=0, tiled=True)  39.4 us
    all_gather x1, blocking collectives, shards(): yb1 = lax.all_gather(yb1, 'row', axis=0, tiled=True)  38.3 us
    all_gather x1, blocking collectives, shards(): z0_right = lax.all_gather(b0[:, half:], 'row', axis=0, tiled=True)  37.3 us
    all_gather x1, blocking collectives, shards(): z1 = lax.all_gather(z1, 'row', axis=0, tiled=False)  35.5 us
    all_to_all x2, blocking collectives, leaf_scatter(): lax.all_to_all(pieces, 'leaf', 0, 0, tiled=True, axis_index_groups=leaf_g...  25.1 us
    all_to_all x5, starting transfers between devices, leaf_scatter(): lax.all_to_all(pieces, 'leaf', 0, 0, tiled=True, axis_index_groups=leaf_g...  23 us
    ppermute x3, starting transfers between devices, core_swap(): return lax.ppermute(block, 'leaf', [(i, i ^ 1) for i in range(count)])  20.3 us
    all_to_all x1, blocking collectives, shards(): turned = lax.all_to_all(turned, 'row', 0, 0, tiled=True)  19.5 us
  transfers between devices with their start and end apart: 11, of which 8 were waited for; matrix products, arithmetic and copies ran while one was open for 9% of the time, Pallas kernels for 1%

profile of v4, /device:TPU:1, one launch (start us, length us, event | category | flops | bytes accessed | tf_op | source)
XLA Modules:
  0.0 347.9 jit_solution(14142093448992949008)
XLA Ops:
  6.5 1.7 slice.162
  8.4 3.0 pack_upper.1
  11.5 39.4 %all_gather.24 = bf16[1536,256]{1,0:T(8,128)(2,1)} all-gather(bf16[96,256]{1,0:T(8,128)(2,1)S(1)} %get-tuple-element.30), channel_id=1, replica_groups=mesh['leaf'=32,'row'=16] {'row'}, dimensions={0}, use_global_device_ids=true | all-gather | bytes 835584 | tf_op jit(solution)/shard_map/all_gather | solution.py:129
  51.3 1.3 fusion.64
  52.6 37.3 %all_gather.25 = bf16[1536,256]{1,0:T(8,128)(2,1)} all-gather(bf16[96,256]{1,0:T(8,128)(2,1)S(1)} %get-tuple-element.29), channel_id=1, replica_groups=mesh['leaf'=32,'row'=16] {'row'}, dimensions={0}, use_global_device_ids=true | all-gather | bytes 835584 | tf_op jit(solution)/shard_map/all_gather | solution.py:130
  89.9 5.5 %all-gather.6.cloned.1.call-done = bf16[1,1,1536,1536]{3,2,1,0:T(8,128)(2,1)} async-done(((bf16[1,1,96,1536]{3,2,1,0:T(8,128)(2,1)}), bf16[1,1,1536,1536]{3,2,1,0:T(8,128)(2,1)}) %all-gather.6.cloned.1.call-update) | async-done | bytes 4718608 | tf_op jit(solution)/shard_map/all_gather | solution.py:127
  95.4 4.2 %fusion.7 = bf16[256,1536]{1,0:T(8,128)(2,1)S(1)} fusion(bf16[1,1,1536,1536]{3,2,1,0:T(8,128)(2,1)} %all-gather.6.cloned.1.call-done, bf16[1536,256]{1,0:T(8,128)(2,1)} %all_gather.25, bf16[1536,256]{1,0:T(8,128)(2,1)} %all_gather.24, pred[]{:T(512)S(6)} %eq.51), kind=kOutput, calls=%fused_computation.5 | convolution fusion | flops 1208745984 | bytes 7077889 | tf_op jit(solution)/shard_map/dot_general | solution.py:24
  99.6 0.4 fusion.51
  100.0 8.8 %collective-permute-start = (bf16[96,256]{1,0:T(8,128)(2,1)S(1)}, bf16[96,256]{1,0:T(8,128)(2,1)S(1)}, u32[]{:S(2)}, u32[]{:S(2)}) collective-permute-start(bf16[96,256]{1,0:T(8,128)(2,1)S(1)} %fusion.51), channel_id=1, source_target_pairs={{0,16},{16,0},{32,48},{48,32},{64,80},{80,64},{96,112},{112,96},{1... | collective-permute-start | bytes 147464 | tf_op jit(solution)/shard_map/ppermute | solution.py:33
  108.8 3.8 %fusion.4 = bf16[256,1536]{1,0:T(8,128)(2,1)S(1)} fusion(bf16[1,1,1536,1536]{3,2,1,0:T(8,128)(2,1)} %all-gather.6.cloned.1.call-done, bf16[1536,256]{1,0:T(8,128)(2,1)S(1)} %copy-done.3, bf16[1536,256]{1,0:T(8,128)(2,1)S(1)} %copy-done.5, pred[]{:T(512)S(6)} %eq.51), kind=kOutput, calls=%fused_computation.4 | convolution fusion | flops 1208745984 | bytes 7077889 | tf_op jit(solution)/shard_map/dot_general | solution.py:24
  112.6 0.6 fusion.40
  113.2 0.4 add_convert_fusion
  113.6 35.5 %all-gather.1 = bf16[1536,256]{1,0:T(8,128)(2,1)S(1)} all-gather(bf16[96,256]{1,0:T(8,128)(2,1)S(1)} %add_convert_fusion), channel_id=3, replica_groups=mesh['leaf'=32,'row'=16] {'row'}, dimensions={0}, use_global_device_ids=true | all-gather | bytes 835584 | tf_op jit(solution)/shard_map/all_gather | solution.py:167
  149.1 6.0 %collective-permute-start.1 = (bf16[1536,256]{1,0:T(8,128)(2,1)S(1)}, bf16[1536,256]{1,0:T(8,128)(2,1)S(1)}, u32[]{:S(2)}, u32[]{:S(2)}) collective-permute-start(bf16[1536,256]{1,0:T(8,128)(2,1)S(1)} %bitcast.224), channel_id=1, source_target_pairs={{0,16},{16,0},{32,48},{48,32},{64,80},{80,64},{96,112},{112,96},{1... | collective-permute-start | bytes 2359304 | tf_op jit(solution)/shard_map/ppermute | solution.py:33
  155.1 0.6 fusion.42
  155.7 0.6 fusion.38
  156.4 0.6 fusion.36
  157.0 0.5 copy-done.1
  157.4 0.9 fusion.93
  158.3 0.9 fusion.92
  159.2 38.3 %all_gather.29 = bf16[768,512]{1,0:T(8,128)(2,1)S(1)} all-gather(bf16[48,512]{1,0:T(8,128)(2,1)S(1)} %pad_maximum_fusion.2), channel_id=1, replica_groups=mesh['leaf'=32,'row'=16] {'row'}, dimensions={0}, use_global_device_ids=true | all-gather | bytes 835584 | tf_op jit(solution)/shard_map/all_gather | solution.py:174
  198.7 5.5 %collective-permute-start.2 = (bf16[384,256]{1,0:T(8,128)(2,1)S(1)}, bf16[384,256]{1,0:T(8,128)(2,1)S(1)}, u32[]{:S(2)}, u32[]{:S(2)}) collective-permute-start(bf16[384,256]{1,0:T(8,128)(2,1)S(1)} %slice.329), channel_id=1, source_target_pairs={{0,16},{16,0},{32,48},{48,32},{64,80},{80,64},{96,112},{112,96},{1... | collective-permute-start | bytes 589832 | tf_op jit(solution)/shard_map/ppermute | solution.py:33
  204.2 1.0 collective-permute-done.2
  205.5 19.5 %all_to_all.45 = bf16[16,16,384]{2,1,0:T(8,128)(2,1)S(1)} all-to-all(bf16[16,16,384]{2,1,0:T(8,128)(2,1)S(1)} %bitcast.240), channel_id=1, replica_groups=mesh['leaf'=32,'row'=16] {'row'}, dimensions={0} | all-to-all | bytes 393216 | tf_op jit(solution)/shard_map/all_to_all | solution.py:188
  225.1 0.7 broadcast_in_dim.102
  225.9 6.9 %all-to-all-start.1 = ((bf16[4,16,16,96]{3,2,1,0:T(8,128)(2,1)}), bf16[4,16,16,96]{3,2,1,0:T(8,128)(2,1)S(1)}, u32[]{:S(2)}, u32[]{:S(2)}) async-start(bf16[4,16,16,96]{3,2,1,0:T(8,128)(2,1)} %broadcast_in_dim.102), calls=%async_computation.1 | async-start | bytes 524288 | tf_op jit(solution)/shard_map/all_to_all | solution.py:43
  233.0 4.8 %all-to-all-done.1 = bf16[4,16,16,96]{3,2,1,0:T(8,128)(2,1)S(1)} async-done(((bf16[4,16,16,96]{3,2,1,0:T(8,128)(2,1)}), bf16[4,16,16,96]{3,2,1,0:T(8,128)(2,1)S(1)}, u32[]{:S(2)}, u32[]{:S(2)}) %all-to-all-start.1) | async-done | bytes 196640 | tf_op jit(solution)/shard_map/all_to_all | solution.py:43
  238.1 0.6 copy.53
  238.7 0.7 reshape.113
  239.5 1.4 slice.232
  240.8 0.5 convolution_convert_fusion
  241.3 2.0 fusion.44
  243.3 10.9 %all_to_all.46 = bf16[8,64,96]{2,1,0:T(8,128)(2,1)S(1)} all-to-all(bf16[8,64,96]{2,1,0:T(8,128)(2,1)S(1)} %bitcast.242), channel_id=1, replica_groups={{0,16,32,48,64,80,96,112},{128,144,160,176,192,208,224,240},{256,272,28..., dimensions={0} | all-to-all | bytes 196608 | tf_op jit(solution)/shard_map/all_to_all | solution.py:43
  254.2 0.7 broadcast_in_dim.109
  254.9 4.1 %all-to-all-start.3 = ((bf16[8,64,96]{2,1,0:T(8,128)(2,1)}), bf16[8,64,96]{2,1,0:T(8,128)(2,1)S(1)}, u32[]{:S(2)}, u32[]{:S(2)}) async-start(bf16[8,64,96]{2,1,0:T(8,128)(2,1)} %broadcast_in_dim.109), calls=%async_computation.3 | async-start | bytes 262144 | tf_op jit(solution)/shard_map/all_to_all | solution.py:43
  259.1 1.9 fusion.12
  261.0 1.2 slice.235
  262.3 2.0 all-to-all-done.3
  265.3 2.2 fusion.43
  267.5 4.2 %all-to-all-start.4 = ((bf16[16,32,96]{2,1,0:T(8,128)(2,1)}), bf16[16,32,96]{2,1,0:T(8,128)(2,1)S(1)}, u32[]{:S(2)}, u32[]{:S(2)}) async-start(bf16[16,32,96]{2,1,0:T(8,128)(2,1)} %fusion.43), calls=%async_computation.4 | async-start | bytes 262144 | tf_op jit(solution)/shard_map/all_to_all | solution.py:43
  271.7 1.9 fusion.10
  273.6 1.3 slice.239
  275.0 2.9 all-to-all-done.4
  277.9 0.7 broadcast_in_dim.112
  278.6 4.0 %all-to-all-start.5 = ((bf16[16,32,96]{2,1,0:T(8,128)(2,1)}), bf16[16,32,96]{2,1,0:T(8,128)(2,1)S(1)}, u32[]{:S(2)}, u32[]{:S(2)}) async-start(bf16[16,32,96]{2,1,0:T(8,128)(2,1)} %broadcast_in_dim.112), calls=%async_computation.5 | async-start | bytes 262144 | tf_op jit(solution)/shard_map/all_to_all | solution.py:43
  282.6 1.7 convolution_add_fusion.1
  284.3 4.4 %all-to-all-done.5 = bf16[16,32,96]{2,1,0:T(8,128)(2,1)S(1)} async-done(((bf16[16,32,96]{2,1,0:T(8,128)(2,1)}), bf16[16,32,96]{2,1,0:T(8,128)(2,1)S(1)}, u32[]{:S(2)}, u32[]{:S(2)}) %all-to-all-start.5) | async-done | bytes 98336 | tf_op jit(solution)/shard_map/all_to_all | solution.py:43
  289.7 1.4 fusion.26
  291.2 14.1 %all_to_all.47 = bf16[32,16,96]{2,1,0:T(8,128)(2,1)S(1)} all-to-all(bf16[32,16,96]{2,1,0:T(8,128)(2,1)S(1)} %bitcast.241), channel_id=1, replica_groups={{0,16,32,48,64,80,96,112,128,144,160,176,192,208,224,240,256,272,288,30..., dimensions={0} | all-to-all | bytes 196608 | tf_op jit(solution)/shard_map/all_to_all | solution.py:43
  305.3 0.7 broadcast_in_dim.115
  306.0 3.9 %all-to-all-start.7 = ((bf16[32,16,96]{2,1,0:T(8,128)(2,1)}), bf16[32,16,96]{2,1,0:T(8,128)(2,1)S(1)}, u32[]{:S(2)}, u32[]{:S(2)}) async-start(bf16[32,16,96]{2,1,0:T(8,128)(2,1)} %broadcast_in_dim.115), calls=%async_computation.7 | async-start | bytes 262144 | tf_op jit(solution)/shard_map/all_to_all | solution.py:43
  309.9 0.9 convolution_bitcast_fusion
  310.9 1.1 slice.244
  312.0 0.8 reshape.115
  312.9 0.8 reshape.137
  313.8 0.8 reshape.138
  314.6 3.1 all-to-all-done.7
  317.7 1.1 copy.60
  318.8 0.3 reshape_reshape.11
  320.3 1.1 maximum_bitcast_fusion.1
  321.4 0.8 reshape.140
  322.2 5.7 %all-to-all-start.8 = ((bf16[16,2,720]{2,1,0:T(2,128)(2,1)}), bf16[16,2,720]{2,1,0:T(2,128)(2,1)S(1)}, u32[]{:S(2)}, u32[]{:S(2)}) async-start(bf16[16,2,720]{2,1,0:T(2,128)(2,1)} %reshape.140), calls=%async_computation.8 | async-start | bytes 98304 | tf_op jit(solution)/shard_map/all_to_all | solution.py:232
  328.3 11.2 %all-to-all-done.8 = bf16[16,2,720]{2,1,0:T(2,128)(2,1)S(1)} async-done(((bf16[16,2,720]{2,1,0:T(2,128)(2,1)}), bf16[16,2,720]{2,1,0:T(2,128)(2,1)S(1)}, u32[]{:S(2)}, u32[]{:S(2)}) %all-to-all-start.8) | async-done | bytes 46112 | tf_op jit(solution)/shard_map/all_to_all | solution.py:232
  339.9 1.1 copy.69
  (101 shorter events, 6.9 us)
Async XLA Ops:
  6.5 4.9 %copy-start.9 = (bf16[1,1,189,512]{3,2,1,0:T(8,128)(2,1)S(1)}, bf16[1,1,189,512]{3,2,1,0:T(8,128)(2,1)}, u32[]{:S(2)}) copy-start(bf16[1,1,189,512]{3,2,1,0:T(8,128)(2,1)} %param.9) | copy-start | bytes 580612
  6.5 88.9 %all-gather.6.cloned.1.call-start = ((), (), s32[]{:S(2)}) async-start(), calls=%async_computation.9 | async-start | bytes 5013504 | tf_op jit(solution)/shard_map/all_gather | solution.py:127
  8.3 231.2 %all-gather.8.cloned.1.call-start = ((), (), s32[]{:S(2)}) async-start(), calls=%async_computation.10 | async-start | bytes 8146944 | tf_op jit(solution)/shard_map/all_gather | solution.py:138
  8.3 42.5 %copy-start.13 = (s32[1,1,15]{2,1,0:T(1,128)S(1)}, s32[1,1,15]{2,1,0:T(1,128)}, u32[]{:S(2)}) copy-start(s32[1,1,15]{2,1,0:T(1,128)} %param.12) | copy-start | bytes 184
  8.4 42.5 %copy-start.15 = (s32[384]{0:T(512)S(1)}, s32[384]{0:T(512)}, u32[]{:S(2)}) copy-start(s32[384]{0:T(512)} %constant.31.clone) | copy-start | bytes 4612
  8.4 42.6 %copy-start.14 = (s32[480]{0:T(512)S(1)}, s32[480]{0:T(512)}, u32[]{:S(2)}) copy-start(s32[480]{0:T(512)} %constant.30.clone) | copy-start | bytes 5764
  8.4 42.7 %copy-start.16 = (s32[93]{0:T(128)S(1)}, s32[93]{0:T(128)}, u32[]{:S(2)}) copy-start(s32[93]{0:T(128)} %constant.27.clone) | copy-start | bytes 1120
  8.4 42.7 %copy-start.17 = (s32[93]{0:T(128)S(1)}, s32[93]{0:T(128)}, u32[]{:S(2)}) copy-start(s32[93]{0:T(128)} %constant.28.clone) | copy-start | bytes 1120
  8.4 42.7 %copy-start.18 = (s32[93]{0:T(128)S(1)}, s32[93]{0:T(128)}, u32[]{:S(2)}) copy-start(s32[93]{0:T(128)} %constant.29.clone) | copy-start | bytes 1120
  89.9 9.7 %copy-start = (bf16[1,1,96,12384]{3,2,1,0:T(8,128)(2,1)S(1)}, bf16[1,1,96,12384]{3,2,1,0:T(8,128)(2,1)}, u32[]{:S(2)}) copy-start(bf16[1,1,96,12384]{3,2,1,0:T(8,128)(2,1)} %off_ref.1) | copy-start | bytes 7133188
  95.4 4.2 %copy-start.2 = (f32[480,512]{1,0:T(8,128)S(1)}, f32[480,512]{1,0:T(8,128)}, u32[]{:S(2)}) copy-start(f32[480,512]{1,0:T(8,128)} %fusion.64) | copy-start | bytes 2949124
  95.4 13.4 %copy-start.3 = (bf16[1536,256]{1,0:T(8,128)(2,1)S(1)}, bf16[1536,256]{1,0:T(8,128)(2,1)}, u32[]{:S(2)}) copy-start(bf16[1536,256]{1,0:T(8,128)(2,1)} %all_gather.24) | copy-start | bytes 2359300
  95.4 13.4 %copy-start.5 = (bf16[1536,256]{1,0:T(8,128)(2,1)S(1)}, bf16[1536,256]{1,0:T(8,128)(2,1)}, u32[]{:S(2)}) copy-start(bf16[1536,256]{1,0:T(8,128)(2,1)} %all_gather.25) | copy-start | bytes 2359300
  100.0 13.2 %collective-permute-start = (bf16[96,256]{1,0:T(8,128)(2,1)S(1)}, bf16[96,256]{1,0:T(8,128)(2,1)S(1)}, u32[]{:S(2)}, u32[]{:S(2)}) collective-permute-start(bf16[96,256]{1,0:T(8,128)(2,1)S(1)} %fusion.51), channel_id=1, source_target_pairs={{0,16},{16,0},{32,48},{48,32},{64,80},{80,64},{96,112},{112,96},{1... | collective-permute-start | bytes 147464 | tf_op jit(solution)/shard_map/ppermute | solution.py:33
  149.1 9.2 %collective-permute-start.1 = (bf16[1536,256]{1,0:T(8,128)(2,1)S(1)}, bf16[1536,256]{1,0:T(8,128)(2,1)S(1)}, u32[]{:S(2)}, u32[]{:S(2)}) collective-permute-start(bf16[1536,256]{1,0:T(8,128)(2,1)S(1)} %bitcast.224), channel_id=1, source_target_pairs={{0,16},{16,0},{32,48},{48,32},{64,80},{80,64},{96,112},{112,96},{1... | collective-permute-start | bytes 2359304 | tf_op jit(solution)/shard_map/ppermute | solution.py:33
  156.4 1.1 copy-start.1
  198.7 6.5 %collective-permute-start.2 = (bf16[384,256]{1,0:T(8,128)(2,1)S(1)}, bf16[384,256]{1,0:T(8,128)(2,1)S(1)}, u32[]{:S(2)}, u32[]{:S(2)}) collective-permute-start(bf16[384,256]{1,0:T(8,128)(2,1)S(1)} %slice.329), channel_id=1, source_target_pairs={{0,16},{16,0},{32,48},{48,32},{64,80},{80,64},{96,112},{112,96},{1... | collective-permute-start | bytes 589832 | tf_op jit(solution)/shard_map/ppermute | solution.py:33
  225.9 11.9 %all-to-all-start.1 = ((bf16[4,16,16,96]{3,2,1,0:T(8,128)(2,1)}), bf16[4,16,16,96]{3,2,1,0:T(8,128)(2,1)S(1)}, u32[]{:S(2)}, u32[]{:S(2)}) async-start(bf16[4,16,16,96]{3,2,1,0:T(8,128)(2,1)} %broadcast_in_dim.102), calls=%async_computation.1 | async-start | bytes 524288 | tf_op jit(solution)/shard_map/all_to_all | solution.py:43
  254.9 9.4 %all-to-all-start.3 = ((bf16[8,64,96]{2,1,0:T(8,128)(2,1)}), bf16[8,64,96]{2,1,0:T(8,128)(2,1)S(1)}, u32[]{:S(2)}, u32[]{:S(2)}) async-start(bf16[8,64,96]{2,1,0:T(8,128)(2,1)} %broadcast_in_dim.109), calls=%async_computation.3 | async-start | bytes 262144 | tf_op jit(solution)/shard_map/all_to_all | solution.py:43
  267.5 10.4 %all-to-all-start.4 = ((bf16[16,32,96]{2,1,0:T(8,128)(2,1)}), bf16[16,32,96]{2,1,0:T(8,128)(2,1)S(1)}, u32[]{:S(2)}, u32[]{:S(2)}) async-start(bf16[16,32,96]{2,1,0:T(8,128)(2,1)} %fusion.43), calls=%async_computation.4 | async-start | bytes 262144 | tf_op jit(solution)/shard_map/all_to_all | solution.py:43
  278.6 10.2 %all-to-all-start.5 = ((bf16[16,32,96]{2,1,0:T(8,128)(2,1)}), bf16[16,32,96]{2,1,0:T(8,128)(2,1)S(1)}, u32[]{:S(2)}, u32[]{:S(2)}) async-start(bf16[16,32,96]{2,1,0:T(8,128)(2,1)} %broadcast_in_dim.112), calls=%async_computation.5 | async-start | bytes 262144 | tf_op jit(solution)/shard_map/all_to_all | solution.py:43
  284.3 25.6 %copy-start.4 = (bf16[1536,256]{1,0:T(8,128)(2,1)S(1)}, bf16[1536,256]{1,0:T(8,128)(2,1)}, u32[]{:S(2)}) copy-start(bf16[1536,256]{1,0:T(8,128)(2,1)} %all_gather.24) | copy-start | bytes 2359300
  289.5 20.5 %copy-start.6 = (bf16[1536,256]{1,0:T(8,128)(2,1)S(1)}, bf16[1536,256]{1,0:T(8,128)(2,1)}, u32[]{:S(2)}) copy-start(bf16[1536,256]{1,0:T(8,128)(2,1)} %all_gather.25) | copy-start | bytes 2359300
  306.0 11.7 %all-to-all-start.7 = ((bf16[32,16,96]{2,1,0:T(8,128)(2,1)}), bf16[32,16,96]{2,1,0:T(8,128)(2,1)S(1)}, u32[]{:S(2)}, u32[]{:S(2)}) async-start(bf16[32,16,96]{2,1,0:T(8,128)(2,1)} %broadcast_in_dim.115), calls=%async_computation.7 | async-start | bytes 262144 | tf_op jit(solution)/shard_map/all_to_all | solution.py:43
  319.2 1.1 copy-start.7
  319.2 1.1 copy-start.8
  319.5 8.7 %copy-start.10 = (f32[48,256]{1,0:T(8,128)S(1)}, f32[48,256]{1,0:T(8,128)}, u32[]{:S(2)}) copy-start(f32[48,256]{1,0:T(8,128)} %get-tuple-element.46) | copy-start | bytes 147460
  319.8 8.4 %copy-start.11 = (f32[48,256]{1,0:T(8,128)S(1)}, f32[48,256]{1,0:T(8,128)}, u32[]{:S(2)}) copy-start(f32[48,256]{1,0:T(8,128)} %get-tuple-element.44) | copy-start | bytes 147460
  319.8 8.4 %copy-start.12 = (f32[96,256]{1,0:T(8,128)S(1)}, f32[96,256]{1,0:T(8,128)}, u32[]{:S(2)}) copy-start(f32[96,256]{1,0:T(8,128)} %convolution_bitcast_fusion) | copy-start | bytes 294916
  322.2 17.3 %all-to-all-start.8 = ((bf16[16,2,720]{2,1,0:T(2,128)(2,1)}), bf16[16,2,720]{2,1,0:T(2,128)(2,1)S(1)}, u32[]{:S(2)}, u32[]{:S(2)}) async-start(bf16[16,2,720]{2,1,0:T(2,128)(2,1)} %reshape.140), calls=%async_computation.8 | async-start | bytes 98304 | tf_op jit(solution)/shard_map/all_to_all | solution.py:232
Sparse Core Ops, SparseCore 0:
  9.4 85.9 all-gather.5
  97.5 116.2 all-gather.7

commit v5 on v4

--- a/solution.py
+++ b/solution.py
@@ -49,39 +49,58 @@
 
 def pack_upper(off_diag, inv_diag, live, pairs, d_start):
     strip, width = off_diag.shape[2], inv_diag.shape[3]
+    mid = width // 2
+    top = max(m for m, _ in pairs)
     d_rows = inv_diag.shape[2] - d_start
+    d_top = strip >> top
+    d_low = d_rows - d_top
     first = min(column_start(m, l, width) for m, l in pairs) // 128 * 128
     span = off_diag.shape[3] - first
-    total = sum(width >> l for _, l in pairs)
-
-    def body(live_ref, off_ref, inv_ref, out_ref, p_ref, d_ref, sems):
+    low_pairs = [p for p in pairs if p[0] < top]
+    top_pairs = [p for p in pairs if p[0] == top]
+    low_cols = mid + sum(width >> l for _, l in low_pairs)
+    room = -2 * d_top % 8
+
+    def body(live_ref, off_ref, inv_ref, low_ref, top_ref, p_ref, d_ref, sems):
         p_copy = pltpu.make_async_copy(off_ref.at[0, 0, :, pl.ds(first, span)], p_ref, sems.at[0])
         d_copy = pltpu.make_async_copy(inv_ref.at[0, 0, pl.ds(d_start, d_rows), :], d_ref, sems.at[1])
         p_copy.start()
         d_copy.start()
         d_copy.wait()
-        out_ref[strip:, :] = jnp.zeros((out_ref.shape[0] - strip, total), BF16)
-        out_ref[strip : strip + d_rows, :width] = d_ref[...]
+        rows = d_ref[...].astype(F32)
+        pad = jnp.zeros((strip // 2 - d_low, mid), F32)
+        low = [rows[:d_low, :mid], pad, rows[:d_low, mid:], pad]
+        low_ref[:, :mid] = jnp.concatenate(low, axis=0).astype(BF16)
+        under = [rows[d_low:, :mid], rows[d_low:, mid:], jnp.zeros((room, mid), F32)]
+        top_ref[strip:, :] = jnp.concatenate(under, axis=0).astype(BF16)
         p_copy.wait()
-        at = 0
-        for m, l in pairs:
-            low = column_start(m, l, width) - first
-            wide = width >> l
-            alive = live_ref[m * (m - 1) // 2 + l].astype(F32)
-            block = p_ref[:, low : low + wide].astype(F32) * alive
-            out_ref[:strip, at : at + wide] = block.astype(BF16)
-            at += wide
-
-    tall = (strip + d_rows + 15) // 16 * 16
+
+        def put(ref, at, some):
+            for m, l in some:
+                start = column_start(m, l, width) - first
+                wide = width >> l
+                alive = live_ref[m * (m - 1) // 2 + l].astype(F32)
+                block = p_ref[:, start : start + wide].astype(F32) * alive
+                ref[:strip, at : at + wide] = block.astype(BF16)
+                at += wide
+            return at
+
+        put(low_ref, mid, low_pairs)
+        end = put(top_ref, 0, top_pairs)
+        top_ref[:strip, end:] = jnp.zeros((strip, mid - end), BF16)
+
     return pl.pallas_call(
         body,
-        out_shape=jax.ShapeDtypeStruct((tall, total), BF16),
+        out_shape=(
+            jax.ShapeDtypeStruct((strip, low_cols), BF16),
+            jax.ShapeDtypeStruct((strip + 2 * d_top + room, mid), BF16),
+        ),
         in_specs=[
             pl.BlockSpec(memory_space=pltpu.SMEM),
             pl.BlockSpec(memory_space=pl.ANY),
             pl.BlockSpec(memory_space=pl.ANY),
         ],
-        out_specs=pl.BlockSpec(memory_space=pltpu.VMEM),
+        out_specs=(pl.BlockSpec(memory_space=pltpu.VMEM), pl.BlockSpec(memory_space=pltpu.VMEM)),
         scratch_shapes=[
             pltpu.VMEM((strip, span), BF16),
             pltpu.VMEM((d_rows, width), BF16),
@@ -89,6 +108,82 @@
         ],
         name="pack_upper",
     )(live, off_diag, inv_diag)
+
+
+def level_zero(core, live, inverse, z_left, z_right, off_diag, placed):
+    rows_n, both, width = inverse.shape
+    half = z_left.shape[1]
+    strip = off_diag.shape[2]
+    under = both - strip
+    parts = 2
+    tall = width // parts
+    each = rows_n // parts
+
+    def body(core_ref, live_ref, inv_ref, left_ref, right_ref, off_ref, placed_ref, *rest):
+        y_ref, kept_ref, sent_ref, d1_ref, d_ref, zl_ref, zr_ref, p_ref, sems = rest
+
+        def d_copy(r):
+            dst = d_ref.at[pl.ds(strip * r, strip), :]
+            return pltpu.make_async_copy(inv_ref.at[r, pl.ds(0, strip), :], dst, sems.at[r])
+
+        def d1_copy(r):
+            dst = d1_ref.at[pl.ds(under * r, under), :]
+            return pltpu.make_async_copy(inv_ref.at[r, pl.ds(strip, under), :], dst, sems.at[rows_n + r])
+
+        left = pltpu.make_async_copy(left_ref, zl_ref, sems.at[2 * rows_n])
+        right = pltpu.make_async_copy(right_ref, zr_ref, sems.at[2 * rows_n + 1])
+        panel = pltpu.make_async_copy(off_ref.at[0, 0, :, pl.ds(0, width)], p_ref, sems.at[2 * rows_n + 2])
+        left.start()
+        right.start()
+        for r in range(rows_n):
+            d_copy(r).start()
+        panel.start()
+        for r in range(rows_n):
+            d1_copy(r).start()
+        left.wait()
+        right.wait()
+        first_core = core_ref[0] == 0
+        z_kept = jnp.where(first_core, zl_ref[...], zr_ref[...])
+        z_sent = jnp.where(first_core, zr_ref[...], zl_ref[...])
+        z = jnp.concatenate([z_kept, z_sent], axis=1)
+        total = jnp.zeros((strip, 2 * half), F32)
+        for i in range(parts):
+            for r in range(each * i, each * (i + 1)):
+                d_copy(r).wait()
+            y = dot(d_ref[tall * i : tall * (i + 1), :], z).astype(BF16)
+            y_ref[tall * i : tall * (i + 1), :] = y
+            if i == 0:
+                panel.wait()
+            total = total + dot(p_ref[:, tall * i : tall * (i + 1)], y)
+        v = placed_ref[...] - total * live_ref[0].astype(F32)
+        kept_ref[...] = v[:, :half]
+        sent_ref[...] = v[:, half:].astype(BF16)
+        for r in range(rows_n):
+            d1_copy(r).wait()
+
+    vmem = pl.BlockSpec(memory_space=pltpu.VMEM)
+    smem = pl.BlockSpec(memory_space=pltpu.SMEM)
+    hbm = pl.BlockSpec(memory_space=pl.ANY)
+    return pl.pallas_call(
+        body,
+        out_shape=(
+            jax.ShapeDtypeStruct((width, 2 * half), BF16),
+            jax.ShapeDtypeStruct((strip, half), F32),
+            jax.ShapeDtypeStruct((strip, half), BF16),
+            jax.ShapeDtypeStruct((rows_n * under, width), BF16),
+        ),
+        in_specs=[smem, smem, hbm, hbm, hbm, hbm, vmem],
+        out_specs=(vmem, vmem, vmem, hbm),
+        scratch_shapes=[
+            pltpu.VMEM((width, width), BF16),
+            pltpu.VMEM((width, half), BF16),
+            pltpu.VMEM((width, half), BF16),
+            pltpu.VMEM((strip, width), BF16),
+            pltpu.SemaphoreType.DMA((2 * rows_n + 3,)),
+        ],
+        compiler_params=pltpu.CompilerParams(vmem_limit_bytes=40 << 20),
+        name="level_zero",
+    )(core, live, inverse, z_left, z_right, off_diag, placed)
 
 
 def shards(rhs, inv_diag, off_diag, pair_mask):
@@ -123,19 +218,18 @@
     def by_core(one, two):
         return jnp.where(first_core, one, two)
 
-    d_own0 = d_all[: heights[0]]
-    d_full0 = lax.all_gather(d_own0, "row", axis=0, tiled=True)
+    d_low = lax.all_gather(d_all[: starts[2]], "row", axis=0, tiled=False)
     b0 = b_all[: heights[0]]
     z0_left = lax.all_gather(b0[:, :half], "row", axis=0, tiled=True)
     z0_right = lax.all_gather(b0[:, half:], "row", axis=0, tiled=True)
 
+    mid = width // 2
     upper_pairs = sorted(
         ((m, l) for l in range(2, levels) for m in range(l + 1, levels + 1)), key=lambda p: (p[1], p[0])
     )
-    d_first = {m: strip + starts[m] - starts[2] for m in range(2, levels + 1)}
-    packed = pack_upper(off_diag, inv_diag, live, upper_pairs, starts[2])
-    packed, z0_left = lax.optimization_barrier((packed, z0_left))
-    everyone = lax.all_gather(packed, "row", axis=0, tiled=False)
+    packed_low, packed_top = pack_upper(off_diag, inv_diag, live, upper_pairs, starts[2])
+    packed_low, z0_left = lax.optimization_barrier((packed_low, z0_left))
+    upper_low = lax.all_gather(packed_low, "row", axis=0, tiled=False)
 
     tall = strip * levels
     base = np.concatenate([strip * (m - 1) + np.arange(heights[m]) for m in range(1, levels + 1)])
@@ -147,33 +241,31 @@
     b_up = by_core(b_up, jnp.concatenate([b_up[:, half:], b_up[:, :half]], axis=1))
     placed = dot(spread, b_up)
 
-    z0_sent = by_core(z0_right, z0_left)
-    z0_kept = by_core(z0_left, z0_right)
     mask0, mask1 = lax.optimization_barrier((mask_rows(0), mask_rows(1)))
-    live1 = mask0[:strip]
-    yb_sent = dot(d_full0, z0_sent).astype(BF16)
-    sent = placed[:strip, half:] - dot(panel(1, 0), yb_sent) * live1
-    got = core_swap(sent.astype(BF16))
-    yb_kept = dot(d_full0, z0_kept).astype(BF16)
-    kept = placed[:strip, :half] - dot(panel(1, 0), yb_kept) * live1
-    yb0 = jnp.concatenate([yb_kept, yb_sent], axis=1)
+    yb0, kept, sent, d_leaf1 = level_zero(
+        core.reshape(1), live, d_low, z0_left, z0_right, off_diag, placed[:strip]
+    )
+    got = core_swap(sent)
+    packed_top, kept = lax.optimization_barrier((packed_top, kept))
+    upper_top = lax.all_gather(packed_top, "row", axis=0, tiled=False)
     parts = [
         placed[strip * (m - 1) : strip * m] - dot(panel(m, 0), yb0) * mask0[strip * (m - 1) : strip * m]
         for m in range(2, levels + 1)
     ]
 
-    d_own1 = d_all[starts[1] : starts[2]]
     z1 = (kept + got.astype(F32)).astype(BF16)
     z1 = lax.all_gather(z1, "row", axis=0, tiled=False)
     z1 = z1.reshape(rows_n, 2, heights[1], half).transpose(1, 0, 2, 3).reshape(width, half)
     z1_got = core_swap(z1)
+    yb_kept1 = dot(d_leaf1, z1).astype(BF16)
+    z1_got, yb_kept1, parts = lax.optimization_barrier((z1_got, yb_kept1, parts))
+    yb1 = jnp.concatenate([yb_kept1, dot(d_leaf1, z1_got).astype(BF16)], axis=1)
+    d_own0 = d_all[: heights[0]]
+    d_own1 = d_all[starts[1] : starts[2]]
     y_kept1 = dot(d_own1, z1)
     y_sent1 = dot(d_own1, z1_got)
-    yb1 = jnp.concatenate([y_kept1, y_sent1], axis=1).astype(BF16)
-    yb1, parts = lax.optimization_barrier((yb1, parts))
-    yb1 = lax.all_gather(yb1, "row", axis=0, tiled=True)
-    out0_kept = dot(d_own0, z0_kept)
-    out0_sent = dot(d_own0, z0_sent)
+    out0_kept = dot(d_own0, by_core(z0_left, z0_right))
+    out0_sent = dot(d_own0, by_core(z0_right, z0_left))
     part = jnp.concatenate(
         [
             parts[m - 2] - dot(panel(m, 1), yb1) * mask1[strip * (m - 2) : strip * (m - 1)]
@@ -190,25 +282,44 @@
     def turned_of(m):
         return turned[:, :, (m - 2) * strip : (m - 1) * strip]
 
-    def d_leaf(m):
-        rows = everyone[:, d_first[m] : d_first[m] + heights[m], :width]
-        return rows.reshape(rows_n * heights[m], width)
-
-    p_leaf = {}
+    def d_leaf(m, low, top):
+        high = heights[m]
+        if m < levels:
+            at = starts[m] - starts[2]
+            left = low[:, at : at + high, :mid]
+            right = low[:, strip // 2 + at : strip // 2 + at + high, :mid]
+        else:
+            left = top[:, strip : strip + high]
+            right = top[:, strip + high : strip + 2 * high]
+        return jnp.concatenate([left, right], axis=2).reshape(rows_n * high, width)
+
+    p_first = {}
+    at = mid
+    for m, l in upper_pairs:
+        if m < levels:
+            p_first[m, l] = at
+            at += width >> l
     at = 0
     for m, l in upper_pairs:
-        p_leaf[m, l] = everyone[:, :strip, at : at + (width >> l)]
-        at += width >> l
+        if m == levels:
+            p_first[m, l] = at
+            at += width >> l
+
+    def p_leaf(m, l, low, top):
+        block = low if m < levels else top
+        return block[:, :strip, p_first[m, l] : p_first[m, l] + (width >> l)]
 
     def natural(z, m):
         z = z.reshape(rows_n, 2 * sub, 2**m, heights[m])
         return z.transpose(1, 2, 0, 3).reshape(2 * sub, width)
 
     solved = []
-    sums = {}
+    terms = {m: [] for m in range(3, levels + 1)}
     for m in range(2, levels + 1):
         if m == 2:
-            pieces = leaf_everyone(turned_of(2), 4).astype(F32)
+            pieces = jnp.broadcast_to(turned_of(2), (4, rows_n, sub, strip))
+            pieces, upper_low = lax.optimization_barrier((pieces, upper_low))
+            pieces = leaf_scatter(pieces).astype(F32)
             pieces = pieces.reshape(2, 2, rows_n, sub, strip).sum(axis=0).astype(BF16)
             z = pieces.transpose(1, 0, 2, 3).reshape(rows_n, 2 * sub, strip)
         else:
@@ -216,16 +327,19 @@
             mine = jnp.where(
                 (jnp.arange(2) == core)[None, :, None, None], turned_of(m)[:, None], jnp.zeros((), BF16)
             ).reshape(rows_n, 2 * sub, strip)
-            v = (mine.astype(F32) - sums[m]).astype(BF16)
-            v = v.reshape(size, rows_n * 2 * sub // size, strip)
+            v = mine.astype(F32)
+            for l, yb in terms[m]:
+                v = v - dot_t(yb, p_leaf(m, l, upper_low, upper_top)).transpose(1, 0, 2)
+            v = v.astype(BF16).reshape(size, rows_n * 2 * sub // size, strip)
             z = leaf_scatter(v).astype(F32).sum(axis=0).astype(BF16)
+            if m == levels - 1:
+                z, upper_top = lax.optimization_barrier((z, upper_top))
             z = leaf_everyone(z, size).reshape(rows_n, 2 * sub, strip)
-        y = dot_t(natural(z, m), d_leaf(m))
+        y = dot_t(natural(z, m), d_leaf(m, upper_low, upper_top))
         yb = y.astype(BF16)
         solved.append(yb.reshape(2 * sub, rows_n, heights[m]))
         for higher in range(m + 1, levels + 1):
-            term = dot_t(yb, p_leaf[higher, m]).transpose(1, 0, 2)
-            sums[higher] = term if m == 2 else sums[higher] + term
+            terms[higher].append((m, yb))
 
     d_rows = sum(heights[2:])
     done = jnp.concatenate(solved, axis=2).transpose(1, 0, 2)

time: 349 us -> 361 us (1.034)
  blocking collectives: 195 us -> 111 us
  waiting for transfers between devices: 35 us -> 98.5 us
  starting transfers between devices: 49.1 us -> 71.9 us
  Pallas kernels: 2.99 us -> 8.51 us
    all_to_all x3 -> x0, blocking collectives: 44.6 us -> none  [the longest x2 25.1 us: leaf_scatter(): lax.all_to_all(pieces, 'leaf', 0, 0, tiled=True, axis_index_groups=leaf_g...]
    all_gather x1 -> x0, blocking collectives: 38.3 us -> none  [shards(): yb1 = lax.all_gather(yb1, 'row', axis=0, tiled=True)]
    all_gather x2 -> x3, waiting for transfers between devices: 5.48 us -> 43.7 us  [the longest x1 31.1 us: shards(): d_low = lax.all_gather(d_all[:starts[2]], 'row', axis=0, tiled=False)]
    all_to_all x5 -> x7, starting transfers between devices: 23 us -> 44.5 us  [leaf_scatter(): lax.all_to_all(pieces, 'leaf', 0, 0, tiled=True, axis_index_groups=leaf_g...]
    all_to_all x5 -> x7, waiting for transfers between devices: 17.2 us -> 30.8 us  [leaf_scatter(): lax.all_to_all(pieces, 'leaf', 0, 0, tiled=True, axis_index_groups=leaf_g...]
    all_to_all x0 -> x1, waiting for transfers between devices: none -> 11.4 us  [shards(): turned = lax.all_to_all(turned, 'row', 0, 0, tiled=True)]
    ppermute x3, starting transfers between devices: 20.3 us -> 11 us  [core_swap(): return lax.ppermute(block, 'leaf', [(i, i ^ 1) for i in range(count)])]
    all_to_all x0 -> x1, starting transfers between devices: none -> 8.71 us  [shards(): turned = lax.all_to_all(turned, 'row', 0, 0, tiled=True)]
  transfers between devices with their start and end apart: 11 -> 15, of which waited for: 8 -> 12; matrix products, arithmetic and copies ran while one was open for 9% -> 12% of each run, Pallas kernels for 1% -> 2%
where the time goes in v5:
time: 361 us; the launch traced here: 359 us
  blocking collectives  111 us (31%)
  waiting for transfers between devices  98.5 us (27%)
  starting transfers between devices  71.9 us (20%)
  matrix products  29 us (8%)
  local copies, waits for them, and re-layouts  23.9 us (7%)
  between operations  14 us (4%)
  Pallas kernels  8.51 us (2%)
    all_to_all x7, starting transfers between devices, leaf_scatter(): lax.all_to_all(pieces, 'leaf', 0, 0, tiled=True, axis_index_groups=leaf_g...  44.5 us
    all_gather x1, blocking collectives, shards(): z0_left = lax.all_gather(b0[:, :half], 'row', axis=0, tiled=True)  39.2 us
    all_gather x1, blocking collectives, shards(): z0_right = lax.all_gather(b0[:, half:], 'row', axis=0, tiled=True)  36.8 us
    all_gather x1, blocking collectives, shards(): z1 = lax.all_gather(z1, 'row', axis=0, tiled=False)  35.5 us
    all_gather x1, waiting for transfers between devices, shards(): d_low = lax.all_gather(d_all[:starts[2]], 'row', axis=0, tiled=False)  31.1 us
    all_to_all x7, waiting for transfers between devices, leaf_scatter(): lax.all_to_all(pieces, 'leaf', 0, 0, tiled=True, axis_index_groups=leaf_g...  30.8 us
    dot_general x15, matrix products, dot(): return jnp.dot(a, b, preferred_element_type=F32)  15.1 us
    dot_general x10, matrix products, dot_t(): lax.dot_general(a, b, (((1,), (b.ndim - 1,)), ((), ())), preferred_elemen...  13.8 us
  transfers between devices with their start and end apart: 15, of which 12 were waited for; matrix products, arithmetic and copies ran while one was open for 12% of the time, Pallas kernels for 2%

profile of v5, /device:TPU:1, one launch (start us, length us, event | category | flops | bytes accessed | tf_op | source)
XLA Modules:
  0.0 359.3 jit_solution(10347749593387998437)
XLA Ops:
  6.5 1.8 slice.170
  8.5 2.9 pack_upper.1
  11.4 39.2 %all_gather.30.left_ref = bf16[1536,256]{1,0:T(8,128)(2,1)S(1)} all-gather(bf16[96,256]{1,0:T(8,128)(2,1)S(1)} %get-tuple-element.64), channel_id=1, replica_groups=mesh['leaf'=32,'row'=16] {'row'}, dimensions={0}, use_global_device_ids=true | all-gather | bytes 835584 | tf_op jit(solution)/shard_map/all_gather | solution.py:223
  52.6 36.8 %all_gather.31.right_ref = bf16[1536,256]{1,0:T(8,128)(2,1)S(1)} all-gather(bf16[96,256]{1,0:T(8,128)(2,1)S(1)} %get-tuple-element.63), channel_id=1, replica_groups=mesh['leaf'=32,'row'=16] {'row'}, dimensions={0}, use_global_device_ids=true | all-gather | bytes 835584 | tf_op jit(solution)/shard_map/all_gather | solution.py:224
  89.4 31.1 %all-gather.8.cloned.1.call-done = bf16[16,1,144,1536]{3,2,1,0:T(8,128)(2,1)} async-done(((bf16[1,1,144,1536]{3,2,1,0:T(8,128)(2,1)}), bf16[16,1,144,1536]{3,2,1,0:T(8,128)(2,1)}) %all-gather.8.cloned.1.call-update) | async-done | bytes 7077904 | tf_op jit(solution)/shard_map/all_gather | solution.py:221
  120.5 1.7 copy-done
  122.1 5.6 %level_zero.1 = (bf16[1536,512]{1,0:T(8,128)(2,1)S(1)}, f32[96,256]{1,0:T(8,128)S(1)}, bf16[96,256]{1,0:T(8,128)(2,1)S(1)}, bf16[768,1536]{1,0:T(8,128)(2,1)S(1)}) custom-call(s32[1]{0:T(128)} %bitcast.4.core_ref, s32[15]{0:T(128)S(1)} %bitcast.193, bf16[16,144,1536]{2,1,0:T(8,128)(2,1)} %bitcast.194, bf16[1536,256]{1,0:T(8,128)(2,1)S(1)} %all_gather.30.left_ref, ...), custom_call_target="tpu_custom_call" | custom-call | tf_op jit(solution)/shard_map/level_zero/pallas_call | solution.py:167
  127.8 2.8 collective-permute-start
  130.6 1.3 fusion.34
  131.9 2.0 fusion.36
  133.9 35.5 %all-gather.1 = bf16[1536,256]{1,0:T(8,128)(2,1)S(1)} all-gather(bf16[96,256]{1,0:T(8,128)(2,1)S(1)} %add_convert_fusion), channel_id=3, replica_groups=mesh['leaf'=32,'row'=16] {'row'}, dimensions={0}, use_global_device_ids=true | all-gather | bytes 835584 | tf_op jit(solution)/shard_map/all_gather | solution.py:257
  169.5 6.2 %collective-permute-start.1 = (bf16[1536,256]{1,0:T(8,128)(2,1)S(1)}, bf16[1536,256]{1,0:T(8,128)(2,1)S(1)}, u32[]{:S(2)}, u32[]{:S(2)}) collective-permute-start(bf16[1536,256]{1,0:T(8,128)(2,1)S(1)} %bitcast.203), channel_id=1, source_target_pairs={{0,16},{16,0},{32,48},{48,32},{64,80},{80,64},{96,112},{112,96},{1... | collective-permute-start | bytes 2359304 | tf_op jit(solution)/shard_map/ppermute | solution.py:33
  175.7 1.4 fusion.38
  177.1 1.5 fusion.40
  178.6 0.8 convolution_convert_fusion.1
  179.5 0.8 convolution_convert_fusion
  180.3 1.2 fusion.29
  181.6 1.2 fusion.30
  182.9 1.2 fusion.31
  184.2 1.2 fusion.32
  185.5 2.1 collective-permute-start.2
  187.7 1.2 collective-permute-done.2
  189.0 0.8 copy.57
  189.8 8.7 %all-to-all-start = ((bf16[16,16,384]{2,1,0:T(8,128)(2,1)}), bf16[16,16,384]{2,1,0:T(8,128)(2,1)S(1)}, u32[]{:S(2)}, u32[]{:S(2)}) async-start(bf16[16,16,384]{2,1,0:T(8,128)(2,1)} %bitcast.34), calls=%async_computation | async-start | bytes 393216 | tf_op jit(solution)/shard_map/all_to_all | solution.py:280
  198.5 0.9 convolution_bitcast_fusion.3
  199.5 0.9 convolution_bitcast_fusion.4
  200.6 11.4 %all-to-all-done = bf16[16,16,384]{2,1,0:T(8,128)(2,1)S(1)} async-done(((bf16[16,16,384]{2,1,0:T(8,128)(2,1)}), bf16[16,16,384]{2,1,0:T(8,128)(2,1)S(1)}, u32[]{:S(2)}, u32[]{:S(2)}) %all-to-all-start) | async-done | bytes 196640 | tf_op jit(solution)/shard_map/all_to_all | solution.py:280
  212.2 0.7 broadcast_in_dim.102
  212.9 6.6 %all-to-all-start.1 = ((bf16[4,16,16,96]{3,2,1,0:T(8,128)(2,1)}), bf16[4,16,16,96]{3,2,1,0:T(8,128)(2,1)S(1)}, u32[]{:S(2)}, u32[]{:S(2)}) async-start(bf16[4,16,16,96]{3,2,1,0:T(8,128)(2,1)} %broadcast_in_dim.102), calls=%async_computation.1 | async-start | bytes 524288 | tf_op jit(solution)/shard_map/all_to_all | solution.py:43
  219.6 0.8 bitcast_select_fusion
  220.4 1.2 fusion.82
  221.6 1.3 fusion.83
  223.1 1.5 all-to-all-done.1
  225.0 1.4 copy.59
  226.4 1.7 reshape.119
  228.6 2.6 fusion.41
  231.2 5.2 %all-to-all-start.2 = ((bf16[8,64,96]{2,1,0:T(8,128)(2,1)}), bf16[8,64,96]{2,1,0:T(8,128)(2,1)S(1)}, u32[]{:S(2)}, u32[]{:S(2)}) async-start(bf16[8,64,96]{2,1,0:T(8,128)(2,1)} %bitcast.43), calls=%async_computation.2 | async-start | bytes 262144 | tf_op jit(solution)/shard_map/all_to_all | solution.py:43
  236.4 1.2 fusion.81
  237.7 3.9 %all-to-all-done.2 = bf16[8,64,96]{2,1,0:T(8,128)(2,1)S(1)} async-done(((bf16[8,64,96]{2,1,0:T(8,128)(2,1)}), bf16[8,64,96]{2,1,0:T(8,128)(2,1)S(1)}, u32[]{:S(2)}, u32[]{:S(2)}) %all-to-all-start.2) | async-done | bytes 98336 | tf_op jit(solution)/shard_map/all_to_all | solution.py:43
  241.6 0.7 broadcast_in_dim.109
  242.3 4.1 %all-to-all-start.3 = ((bf16[8,64,96]{2,1,0:T(8,128)(2,1)}), bf16[8,64,96]{2,1,0:T(8,128)(2,1)S(1)}, u32[]{:S(2)}, u32[]{:S(2)}) async-start(bf16[8,64,96]{2,1,0:T(8,128)(2,1)} %broadcast_in_dim.109), calls=%async_computation.3 | async-start | bytes 262144 | tf_op jit(solution)/shard_map/all_to_all | solution.py:43
  246.5 1.9 fusion.21
  248.4 3.3 all-to-all-done.3
  252.7 2.2 fusion.27
  254.9 4.2 %all-to-all-start.4 = ((bf16[16,32,96]{2,1,0:T(8,128)(2,1)}), bf16[16,32,96]{2,1,0:T(8,128)(2,1)S(1)}, u32[]{:S(2)}, u32[]{:S(2)}) async-start(bf16[16,32,96]{2,1,0:T(8,128)(2,1)} %fusion.27), calls=%async_computation.4 | async-start | bytes 262144 | tf_op jit(solution)/shard_map/all_to_all | solution.py:43
  259.7 5.6 %all-to-all-done.4 = bf16[16,32,96]{2,1,0:T(8,128)(2,1)S(1)} async-done(((bf16[16,32,96]{2,1,0:T(8,128)(2,1)}), bf16[16,32,96]{2,1,0:T(8,128)(2,1)S(1)}, u32[]{:S(2)}, u32[]{:S(2)}) %all-to-all-start.4) | async-done | bytes 98336 | tf_op jit(solution)/shard_map/all_to_all | solution.py:43
  265.3 12.6 %all-gather.12.cloned.1.call-done = bf16[1664,768]{1,0:T(8,128)(2,1)} async-done(((bf16[104,768]{1,0:T(8,128)(2,1)}), bf16[1664,768]{1,0:T(8,128)(2,1)}) %all-gather.12.cloned.1.call-update) | async-done | bytes 2555920 | tf_op jit(solution)/shard_map/all_gather | solution.py:250
  277.9 0.7 broadcast_in_dim.112
  278.6 15.1 %all-to-all-start.5 = ((bf16[16,32,96]{2,1,0:T(8,128)(2,1)}), bf16[16,32,96]{2,1,0:T(8,128)(2,1)S(1)}, u32[]{:S(2)}, u32[]{:S(2)}) async-start(bf16[16,32,96]{2,1,0:T(8,128)(2,1)} %broadcast_in_dim.112), calls=%async_computation.5 | async-start | bytes 262144 | tf_op jit(solution)/shard_map/all_to_all | solution.py:43
  293.7 1.9 fusion.18
  295.7 1.5 fusion.7
  297.2 2.6 all-to-all-done.5
  300.8 2.3 fusion.28
  303.1 5.3 %all-to-all-start.6 = ((bf16[32,16,96]{2,1,0:T(8,128)(2,1)}), bf16[32,16,96]{2,1,0:T(8,128)(2,1)S(1)}, u32[]{:S(2)}, u32[]{:S(2)}) async-start(bf16[32,16,96]{2,1,0:T(8,128)(2,1)} %bitcast.57), calls=%async_computation.6 | async-start | bytes 262144 | tf_op jit(solution)/shard_map/all_to_all | solution.py:43
  308.4 1.1 fusion.84
  309.5 6.6 %all-to-all-done.6 = bf16[32,16,96]{2,1,0:T(8,128)(2,1)S(1)} async-done(((bf16[32,16,96]{2,1,0:T(8,128)(2,1)}), bf16[32,16,96]{2,1,0:T(8,128)(2,1)S(1)}, u32[]{:S(2)}, u32[]{:S(2)}) %all-to-all-start.6) | async-done | bytes 98336 | tf_op jit(solution)/shard_map/all_to_all | solution.py:43
  316.1 0.7 broadcast_in_dim.115
  316.8 3.9 %all-to-all-start.7 = ((bf16[32,16,96]{2,1,0:T(8,128)(2,1)}), bf16[32,16,96]{2,1,0:T(8,128)(2,1)S(1)}, u32[]{:S(2)}, u32[]{:S(2)}) async-start(bf16[32,16,96]{2,1,0:T(8,128)(2,1)} %broadcast_in_dim.115), calls=%async_computation.7 | async-start | bytes 262144 | tf_op jit(solution)/shard_map/all_to_all | solution.py:43
  321.1 7.4 %all-to-all-done.7 = bf16[32,16,96]{2,1,0:T(8,128)(2,1)S(1)} async-done(((bf16[32,16,96]{2,1,0:T(8,128)(2,1)}), bf16[32,16,96]{2,1,0:T(8,128)(2,1)S(1)}, u32[]{:S(2)}, u32[]{:S(2)}) %all-to-all-start.7) | async-done | bytes 98336 | tf_op jit(solution)/shard_map/all_to_all | solution.py:43
  328.5 1.1 copy.66
  331.3 0.8 reshape.147
  332.1 7.5 %all-to-all-start.8 = ((bf16[16,2,720]{2,1,0:T(2,128)(2,1)}), bf16[16,2,720]{2,1,0:T(2,128)(2,1)S(1)}, u32[]{:S(2)}, u32[]{:S(2)}) async-start(bf16[16,2,720]{2,1,0:T(2,128)(2,1)} %reshape.147), calls=%async_computation.8 | async-start | bytes 98304 | tf_op jit(solution)/shard_map/all_to_all | solution.py:346
  339.9 11.2 %all-to-all-done.8 = bf16[16,2,720]{2,1,0:T(2,128)(2,1)S(1)} async-done(((bf16[16,2,720]{2,1,0:T(2,128)(2,1)}), bf16[16,2,720]{2,1,0:T(2,128)(2,1)S(1)}, u32[]{:S(2)}, u32[]{:S(2)}) %all-to-all-start.8) | async-done | bytes 46112 | tf_op jit(solution)/shard_map/all_to_all | solution.py:346
  351.6 1.1 copy.75
  (130 shorter events, 9.3 us)
Async XLA Ops:
  6.5 4.8 %copy-start.14 = (bf16[1,1,189,512]{3,2,1,0:T(8,128)(2,1)S(1)}, bf16[1,1,189,512]{3,2,1,0:T(8,128)(2,1)}, u32[]{:S(2)}) copy-start(bf16[1,1,189,512]{3,2,1,0:T(8,128)(2,1)} %param.9) | copy-start | bytes 580612
  6.5 113.9 %all-gather.8.cloned.1.call-start = ((), (), s32[]{:S(2)}) async-start(), calls=%async_computation.9 | async-start | bytes 7520256 | tf_op jit(solution)/shard_map/all_gather | solution.py:221
  8.4 42.3 %copy-start.20 = (s32[93]{0:T(128)S(1)}, s32[93]{0:T(128)}, u32[]{:S(2)}) copy-start(s32[93]{0:T(128)} %constant.27.clone) | copy-start | bytes 1120
  8.4 42.3 %copy-start.21 = (s32[93]{0:T(128)S(1)}, s32[93]{0:T(128)}, u32[]{:S(2)}) copy-start(s32[93]{0:T(128)} %constant.29.clone) | copy-start | bytes 1120
  8.4 42.3 %copy-start.22 = (s32[93]{0:T(128)S(1)}, s32[93]{0:T(128)}, u32[]{:S(2)}) copy-start(s32[93]{0:T(128)} %constant.28.clone) | copy-start | bytes 1120
  8.4 203.8 %all-gather.10.cloned.1.call-start = ((), (), s32[]{:S(2)}) async-start(), calls=%async_computation.10 | async-start | bytes 5849088 | tf_op jit(solution)/shard_map/all_gather | solution.py:232
  11.4 39.7 %copy-start.1 = (s32[1,1,15]{2,1,0:T(1,128)S(1)}, s32[1,1,15]{2,1,0:T(1,128)}, u32[]{:S(2)}) copy-start(s32[1,1,15]{2,1,0:T(1,128)} %param.12) | copy-start | bytes 184
  11.4 39.7 %copy-start.19 = (s32[480]{0:T(512)S(1)}, s32[480]{0:T(512)}, u32[]{:S(2)}) copy-start(s32[480]{0:T(512)} %constant.30.clone) | copy-start | bytes 5764
  11.4 39.8 %copy-start.18 = (s32[384]{0:T(512)S(1)}, s32[384]{0:T(512)}, u32[]{:S(2)}) copy-start(s32[384]{0:T(512)} %constant.31.clone) | copy-start | bytes 4612
  50.6 227.3 %all-gather.12.cloned.1.call-start = ((), (), s32[]{:S(2)}) async-start(), calls=%async_computation.11 | async-start | bytes 2715648 | tf_op jit(solution)/shard_map/all_gather | solution.py:250
  51.1 69.4 %copy-start.4 = (f32[480,512]{1,0:T(8,128)}, f32[480,512]{1,0:T(8,128)S(1)}, u32[]{:S(2)}) copy-start(f32[480,512]{1,0:T(8,128)S(1)} %fusion.60) | copy-start | bytes 2949124
  120.5 1.7 copy-start
  122.1 8.4 %copy-start.17 = (f32[96]{0:T(128)S(1)}, f32[96]{0:T(128)}, u32[]{:S(2)}) copy-start(f32[96]{0:T(128)} %get-tuple-element.68) | copy-start | bytes 1156
  127.8 6.1 %copy-start.2 = (bf16[768,1536]{1,0:T(8,128)(2,1)}, bf16[768,1536]{1,0:T(8,128)(2,1)S(1)}, u32[]{:S(2)}) copy-start(bf16[768,1536]{1,0:T(8,128)(2,1)S(1)} %get-tuple-element.33) | copy-start | bytes 7077892
  127.8 6.1 %collective-permute-start = (bf16[96,256]{1,0:T(8,128)(2,1)S(1)}, bf16[96,256]{1,0:T(8,128)(2,1)S(1)}, u32[]{:S(2)}, u32[]{:S(2)}) collective-permute-start(bf16[96,256]{1,0:T(8,128)(2,1)S(1)} %get-tuple-element.32), channel_id=1, source_target_pairs={{0,16},{16,0},{32,48},{48,32},{64,80},{80,64},{96,112},{112,96},{1... | collective-permute-start | bytes 147464 | tf_op jit(solution)/shard_map/ppermute | solution.py:33
  169.4 10.0 %copy-start.5 = (bf16[16,2,48,256]{3,2,0,1:T(8,128)(2,1)}, bf16[16,2,48,256]{3,2,0,1:T(8,128)(2,1)S(1)}, u32[]{:S(2)}) copy-start(bf16[16,2,48,256]{3,2,0,1:T(8,128)(2,1)S(1)} %copy.55) | copy-start | bytes 2359300
  169.5 9.2 %copy-start.3 = (bf16[768,1536]{1,0:T(8,128)(2,1)S(1)}, bf16[768,1536]{1,0:T(8,128)(2,1)}, u32[]{:S(2)}) copy-start(bf16[768,1536]{1,0:T(8,128)(2,1)} %copy-done.2) | copy-start | bytes 7077892
  169.5 10.0 %collective-permute-start.1 = (bf16[1536,256]{1,0:T(8,128)(2,1)S(1)}, bf16[1536,256]{1,0:T(8,128)(2,1)S(1)}, u32[]{:S(2)}, u32[]{:S(2)}) collective-permute-start(bf16[1536,256]{1,0:T(8,128)(2,1)S(1)} %bitcast.203), channel_id=1, source_target_pairs={{0,16},{16,0},{32,48},{48,32},{64,80},{80,64},{96,112},{112,96},{1... | collective-permute-start | bytes 2359304 | tf_op jit(solution)/shard_map/ppermute | solution.py:33
  179.4 0.9 copy-start.26
  179.4 2.2 copy-start.25
  179.4 0.9 copy-start.9
  180.3 2.6 copy-start.24
  181.6 2.5 copy-start.8
  181.6 2.6 copy-start.23
  185.3 13.2 %copy-start.7 = (bf16[1,1,189,1536]{3,2,1,0:T(8,128)(2,1)S(1)}, bf16[1,1,189,1536]{3,2,1,0:T(8,128)(2,1)}, u32[]{:S(2)}) copy-start(bf16[1,1,189,1536]{3,2,1,0:T(8,128)(2,1)} %inv_ref.1) | copy-start | bytes 1741828
  185.5 3.5 collective-permute-start.2
  189.8 10.5 %copy-start.6 = (bf16[16,2,48,256]{3,2,0,1:T(8,128)(2,1)S(1)}, bf16[16,2,48,256]{3,2,0,1:T(8,128)(2,1)}, u32[]{:S(2)}) copy-start(bf16[16,2,48,256]{3,2,0,1:T(8,128)(2,1)} %copy-done.5) | copy-start | bytes 2359300
  189.8 22.2 %all-to-all-start = ((bf16[16,16,384]{2,1,0:T(8,128)(2,1)}), bf16[16,16,384]{2,1,0:T(8,128)(2,1)S(1)}, u32[]{:S(2)}, u32[]{:S(2)}) async-start(bf16[16,16,384]{2,1,0:T(8,128)(2,1)} %bitcast.34), calls=%async_computation | async-start | bytes 393216 | tf_op jit(solution)/shard_map/all_to_all | solution.py:280
  212.9 11.7 %all-to-all-start.1 = ((bf16[4,16,16,96]{3,2,1,0:T(8,128)(2,1)}), bf16[4,16,16,96]{3,2,1,0:T(8,128)(2,1)S(1)}, u32[]{:S(2)}, u32[]{:S(2)}) async-start(bf16[4,16,16,96]{3,2,1,0:T(8,128)(2,1)} %broadcast_in_dim.102), calls=%async_computation.1 | async-start | bytes 524288 | tf_op jit(solution)/shard_map/all_to_all | solution.py:43
  223.1 5.4 %copy-start.13 = (bf16[16,32,96]{2,1,0:T(8,128)(2,1)S(1)}, bf16[16,32,96]{2,1,0:T(8,128)(2,1)}, u32[]{:S(2)}) copy-start(bf16[16,32,96]{2,1,0:T(8,128)(2,1)} %get-tuple-element.75) | copy-start | bytes 294916
  228.5 17.9 %copy-start.12 = (bf16[16,32,96]{2,1,0:T(8,128)(2,1)S(1)}, bf16[16,32,96]{2,1,0:T(8,128)(2,1)}, u32[]{:S(2)}) copy-start(bf16[16,32,96]{2,1,0:T(8,128)(2,1)} %get-tuple-element.74) | copy-start | bytes 294916
  231.2 10.4 %all-to-all-start.2 = ((bf16[8,64,96]{2,1,0:T(8,128)(2,1)}), bf16[8,64,96]{2,1,0:T(8,128)(2,1)S(1)}, u32[]{:S(2)}, u32[]{:S(2)}) async-start(bf16[8,64,96]{2,1,0:T(8,128)(2,1)} %bitcast.43), calls=%async_computation.2 | async-start | bytes 262144 | tf_op jit(solution)/shard_map/all_to_all | solution.py:43
  242.3 9.4 %all-to-all-start.3 = ((bf16[8,64,96]{2,1,0:T(8,128)(2,1)}), bf16[8,64,96]{2,1,0:T(8,128)(2,1)S(1)}, u32[]{:S(2)}, u32[]{:S(2)}) async-start(bf16[8,64,96]{2,1,0:T(8,128)(2,1)} %broadcast_in_dim.109), calls=%async_computation.3 | async-start | bytes 262144 | tf_op jit(solution)/shard_map/all_to_all | solution.py:43
  252.4 41.3 %copy-start.11 = (bf16[16,32,96]{2,1,0:T(8,128)(2,1)S(1)}, bf16[16,32,96]{2,1,0:T(8,128)(2,1)}, u32[]{:S(2)}) copy-start(bf16[16,32,96]{2,1,0:T(8,128)(2,1)} %get-tuple-element.73) | copy-start | bytes 294916
  254.9 10.4 %all-to-all-start.4 = ((bf16[16,32,96]{2,1,0:T(8,128)(2,1)}), bf16[16,32,96]{2,1,0:T(8,128)(2,1)S(1)}, u32[]{:S(2)}, u32[]{:S(2)}) async-start(bf16[16,32,96]{2,1,0:T(8,128)(2,1)} %fusion.27), calls=%async_computation.4 | async-start | bytes 262144 | tf_op jit(solution)/shard_map/all_to_all | solution.py:43
  278.6 21.2 %all-to-all-start.5 = ((bf16[16,32,96]{2,1,0:T(8,128)(2,1)}), bf16[16,32,96]{2,1,0:T(8,128)(2,1)S(1)}, u32[]{:S(2)}, u32[]{:S(2)}) async-start(bf16[16,32,96]{2,1,0:T(8,128)(2,1)} %broadcast_in_dim.112), calls=%async_computation.5 | async-start | bytes 262144 | tf_op jit(solution)/shard_map/all_to_all | solution.py:43
  303.1 13.0 %all-to-all-start.6 = ((bf16[32,16,96]{2,1,0:T(8,128)(2,1)}), bf16[32,16,96]{2,1,0:T(8,128)(2,1)S(1)}, u32[]{:S(2)}, u32[]{:S(2)}) async-start(bf16[32,16,96]{2,1,0:T(8,128)(2,1)} %bitcast.57), calls=%async_computation.6 | async-start | bytes 262144 | tf_op jit(solution)/shard_map/all_to_all | solution.py:43
  316.8 11.7 %all-to-all-start.7 = ((bf16[32,16,96]{2,1,0:T(8,128)(2,1)}), bf16[32,16,96]{2,1,0:T(8,128)(2,1)S(1)}, u32[]{:S(2)}, u32[]{:S(2)}) async-start(bf16[32,16,96]{2,1,0:T(8,128)(2,1)} %broadcast_in_dim.115), calls=%async_computation.7 | async-start | bytes 262144 | tf_op jit(solution)/shard_map/all_to_all | solution.py:43
  329.6 10.0 %copy-start.10 = (bf16[1536,256]{1,0:T(8,128)(2,1)S(1)}, bf16[1536,256]{1,0:T(8,128)(2,1)}, u32[]{:S(2)}) copy-start(bf16[1536,256]{1,0:T(8,128)(2,1)} %copy-done.9) | copy-start | bytes 2359300
  330.0 9.9 %copy-start.15 = (f32[96,256]{1,0:T(8,128)S(1)}, f32[96,256]{1,0:T(8,128)}, u32[]{:S(2)}) copy-start(f32[96,256]{1,0:T(8,128)} %convolution_bitcast_fusion.3) | copy-start | bytes 294916
  330.0 9.9 %copy-start.16 = (f32[96,256]{1,0:T(8,128)S(1)}, f32[96,256]{1,0:T(8,128)}, u32[]{:S(2)}) copy-start(f32[96,256]{1,0:T(8,128)} %convolution_bitcast_fusion.4) | copy-start | bytes 294916
  332.1 19.1 %all-to-all-start.8 = ((bf16[16,2,720]{2,1,0:T(2,128)(2,1)}), bf16[16,2,720]{2,1,0:T(2,128)(2,1)S(1)}, u32[]{:S(2)}, u32[]{:S(2)}) async-start(bf16[16,2,720]{2,1,0:T(2,128)(2,1)} %reshape.147), calls=%async_computation.8 | async-start | bytes 98304 | tf_op jit(solution)/shard_map/all_to_all | solution.py:346
Sparse Core Ops, SparseCore 0:
  9.4 110.9 all-gather.7
  122.5 80.9 all-gather.9
  205.7 72.2 all-gather.11

commit v6 on v5

--- a/solution.py
+++ b/solution.py
@@ -49,63 +49,45 @@
 
 def pack_upper(off_diag, inv_diag, live, pairs, d_start):
     strip, width = off_diag.shape[2], inv_diag.shape[3]
-    mid = width // 2
-    top = max(m for m, _ in pairs)
     d_rows = inv_diag.shape[2] - d_start
-    d_top = strip >> top
-    d_low = d_rows - d_top
     first = min(column_start(m, l, width) for m, l in pairs) // 128 * 128
     span = off_diag.shape[3] - first
-    low_pairs = [p for p in pairs if p[0] < top]
-    top_pairs = [p for p in pairs if p[0] == top]
-    low_cols = mid + sum(width >> l for _, l in low_pairs)
-    room = -2 * d_top % 8
-
-    def body(live_ref, off_ref, inv_ref, low_ref, top_ref, p_ref, d_ref, sems):
+    total = sum(width >> l for _, l in pairs)
+
+    def body(live_ref, off_ref, inv_ref, out_ref, p_ref, d_ref, sems):
         p_copy = pltpu.make_async_copy(off_ref.at[0, 0, :, pl.ds(first, span)], p_ref, sems.at[0])
         d_copy = pltpu.make_async_copy(inv_ref.at[0, 0, pl.ds(d_start, d_rows), :], d_ref, sems.at[1])
         p_copy.start()
         d_copy.start()
         d_copy.wait()
-        rows = d_ref[...].astype(F32)
-        pad = jnp.zeros((strip // 2 - d_low, mid), F32)
-        low = [rows[:d_low, :mid], pad, rows[:d_low, mid:], pad]
-        low_ref[:, :mid] = jnp.concatenate(low, axis=0).astype(BF16)
-        under = [rows[d_low:, :mid], rows[d_low:, mid:], jnp.zeros((room, mid), F32)]
-        top_ref[strip:, :] = jnp.concatenate(under, axis=0).astype(BF16)
+        out_ref[strip:, :] = jnp.zeros((out_ref.shape[0] - strip, total), BF16)
+        out_ref[strip : strip + d_rows, :width] = d_ref[...]
         p_copy.wait()
-
-        def put(ref, at, some):
-            for m, l in some:
-                start = column_start(m, l, width) - first
-                wide = width >> l
-                alive = live_ref[m * (m - 1) // 2 + l].astype(F32)
-                block = p_ref[:, start : start + wide].astype(F32) * alive
-                ref[:strip, at : at + wide] = block.astype(BF16)
-                at += wide
-            return at
-
-        put(low_ref, mid, low_pairs)
-        end = put(top_ref, 0, top_pairs)
-        top_ref[:strip, end:] = jnp.zeros((strip, mid - end), BF16)
-
+        at = 0
+        for m, l in pairs:
+            low = column_start(m, l, width) - first
+            wide = width >> l
+            alive = live_ref[m * (m - 1) // 2 + l].astype(F32)
+            block = p_ref[:, low : low + wide].astype(F32) * alive
+            out_ref[:strip, at : at + wide] = block.astype(BF16)
+            at += wide
+
+    tall = (strip + d_rows + 15) // 16 * 16
     return pl.pallas_call(
         body,
-        out_shape=(
-            jax.ShapeDtypeStruct((strip, low_cols), BF16),
-            jax.ShapeDtypeStruct((strip + 2 * d_top + room, mid), BF16),
-        ),
+        out_shape=jax.ShapeDtypeStruct((tall, total), BF16),
         in_specs=[
             pl.BlockSpec(memory_space=pltpu.SMEM),
             pl.BlockSpec(memory_space=pl.ANY),
             pl.BlockSpec(memory_space=pl.ANY),
         ],
-        out_specs=(pl.BlockSpec(memory_space=pltpu.VMEM), pl.BlockSpec(memory_space=pltpu.VMEM)),
+        out_specs=pl.BlockSpec(memory_space=pltpu.VMEM),
         scratch_shapes=[
             pltpu.VMEM((strip, span), BF16),
             pltpu.VMEM((d_rows, width), BF16),
             pltpu.SemaphoreType.DMA((2,)),
         ],
+        compiler_params=pltpu.CompilerParams(vmem_limit_bytes=8 << 20),
         name="pack_upper",
     )(live, off_diag, inv_diag)
 
@@ -163,7 +145,8 @@
 
     vmem = pl.BlockSpec(memory_space=pltpu.VMEM)
     smem = pl.BlockSpec(memory_space=pltpu.SMEM)
-    hbm = pl.BlockSpec(memory_space=pl.ANY)
+    hbm = pl.BlockSpec(memory_space=pltpu.HBM)
+    anywhere = pl.BlockSpec(memory_space=pl.ANY)
     return pl.pallas_call(
         body,
         out_shape=(
@@ -172,8 +155,8 @@
             jax.ShapeDtypeStruct((strip, half), BF16),
             jax.ShapeDtypeStruct((rows_n * under, width), BF16),
         ),
-        in_specs=[smem, smem, hbm, hbm, hbm, hbm, vmem],
-        out_specs=(vmem, vmem, vmem, hbm),
+        in_specs=[smem, smem, hbm, anywhere, anywhere, anywhere, vmem],
+        out_specs=(vmem, vmem, vmem, anywhere),
         scratch_shapes=[
             pltpu.VMEM((width, width), BF16),
             pltpu.VMEM((width, half), BF16),
@@ -181,7 +164,7 @@
             pltpu.VMEM((strip, width), BF16),
             pltpu.SemaphoreType.DMA((2 * rows_n + 3,)),
         ],
-        compiler_params=pltpu.CompilerParams(vmem_limit_bytes=40 << 20),
+        compiler_params=pltpu.CompilerParams(vmem_limit_bytes=20 << 20),
         name="level_zero",
     )(core, live, inverse, z_left, z_right, off_diag, placed)
 
@@ -223,13 +206,13 @@
     z0_left = lax.all_gather(b0[:, :half], "row", axis=0, tiled=True)
     z0_right = lax.all_gather(b0[:, half:], "row", axis=0, tiled=True)
 
-    mid = width // 2
     upper_pairs = sorted(
         ((m, l) for l in range(2, levels) for m in range(l + 1, levels + 1)), key=lambda p: (p[1], p[0])
     )
-    packed_low, packed_top = pack_upper(off_diag, inv_diag, live, upper_pairs, starts[2])
-    packed_low, z0_left = lax.optimization_barrier((packed_low, z0_left))
-    upper_low = lax.all_gather(packed_low, "row", axis=0, tiled=False)
+    d_first = {m: strip + starts[m] - starts[2] for m in range(2, levels + 1)}
+    packed = pack_upper(off_diag, inv_diag, live, upper_pairs, starts[2])
+    packed, z0_left = lax.optimization_barrier((packed, z0_left))
+    everyone = lax.all_gather(packed, "row", axis=0, tiled=False)
 
     tall = strip * levels
     base = np.concatenate([strip * (m - 1) + np.arange(heights[m]) for m in range(1, levels + 1)])
@@ -246,8 +229,6 @@
         core.reshape(1), live, d_low, z0_left, z0_right, off_diag, placed[:strip]
     )
     got = core_swap(sent)
-    packed_top, kept = lax.optimization_barrier((packed_top, kept))
-    upper_top = lax.all_gather(packed_top, "row", axis=0, tiled=False)
     parts = [
         placed[strip * (m - 1) : strip * m] - dot(panel(m, 0), yb0) * mask0[strip * (m - 1) : strip * m]
         for m in range(2, levels + 1)
@@ -260,6 +241,7 @@
     yb_kept1 = dot(d_leaf1, z1).astype(BF16)
     z1_got, yb_kept1, parts = lax.optimization_barrier((z1_got, yb_kept1, parts))
     yb1 = jnp.concatenate([yb_kept1, dot(d_leaf1, z1_got).astype(BF16)], axis=1)
+    yb1 = lax.optimization_barrier(yb1)
     d_own0 = d_all[: heights[0]]
     d_own1 = d_all[starts[1] : starts[2]]
     y_kept1 = dot(d_own1, z1)
@@ -282,32 +264,15 @@
     def turned_of(m):
         return turned[:, :, (m - 2) * strip : (m - 1) * strip]
 
-    def d_leaf(m, low, top):
-        high = heights[m]
-        if m < levels:
-            at = starts[m] - starts[2]
-            left = low[:, at : at + high, :mid]
-            right = low[:, strip // 2 + at : strip // 2 + at + high, :mid]
-        else:
-            left = top[:, strip : strip + high]
-            right = top[:, strip + high : strip + 2 * high]
-        return jnp.concatenate([left, right], axis=2).reshape(rows_n * high, width)
-
-    p_first = {}
-    at = mid
-    for m, l in upper_pairs:
-        if m < levels:
-            p_first[m, l] = at
-            at += width >> l
+    def d_leaf(m):
+        rows = everyone[:, d_first[m] : d_first[m] + heights[m], :width]
+        return rows.reshape(rows_n * heights[m], width)
+
+    p_leaf = {}
     at = 0
     for m, l in upper_pairs:
-        if m == levels:
-            p_first[m, l] = at
-            at += width >> l
-
-    def p_leaf(m, l, low, top):
-        block = low if m < levels else top
-        return block[:, :strip, p_first[m, l] : p_first[m, l] + (width >> l)]
+        p_leaf[m, l] = everyone[:, :strip, at : at + (width >> l)]
+        at += width >> l
 
     def natural(z, m):
         z = z.reshape(rows_n, 2 * sub, 2**m, heights[m])
@@ -317,9 +282,7 @@
     terms = {m: [] for m in range(3, levels + 1)}
     for m in range(2, levels + 1):
         if m == 2:
-            pieces = jnp.broadcast_to(turned_of(2), (4, rows_n, sub, strip))
-            pieces, upper_low = lax.optimization_barrier((pieces, upper_low))
-            pieces = leaf_scatter(pieces).astype(F32)
+            pieces = leaf_everyone(turned_of(2), 4).astype(F32)
             pieces = pieces.reshape(2, 2, rows_n, sub, strip).sum(axis=0).astype(BF16)
             z = pieces.transpose(1, 0, 2, 3).reshape(rows_n, 2 * sub, strip)
         else:
@@ -329,13 +292,11 @@
             ).reshape(rows_n, 2 * sub, strip)
             v = mine.astype(F32)
             for l, yb in terms[m]:
-                v = v - dot_t(yb, p_leaf(m, l, upper_low, upper_top)).transpose(1, 0, 2)
+                v = v - dot_t(yb, p_leaf[m, l]).transpose(1, 0, 2)
             v = v.astype(BF16).reshape(size, rows_n * 2 * sub // size, strip)
             z = leaf_scatter(v).astype(F32).sum(axis=0).astype(BF16)
-            if m == levels - 1:
-                z, upper_top = lax.optimization_barrier((z, upper_top))
             z = leaf_everyone(z, size).reshape(rows_n, 2 * sub, strip)
-        y = dot_t(natural(z, m), d_leaf(m, upper_low, upper_top))
+        y = dot_t(natural(z, m), d_leaf(m))
         yb = y.astype(BF16)
         solved.append(yb.reshape(2 * sub, rows_n, heights[m]))
         for higher in range(m + 1, levels + 1):

time: 361 us -> 363 us (level)
  blocking collectives: 111 us -> 139 us
  waiting for transfers between devices: 98.5 us -> 79.8 us
  starting transfers between devices: 71.9 us -> 54.2 us
  local copies, waits for them, and re-layouts: 23.9 us -> 38 us
  matrix products: 29 us -> 23.7 us
    all_to_all x0 -> x1, blocking collectives: none -> 24 us  [shards(): turned = lax.all_to_all(turned, 'row', 0, 0, tiled=True)]
    all_to_all x1 -> x0, waiting for transfers between devices: 11.4 us -> none  [shards(): turned = lax.all_to_all(turned, 'row', 0, 0, tiled=True)]
    all_to_all x7, starting transfers between devices: 44.5 us -> 34.2 us  [leaf_scatter(): lax.all_to_all(pieces, 'leaf', 0, 0, tiled=True, axis_index_groups=leaf_g...]
    dot_general x15, matrix products: 15.1 us -> 6.2 us  [dot(): return jnp.dot(a, b, preferred_element_type=F32)]
    all_to_all x1 -> x0, starting transfers between devices: 8.71 us -> none  [shards(): turned = lax.all_to_all(turned, 'row', 0, 0, tiled=True)]
    unnamed x56, local copies, waits for them, and re-layouts: 2.94 us -> 11.1 us
    all_to_all x7, waiting for transfers between devices: 30.8 us -> 24.3 us  [leaf_scatter(): lax.all_to_all(pieces, 'leaf', 0, 0, tiled=True, axis_index_groups=leaf_g...]
    dot_general x10, matrix products: 13.8 us -> 17.5 us  [dot_t(): lax.dot_general(a, b, (((1,), (b.ndim - 1,)), ((), ())), preferred_elemen...]
  transfers between devices with their start and end apart: 15 -> 13, of which waited for: 12 -> 11; matrix products, arithmetic and copies ran while one was open for 12% -> 7% of each run, Pallas kernels for 2% -> 3%
where the time goes in v6:
time: 363 us; the launch traced here: 361 us
  blocking collectives  139 us (38%)
  waiting for transfers between devices  79.8 us (22%)
  starting transfers between devices  54.2 us (15%)
  local copies, waits for them, and re-layouts  38 us (10%)
  matrix products  23.7 us (7%)
  between operations  14.1 us (4%)
  Pallas kernels  9.34 us (3%)
    all_gather x1, blocking collectives, shards(): z0_left = lax.all_gather(b0[:, :half], 'row', axis=0, tiled=True)  39.6 us
    all_gather x1, blocking collectives, shards(): z0_right = lax.all_gather(b0[:, half:], 'row', axis=0, tiled=True)  38.5 us
    all_gather x1, blocking collectives, shards(): z1 = lax.all_gather(z1, 'row', axis=0, tiled=False)  36.9 us
    all_to_all x7, starting transfers between devices, leaf_scatter(): lax.all_to_all(pieces, 'leaf', 0, 0, tiled=True, axis_index_groups=leaf_g...  34.2 us
    all_gather x1, waiting for transfers between devices, shards(): d_low = lax.all_gather(d_all[:starts[2]], 'row', axis=0, tiled=False)  27.5 us
    all_to_all x7, waiting for transfers between devices, leaf_scatter(): lax.all_to_all(pieces, 'leaf', 0, 0, tiled=True, axis_index_groups=leaf_g...  24.3 us
    all_to_all x1, blocking collectives, shards(): turned = lax.all_to_all(turned, 'row', 0, 0, tiled=True)  24 us
    dot_general x10, matrix products, dot_t(): lax.dot_general(a, b, (((1,), (b.ndim - 1,)), ((), ())), preferred_elemen...  17.5 us
  transfers between devices with their start and end apart: 13, of which 11 were waited for; matrix products, arithmetic and copies ran while one was open for 7% of the time, Pallas kernels for 3%

profile of v6, /device:TPU:1, one launch (start us, length us, event | category | flops | bytes accessed | tf_op | source)
XLA Modules:
  0.0 360.9 jit_solution(5802072927460164742)
XLA Ops:
  6.5 1.9 slice.158
  8.5 1.7 copy-done
  10.1 1.1 copy-done.5
  11.9 1.0 pack_upper.1
  12.9 0.8 copy-done.7
  13.7 39.6 %all_gather.24.left_ref = bf16[1536,256]{1,0:T(8,128)(2,1)S(1)} all-gather(bf16[96,256]{1,0:T(8,128)(2,1)S(1)} %get-tuple-element.40), channel_id=1, replica_groups=mesh['leaf'=32,'row'=16] {'row'}, dimensions={0}, use_global_device_ids=true | all-gather | bytes 835584 | tf_op jit(solution)/shard_map/all_gather | solution.py:206
  53.7 1.0 copy-done.10
  55.1 38.5 %all_gather.25.right_ref = bf16[1536,256]{1,0:T(8,128)(2,1)} all-gather(bf16[96,256]{1,0:T(8,128)(2,1)S(1)} %get-tuple-element.39), channel_id=1, replica_groups=mesh['leaf'=32,'row'=16] {'row'}, dimensions={0}, use_global_device_ids=true | all-gather | bytes 835584 | tf_op jit(solution)/shard_map/all_gather | solution.py:207
  93.6 27.5 %all-gather.6.cloned.1.call-done = bf16[16,1,144,1536]{3,2,1,0:T(8,128)(2,1)} async-done(((bf16[1,1,144,1536]{3,2,1,0:T(8,128)(2,1)}), bf16[16,1,144,1536]{3,2,1,0:T(8,128)(2,1)}) %all-gather.6.cloned.1.call-update) | async-done | bytes 7077904 | tf_op jit(solution)/shard_map/all_gather | solution.py:204
  121.2 3.0 copy-done.2
  124.2 1.1 copy-done.3
  125.3 8.4 %level_zero.1 = (bf16[1536,512]{1,0:T(8,128)(2,1)S(1)}, f32[96,256]{1,0:T(8,128)S(1)}, bf16[96,256]{1,0:T(8,128)(2,1)S(1)}, bf16[768,1536]{1,0:T(8,128)(2,1)S(1)}) custom-call(s32[1]{0:T(128)} %bitcast.4.core_ref, s32[15]{0:T(128)S(1)} %bitcast.197, bf16[16,144,1536]{2,1,0:T(8,128)(2,1)S(1)} %bitcast.193, bf16[1536,256]{1,0:T(8,128)(2,1)S(1)} %all_gather.24.left_ref, ...), custom_call_target="tpu_custom_call" | custom-call | tf_op jit(solution)/shard_map/level_zero/pallas_call | solution.py:150
  133.7 2.5 collective-permute-start
  137.1 36.9 %all-gather.1 = bf16[1536,256]{1,0:T(8,128)(2,1)S(1)} all-gather(bf16[96,256]{1,0:T(8,128)(2,1)S(1)} %add_convert_fusion), channel_id=3, replica_groups=mesh['leaf'=32,'row'=16] {'row'}, dimensions={0}, use_global_device_ids=true | all-gather | bytes 835584 | tf_op jit(solution)/shard_map/all_gather | solution.py:238
  174.1 7.1 %collective-permute-start.1 = (bf16[1536,256]{1,0:T(8,128)(2,1)S(1)}, bf16[1536,256]{1,0:T(8,128)(2,1)S(1)}, u32[]{:S(2)}, u32[]{:S(2)}) collective-permute-start(bf16[1536,256]{1,0:T(8,128)(2,1)S(1)} %bitcast.210), channel_id=1, source_target_pairs={{0,16},{16,0},{32,48},{48,32},{64,80},{80,64},{96,112},{112,96},{1... | collective-permute-start | bytes 2359304 | tf_op jit(solution)/shard_map/ppermute | solution.py:33
  182.0 0.8 convolution_convert_fusion.1
  183.1 0.8 convolution_convert_fusion
  185.4 2.3 collective-permute-start.2
  187.7 1.0 collective-permute-done.2
  189.0 24.0 %all_to_all.45 = bf16[16,16,384]{2,1,0:T(8,128)(2,1)S(1)} all-to-all(bf16[16,16,384]{2,1,0:T(8,128)(2,1)S(1)} %bitcast.219), channel_id=1, replica_groups=mesh['leaf'=32,'row'=16] {'row'}, dimensions={0} | all-to-all | bytes 393216 | tf_op jit(solution)/shard_map/all_to_all | solution.py:262
  213.2 0.7 broadcast_in_dim.102
  213.9 6.7 %all-to-all-start.1 = ((bf16[4,16,16,96]{3,2,1,0:T(8,128)(2,1)}), bf16[4,16,16,96]{3,2,1,0:T(8,128)(2,1)S(1)}, u32[]{:S(2)}, u32[]{:S(2)}) async-start(bf16[4,16,16,96]{3,2,1,0:T(8,128)(2,1)} %broadcast_in_dim.102), calls=%async_computation.1 | async-start | bytes 524288 | tf_op jit(solution)/shard_map/all_to_all | solution.py:43
  220.8 15.3 %all-gather.8.cloned.1.call-done = bf16[2304,1632]{1,0:T(8,128)(2,1)} async-done(((bf16[144,1632]{1,0:T(8,128)(2,1)}), bf16[2304,1632]{1,0:T(8,128)(2,1)}) %all-gather.8.cloned.1.call-update) | async-done | bytes 7520272 | tf_op jit(solution)/shard_map/all_gather | solution.py:215
  236.1 1.4 slice.222
  237.5 0.8 bitcast_select_fusion.1
  238.4 1.0 reshape_reshape.9
  239.4 2.6 copy.59
  242.0 2.3 reshape.119
  244.3 1.3 convolution_convert_fusion.2
  246.3 2.6 fusion.41
  248.9 4.9 %all-to-all-start.2 = ((bf16[8,64,96]{2,1,0:T(8,128)(2,1)}), bf16[8,64,96]{2,1,0:T(8,128)(2,1)}, u32[]{:S(2)}, u32[]{:S(2)}) async-start(bf16[8,64,96]{2,1,0:T(8,128)(2,1)} %bitcast.43), calls=%async_computation.2 | async-start | bytes 262144 | tf_op jit(solution)/shard_map/all_to_all | solution.py:43
  253.8 0.9 convolution_bitcast_fusion.3
  254.7 1.2 slice.225
  255.9 2.0 slice.229
  258.0 1.8 reshape.128
  259.9 0.9 reduce_sum.66
  261.5 4.8 %all-to-all-start.3 = ((bf16[8,64,96]{2,1,0:T(8,128)(2,1)}), bf16[8,64,96]{2,1,0:T(8,128)(2,1)S(1)}, u32[]{:S(2)}, u32[]{:S(2)}) async-start(bf16[8,64,96]{2,1,0:T(8,128)(2,1)} %broadcast_in_dim.109), calls=%async_computation.3 | async-start | bytes 262144 | tf_op jit(solution)/shard_map/all_to_all | solution.py:43
  266.3 2.0 fusion.21
  268.2 3.3 all-to-all-done.3
  271.7 0.9 reshape_reshape.10
  272.6 1.1 copy.61
  273.7 0.9 reshape.123
  274.7 1.3 convolution_convert_fusion.3
  276.0 2.2 fusion.27
  278.2 4.2 %all-to-all-start.4 = ((bf16[16,32,96]{2,1,0:T(8,128)(2,1)}), bf16[16,32,96]{2,1,0:T(8,128)(2,1)S(1)}, u32[]{:S(2)}, u32[]{:S(2)}) async-start(bf16[16,32,96]{2,1,0:T(8,128)(2,1)} %fusion.27), calls=%async_computation.4 | async-start | bytes 262144 | tf_op jit(solution)/shard_map/all_to_all | solution.py:43
  282.4 1.9 fusion.18
  284.4 4.2 %all-to-all-done.4 = bf16[16,32,96]{2,1,0:T(8,128)(2,1)S(1)} async-done(((bf16[16,32,96]{2,1,0:T(8,128)(2,1)}), bf16[16,32,96]{2,1,0:T(8,128)(2,1)S(1)}, u32[]{:S(2)}, u32[]{:S(2)}) %all-to-all-start.4) | async-done | bytes 98336 | tf_op jit(solution)/shard_map/all_to_all | solution.py:43
  288.6 0.7 broadcast_in_dim.112
  289.3 4.0 %all-to-all-start.5 = ((bf16[16,32,96]{2,1,0:T(8,128)(2,1)}), bf16[16,32,96]{2,1,0:T(8,128)(2,1)S(1)}, u32[]{:S(2)}, u32[]{:S(2)}) async-start(bf16[16,32,96]{2,1,0:T(8,128)(2,1)} %broadcast_in_dim.112), calls=%async_computation.5 | async-start | bytes 262144 | tf_op jit(solution)/shard_map/all_to_all | solution.py:43
  293.2 2.4 fusion.7
  295.7 3.8 %all-to-all-done.5 = bf16[16,32,96]{2,1,0:T(8,128)(2,1)S(1)} async-done(((bf16[16,32,96]{2,1,0:T(8,128)(2,1)}), bf16[16,32,96]{2,1,0:T(8,128)(2,1)S(1)}, u32[]{:S(2)}, u32[]{:S(2)}) %all-to-all-start.5) | async-done | bytes 98336 | tf_op jit(solution)/shard_map/all_to_all | solution.py:43
  300.1 1.3 convolution_convert_fusion.4
  301.4 2.1 fusion.28
  303.6 5.7 %all-to-all-start.6 = ((bf16[32,16,96]{2,1,0:T(8,128)(2,1)}), bf16[32,16,96]{2,1,0:T(8,128)(2,1)S(1)}, u32[]{:S(2)}, u32[]{:S(2)}) async-start(bf16[32,16,96]{2,1,0:T(8,128)(2,1)} %bitcast.56), calls=%async_computation.6 | async-start | bytes 262144 | tf_op jit(solution)/shard_map/all_to_all | solution.py:43
  309.5 7.4 %all-to-all-done.6 = bf16[32,16,96]{2,1,0:T(8,128)(2,1)S(1)} async-done(((bf16[32,16,96]{2,1,0:T(8,128)(2,1)}), bf16[32,16,96]{2,1,0:T(8,128)(2,1)S(1)}, u32[]{:S(2)}, u32[]{:S(2)}) %all-to-all-start.6) | async-done | bytes 98336 | tf_op jit(solution)/shard_map/all_to_all | solution.py:43
  317.0 0.7 broadcast_in_dim.115
  317.6 3.9 %all-to-all-start.7 = ((bf16[32,16,96]{2,1,0:T(8,128)(2,1)}), bf16[32,16,96]{2,1,0:T(8,128)(2,1)S(1)}, u32[]{:S(2)}, u32[]{:S(2)}) async-start(bf16[32,16,96]{2,1,0:T(8,128)(2,1)} %broadcast_in_dim.115), calls=%async_computation.7 | async-start | bytes 262144 | tf_op jit(solution)/shard_map/all_to_all | solution.py:43
  321.8 1.1 slice.234
  323.6 5.7 %all-to-all-done.7 = bf16[32,16,96]{2,1,0:T(8,128)(2,1)S(1)} async-done(((bf16[32,16,96]{2,1,0:T(8,128)(2,1)}), bf16[32,16,96]{2,1,0:T(8,128)(2,1)S(1)}, u32[]{:S(2)}, u32[]{:S(2)}) %all-to-all-start.7) | async-done | bytes 98336 | tf_op jit(solution)/shard_map/all_to_all | solution.py:43
  329.3 1.1 copy.66
  332.1 0.8 reshape.146
  332.9 8.0 %all-to-all-start.8 = ((bf16[16,2,720]{2,1,0:T(2,128)(2,1)}), bf16[16,2,720]{2,1,0:T(2,128)(2,1)S(1)}, u32[]{:S(2)}, u32[]{:S(2)}) async-start(bf16[16,2,720]{2,1,0:T(2,128)(2,1)} %reshape.146), calls=%async_computation.8 | async-start | bytes 98304 | tf_op jit(solution)/shard_map/all_to_all | solution.py:307
  341.3 11.2 %all-to-all-done.8 = bf16[16,2,720]{2,1,0:T(2,128)(2,1)S(1)} async-done(((bf16[16,2,720]{2,1,0:T(2,128)(2,1)}), bf16[16,2,720]{2,1,0:T(2,128)(2,1)S(1)}, u32[]{:S(2)}, u32[]{:S(2)}) %all-to-all-start.8) | async-done | bytes 46112 | tf_op jit(solution)/shard_map/all_to_all | solution.py:307
  353.0 1.1 copy.75
  (123 shorter events, 11.4 us)
Async XLA Ops:
  6.5 7.1 %copy-start.20 = (bf16[1,1,189,512]{3,2,1,0:T(8,128)(2,1)S(1)}, bf16[1,1,189,512]{3,2,1,0:T(8,128)(2,1)}, u32[]{:S(2)}) copy-start(bf16[1,1,189,512]{3,2,1,0:T(8,128)(2,1)} %param.9) | copy-start | bytes 580612
  6.5 114.6 %all-gather.6.cloned.1.call-start = ((), (), s32[]{:S(2)}) async-start(), calls=%async_computation.9 | async-start | bytes 7520256 | tf_op jit(solution)/shard_map/all_gather | solution.py:204
  8.4 227.7 %all-gather.8.cloned.1.call-start = ((), (), s32[]{:S(2)}) async-start(), calls=%async_computation.10 | async-start | bytes 8146944 | tf_op jit(solution)/shard_map/all_gather | solution.py:215
  8.5 1.7 copy-start
  10.1 1.1 copy-start.5
  11.2 0.7 copy-start.8
  11.9 41.5 %copy-start.24 = (s32[93]{0:T(128)S(1)}, s32[93]{0:T(128)}, u32[]{:S(2)}) copy-start(s32[93]{0:T(128)} %constant.27.clone) | copy-start | bytes 1120
  11.9 41.5 %copy-start.25 = (s32[93]{0:T(128)S(1)}, s32[93]{0:T(128)}, u32[]{:S(2)}) copy-start(s32[93]{0:T(128)} %constant.28.clone) | copy-start | bytes 1120
  11.9 41.5 %copy-start.26 = (s32[93]{0:T(128)S(1)}, s32[93]{0:T(128)}, u32[]{:S(2)}) copy-start(s32[93]{0:T(128)} %constant.29.clone) | copy-start | bytes 1120
  12.9 0.8 copy-start.7
  13.6 41.1 %copy-start.9 = (s32[1,1,15]{2,1,0:T(1,128)S(1)}, s32[1,1,15]{2,1,0:T(1,128)}, u32[]{:S(2)}) copy-start(s32[1,1,15]{2,1,0:T(1,128)} %param.12) | copy-start | bytes 184
  13.6 41.1 %copy-start.23 = (s32[384]{0:T(512)S(1)}, s32[384]{0:T(512)}, u32[]{:S(2)}) copy-start(s32[384]{0:T(512)} %constant.31.clone) | copy-start | bytes 4612
  13.6 41.2 %copy-start.22 = (s32[480]{0:T(512)S(1)}, s32[480]{0:T(512)}, u32[]{:S(2)}) copy-start(s32[480]{0:T(512)} %constant.30.clone) | copy-start | bytes 5764
  13.7 107.5 %copy-start.1 = (bf16[1,1,96,12384]{3,2,1,0:T(8,128)(2,1)S(1)}, bf16[1,1,96,12384]{3,2,1,0:T(8,128)(2,1)}, u32[]{:S(2)}) copy-start(bf16[1,1,96,12384]{3,2,1,0:T(8,128)(2,1)} %off_ref.3) | copy-start | bytes 7133188
  53.7 1.0 copy-start.10
  121.2 3.0 copy-start.2
  124.2 1.1 copy-start.3
  125.3 10.9 %copy-start.11 = (f32[480,512]{1,0:T(8,128)S(1)}, f32[480,512]{1,0:T(8,128)}, u32[]{:S(2)}) copy-start(f32[480,512]{1,0:T(8,128)} %copy-done.10) | copy-start | bytes 2949124
  133.7 3.4 collective-permute-start
  174.1 8.7 %copy-start.12 = (bf16[16,2,48,256]{3,2,0,1:T(8,128)(2,1)}, bf16[16,2,48,256]{3,2,0,1:T(8,128)(2,1)S(1)}, u32[]{:S(2)}) copy-start(bf16[16,2,48,256]{3,2,0,1:T(8,128)(2,1)S(1)} %copy.55) | copy-start | bytes 2359300
  174.1 9.0 %collective-permute-start.1 = (bf16[1536,256]{1,0:T(8,128)(2,1)S(1)}, bf16[1536,256]{1,0:T(8,128)(2,1)S(1)}, u32[]{:S(2)}, u32[]{:S(2)}) collective-permute-start(bf16[1536,256]{1,0:T(8,128)(2,1)S(1)} %bitcast.210), channel_id=1, source_target_pairs={{0,16},{16,0},{32,48},{48,32},{64,80},{80,64},{96,112},{112,96},{1... | collective-permute-start | bytes 2359304 | tf_op jit(solution)/shard_map/ppermute | solution.py:33
  183.1 0.9 copy-start.14
  185.4 3.3 collective-permute-start.2
  213.9 24.4 %all-to-all-start.1 = ((bf16[4,16,16,96]{3,2,1,0:T(8,128)(2,1)}), bf16[4,16,16,96]{3,2,1,0:T(8,128)(2,1)S(1)}, u32[]{:S(2)}, u32[]{:S(2)}) async-start(bf16[4,16,16,96]{3,2,1,0:T(8,128)(2,1)} %broadcast_in_dim.102), calls=%async_computation.1 | async-start | bytes 524288 | tf_op jit(solution)/shard_map/all_to_all | solution.py:43
  239.4 14.4 %copy-start.4 = (bf16[1536,256]{1,0:T(8,128)(2,1)S(1)}, bf16[1536,256]{1,0:T(8,128)(2,1)}, u32[]{:S(2)}) copy-start(bf16[1536,256]{1,0:T(8,128)(2,1)} %all_gather.25.right_ref) | copy-start | bytes 2359300
  239.4 14.4 %copy-start.6 = (bf16[1,1,189,1536]{3,2,1,0:T(8,128)(2,1)S(1)}, bf16[1,1,189,1536]{3,2,1,0:T(8,128)(2,1)}, u32[]{:S(2)}) copy-start(bf16[1,1,189,1536]{3,2,1,0:T(8,128)(2,1)} %inv_ref.1) | copy-start | bytes 1741828
  245.7 0.6 copy-start.16
  248.9 11.0 %all-to-all-start.2 = ((bf16[8,64,96]{2,1,0:T(8,128)(2,1)}), bf16[8,64,96]{2,1,0:T(8,128)(2,1)}, u32[]{:S(2)}, u32[]{:S(2)}) async-start(bf16[8,64,96]{2,1,0:T(8,128)(2,1)} %bitcast.43), calls=%async_computation.2 | async-start | bytes 262144 | tf_op jit(solution)/shard_map/all_to_all | solution.py:43
  261.5 10.0 %all-to-all-start.3 = ((bf16[8,64,96]{2,1,0:T(8,128)(2,1)}), bf16[8,64,96]{2,1,0:T(8,128)(2,1)S(1)}, u32[]{:S(2)}, u32[]{:S(2)}) async-start(bf16[8,64,96]{2,1,0:T(8,128)(2,1)} %broadcast_in_dim.109), calls=%async_computation.3 | async-start | bytes 262144 | tf_op jit(solution)/shard_map/all_to_all | solution.py:43
  274.7 7.8 %copy-start.17 = (bf16[32,384]{1,0:T(8,128)(2,1)S(1)}, bf16[32,384]{1,0:T(8,128)(2,1)}, u32[]{:S(2)}) copy-start(bf16[32,384]{1,0:T(8,128)(2,1)} %copy-done.16) | copy-start | bytes 73732
  274.7 7.8 %copy-start.19 = (bf16[16,32,96]{2,1,0:T(8,128)(2,1)S(1)}, bf16[16,32,96]{2,1,0:T(8,128)(2,1)}, u32[]{:S(2)}) copy-start(bf16[16,32,96]{2,1,0:T(8,128)(2,1)} %get-tuple-element.50) | copy-start | bytes 294916
  278.2 10.4 %all-to-all-start.4 = ((bf16[16,32,96]{2,1,0:T(8,128)(2,1)}), bf16[16,32,96]{2,1,0:T(8,128)(2,1)S(1)}, u32[]{:S(2)}, u32[]{:S(2)}) async-start(bf16[16,32,96]{2,1,0:T(8,128)(2,1)} %fusion.27), calls=%async_computation.4 | async-start | bytes 262144 | tf_op jit(solution)/shard_map/all_to_all | solution.py:43
  289.3 10.2 %all-to-all-start.5 = ((bf16[16,32,96]{2,1,0:T(8,128)(2,1)}), bf16[16,32,96]{2,1,0:T(8,128)(2,1)S(1)}, u32[]{:S(2)}, u32[]{:S(2)}) async-start(bf16[16,32,96]{2,1,0:T(8,128)(2,1)} %broadcast_in_dim.112), calls=%async_computation.5 | async-start | bytes 262144 | tf_op jit(solution)/shard_map/all_to_all | solution.py:43
  300.1 21.4 %copy-start.13 = (bf16[16,2,48,256]{3,2,0,1:T(8,128)(2,1)S(1)}, bf16[16,2,48,256]{3,2,0,1:T(8,128)(2,1)}, u32[]{:S(2)}) copy-start(bf16[16,2,48,256]{3,2,0,1:T(8,128)(2,1)} %copy-done.12) | copy-start | bytes 2359300
  303.6 19.5 %copy-start.18 = (bf16[32,384]{1,0:T(8,128)(2,1)S(1)}, bf16[32,384]{1,0:T(8,128)(2,1)}, u32[]{:S(2)}) copy-start(bf16[32,384]{1,0:T(8,128)(2,1)} %copy-done.16) | copy-start | bytes 73732
  303.6 13.3 %all-to-all-start.6 = ((bf16[32,16,96]{2,1,0:T(8,128)(2,1)}), bf16[32,16,96]{2,1,0:T(8,128)(2,1)S(1)}, u32[]{:S(2)}, u32[]{:S(2)}) async-start(bf16[32,16,96]{2,1,0:T(8,128)(2,1)} %bitcast.56), calls=%async_computation.6 | async-start | bytes 262144 | tf_op jit(solution)/shard_map/all_to_all | solution.py:43
  317.6 11.7 %all-to-all-start.7 = ((bf16[32,16,96]{2,1,0:T(8,128)(2,1)}), bf16[32,16,96]{2,1,0:T(8,128)(2,1)S(1)}, u32[]{:S(2)}, u32[]{:S(2)}) async-start(bf16[32,16,96]{2,1,0:T(8,128)(2,1)} %broadcast_in_dim.115), calls=%async_computation.7 | async-start | bytes 262144 | tf_op jit(solution)/shard_map/all_to_all | solution.py:43
  330.5 10.5 %copy-start.15 = (bf16[1536,256]{1,0:T(8,128)(2,1)S(1)}, bf16[1536,256]{1,0:T(8,128)(2,1)}, u32[]{:S(2)}) copy-start(bf16[1536,256]{1,0:T(8,128)(2,1)} %copy-done.14) | copy-start | bytes 2359300
  330.8 10.4 %copy-start.21 = (f32[96,256]{1,0:T(8,128)S(1)}, f32[96,256]{1,0:T(8,128)}, u32[]{:S(2)}) copy-start(f32[96,256]{1,0:T(8,128)} %convolution_bitcast_fusion.3) | copy-start | bytes 294916
  332.9 19.6 %all-to-all-start.8 = ((bf16[16,2,720]{2,1,0:T(2,128)(2,1)}), bf16[16,2,720]{2,1,0:T(2,128)(2,1)S(1)}, u32[]{:S(2)}, u32[]{:S(2)}) async-start(bf16[16,2,720]{2,1,0:T(2,128)(2,1)} %reshape.146), calls=%async_computation.8 | async-start | bytes 98304 | tf_op jit(solution)/shard_map/all_to_all | solution.py:307
Sparse Core Ops, SparseCore 0:
  9.4 111.7 all-gather.5
  123.2 112.8 all-gather.7

commit v7 on v4

--- a/solution.py
+++ b/solution.py
@@ -123,8 +123,7 @@
     def by_core(one, two):
         return jnp.where(first_core, one, two)
 
-    d_own0 = d_all[: heights[0]]
-    d_full0 = lax.all_gather(d_own0, "row", axis=0, tiled=True)
+    d_low = lax.all_gather(d_all[: starts[2]], "row", axis=0, tiled=False)
     b0 = b_all[: heights[0]]
     z0_left = lax.all_gather(b0[:, :half], "row", axis=0, tiled=True)
     z0_right = lax.all_gather(b0[:, half:], "row", axis=0, tiled=True)
@@ -151,6 +150,8 @@
     z0_kept = by_core(z0_left, z0_right)
     mask0, mask1 = lax.optimization_barrier((mask_rows(0), mask_rows(1)))
     live1 = mask0[:strip]
+    d_full0 = d_low[:, :strip].reshape(width, width)
+    d_leaf1 = d_low[:, strip:].reshape(rows_n * heights[1], width)
     yb_sent = dot(d_full0, z0_sent).astype(BF16)
     sent = placed[:strip, half:] - dot(panel(1, 0), yb_sent) * live1
     got = core_swap(sent.astype(BF16))
@@ -162,16 +163,18 @@
         for m in range(2, levels + 1)
     ]
 
-    d_own1 = d_all[starts[1] : starts[2]]
     z1 = (kept + got.astype(F32)).astype(BF16)
     z1 = lax.all_gather(z1, "row", axis=0, tiled=False)
     z1 = z1.reshape(rows_n, 2, heights[1], half).transpose(1, 0, 2, 3).reshape(width, half)
     z1_got = core_swap(z1)
+    yb_kept1 = dot(d_leaf1, z1).astype(BF16)
+    z1_got, yb_kept1, parts = lax.optimization_barrier((z1_got, yb_kept1, parts))
+    yb1 = jnp.concatenate([yb_kept1, dot(d_leaf1, z1_got).astype(BF16)], axis=1)
+    yb1 = lax.optimization_barrier(yb1)
+    d_own0 = d_all[: heights[0]]
+    d_own1 = d_all[starts[1] : starts[2]]
     y_kept1 = dot(d_own1, z1)
     y_sent1 = dot(d_own1, z1_got)
-    yb1 = jnp.concatenate([y_kept1, y_sent1], axis=1).astype(BF16)
-    yb1, parts = lax.optimization_barrier((yb1, parts))
-    yb1 = lax.all_gather(yb1, "row", axis=0, tiled=True)
     out0_kept = dot(d_own0, z0_kept)
     out0_sent = dot(d_own0, z0_sent)
     part = jnp.concatenate(

time: 349 us -> 350 us (level)
  blocking collectives: 195 us -> 137 us
  waiting for transfers between devices: 35 us -> 86.6 us
  local copies, waits for them, and re-layouts: 21 us -> 25.2 us
    all_gather x1 -> x0, blocking collectives: 38.3 us -> none  [shards(): yb1 = lax.all_gather(yb1, 'row', axis=0, tiled=True)]
    all_gather x1, waiting for transfers between devices: 5.46 us -> 31.5 us  [shards(): d_low = lax.all_gather(d_all[:starts[2]], 'row', axis=0, tiled=False)]
    all_to_all x2 -> x0, blocking collectives: 25.1 us -> none  [leaf_scatter(): lax.all_to_all(pieces, 'leaf', 0, 0, tiled=True, axis_index_groups=leaf_g...]
    all_gather x1, waiting for transfers between devices: 0.01 us -> 18.7 us  [shards(): everyone = lax.all_gather(packed, 'row', axis=0, tiled=False)]
    all_to_all x5 -> x7, starting transfers between devices: 23 us -> 33.4 us  [leaf_scatter(): lax.all_to_all(pieces, 'leaf', 0, 0, tiled=True, axis_index_groups=leaf_g...]
    ppermute x3, starting transfers between devices: 20.3 us -> 10.4 us  [core_swap(): return lax.ppermute(block, 'leaf', [(i, i ^ 1) for i in range(count)])]
    all_to_all x5 -> x7, waiting for transfers between devices: 17.2 us -> 23.9 us  [leaf_scatter(): lax.all_to_all(pieces, 'leaf', 0, 0, tiled=True, axis_index_groups=leaf_g...]
    all_to_all x1, blocking collectives: 19.5 us -> 25.4 us  [shards(): turned = lax.all_to_all(turned, 'row', 0, 0, tiled=True)]
  transfers between devices with their start and end apart: 11 -> 13, of which waited for: 8 -> 10; matrix products, arithmetic and copies ran while one was open for 9% -> 9% of each run, Pallas kernels for 1% -> 1%
where the time goes in v7:
time: 350 us; the launch traced here: 349 us
  blocking collectives  137 us (39%)
  waiting for transfers between devices  86.6 us (25%)
  starting transfers between devices  52 us (15%)
  matrix products  28 us (8%)
  local copies, waits for them, and re-layouts  25.2 us (7%)
  between operations  14.2 us (4%)
    all_gather x1, blocking collectives, shards(): z0_left = lax.all_gather(b0[:, :half], 'row', axis=0, tiled=True)  39.6 us
    all_gather x1, blocking collectives, shards(): z0_right = lax.all_gather(b0[:, half:], 'row', axis=0, tiled=True)  37.1 us
    all_gather x1, blocking collectives, shards(): z1 = lax.all_gather(z1, 'row', axis=0, tiled=False)  35.1 us
    all_to_all x7, starting transfers between devices, leaf_scatter(): lax.all_to_all(pieces, 'leaf', 0, 0, tiled=True, axis_index_groups=leaf_g...  33.4 us
    all_gather x1, waiting for transfers between devices, shards(): d_low = lax.all_gather(d_all[:starts[2]], 'row', axis=0, tiled=False)  31.5 us
    all_to_all x1, blocking collectives, shards(): turned = lax.all_to_all(turned, 'row', 0, 0, tiled=True)  25.4 us
    all_to_all x7, waiting for transfers between devices, leaf_scatter(): lax.all_to_all(pieces, 'leaf', 0, 0, tiled=True, axis_index_groups=leaf_g...  23.9 us
    all_gather x1, waiting for transfers between devices, shards(): everyone = lax.all_gather(packed, 'row', axis=0, tiled=False)  18.7 us
  transfers between devices with their start and end apart: 13, of which 10 were waited for; matrix products, arithmetic and copies ran while one was open for 9% of the time, Pallas kernels for 1%

profile of v7, /device:TPU:1, one launch (start us, length us, event | category | flops | bytes accessed | tf_op | source)
XLA Modules:
  0.0 348.7 jit_solution(7578430788648885650)
XLA Ops:
  6.5 1.8 slice.179
  8.5 3.0 pack_upper.1
  11.6 39.6 %all_gather.24 = bf16[1536,256]{1,0:T(8,128)(2,1)S(1)} all-gather(bf16[96,256]{1,0:T(8,128)(2,1)S(1)} %get-tuple-element.32), channel_id=1, replica_groups=mesh['leaf'=32,'row'=16] {'row'}, dimensions={0}, use_global_device_ids=true | all-gather | bytes 835584 | tf_op jit(solution)/shard_map/all_gather | solution.py:128
  51.9 37.1 %all_gather.25 = bf16[1536,256]{1,0:T(8,128)(2,1)S(1)} all-gather(bf16[96,256]{1,0:T(8,128)(2,1)S(1)} %get-tuple-element.31), channel_id=1, replica_groups=mesh['leaf'=32,'row'=16] {'row'}, dimensions={0}, use_global_device_ids=true | all-gather | bytes 835584 | tf_op jit(solution)/shard_map/all_gather | solution.py:129
  89.0 31.5 %all-gather.6.cloned.1.call-done = bf16[16,1,144,1536]{3,2,1,0:T(8,128)(2,1)} async-done(((bf16[1,1,144,1536]{3,2,1,0:T(8,128)(2,1)}), bf16[16,1,144,1536]{3,2,1,0:T(8,128)(2,1)}) %all-gather.6.cloned.1.call-update) | async-done | bytes 7077904 | tf_op jit(solution)/shard_map/all_gather | solution.py:126
  120.4 2.6 slice.228
  123.1 1.5 convolution_convert_fusion
  124.8 0.4 fusion.39
  125.2 2.7 collective-permute-start
  127.9 1.5 convolution_convert_fusion.1
  129.4 0.6 fusion.30
  130.1 0.6 fusion.28
  130.7 1.8 slice.231
  132.5 0.4 add_convert_fusion
  132.9 35.1 %all-gather.1 = bf16[1536,256]{1,0:T(8,128)(2,1)S(1)} all-gather(bf16[96,256]{1,0:T(8,128)(2,1)S(1)} %add_convert_fusion), channel_id=3, replica_groups=mesh['leaf'=32,'row'=16] {'row'}, dimensions={0}, use_global_device_ids=true | all-gather | bytes 835584 | tf_op jit(solution)/shard_map/all_gather | solution.py:167
  168.1 5.5 %collective-permute-start.1 = (bf16[1536,256]{1,0:T(8,128)(2,1)S(1)}, bf16[1536,256]{1,0:T(8,128)(2,1)S(1)}, u32[]{:S(2)}, u32[]{:S(2)}) collective-permute-start(bf16[1536,256]{1,0:T(8,128)(2,1)S(1)} %bitcast.220), channel_id=1, source_target_pairs={{0,16},{16,0},{32,48},{48,32},{64,80},{80,64},{96,112},{112,96},{1... | collective-permute-start | bytes 2359304 | tf_op jit(solution)/shard_map/ppermute | solution.py:33
  173.6 0.6 fusion.26
  174.2 0.6 fusion.24
  174.8 0.8 fusion
  175.7 0.8 fusion.1
  177.9 0.4 fusion.19
  178.4 2.1 collective-permute-start.2
  180.5 1.2 collective-permute-done.2
  181.9 25.4 %all_to_all.45 = bf16[16,16,384]{2,1,0:T(8,128)(2,1)S(1)} all-to-all(bf16[16,16,384]{2,1,0:T(8,128)(2,1)S(1)} %bitcast.239), channel_id=1, replica_groups=mesh['leaf'=32,'row'=16] {'row'}, dimensions={0} | all-to-all | bytes 393216 | tf_op jit(solution)/shard_map/all_to_all | solution.py:191
  207.5 0.7 broadcast_in_dim.102
  208.2 6.5 %all-to-all-start.1 = ((bf16[4,16,16,96]{3,2,1,0:T(8,128)(2,1)}), bf16[4,16,16,96]{3,2,1,0:T(8,128)(2,1)S(1)}, u32[]{:S(2)}, u32[]{:S(2)}) async-start(bf16[4,16,16,96]{3,2,1,0:T(8,128)(2,1)} %broadcast_in_dim.102), calls=%async_computation.1 | async-start | bytes 524288 | tf_op jit(solution)/shard_map/all_to_all | solution.py:43
  214.9 18.7 %all-gather.8.cloned.1.call-done = bf16[2304,1632]{1,0:T(8,128)(2,1)} async-done(((bf16[144,1632]{1,0:T(8,128)(2,1)}), bf16[2304,1632]{1,0:T(8,128)(2,1)}) %all-gather.8.cloned.1.call-update) | async-done | bytes 7520272 | tf_op jit(solution)/shard_map/all_gather | solution.py:137
  233.6 1.4 slice.247
  235.0 0.8 bitcast_select_fusion.1
  236.1 1.5 copy.53
  237.6 1.7 reshape.123
  239.3 0.5 convolution_convert_fusion.4
  239.7 2.6 fusion.32
  242.4 5.1 %all-to-all-start.2 = ((bf16[8,64,96]{2,1,0:T(8,128)(2,1)}), bf16[8,64,96]{2,1,0:T(8,128)(2,1)}, u32[]{:S(2)}, u32[]{:S(2)}) async-start(bf16[8,64,96]{2,1,0:T(8,128)(2,1)} %bitcast.51), calls=%async_computation.2 | async-start | bytes 262144 | tf_op jit(solution)/shard_map/all_to_all | solution.py:43
  247.5 2.0 convolution_bitcast_fusion
  249.5 1.2 slice.250
  250.7 1.3 slice.254
  252.2 0.6 all-to-all-done.2
  252.8 0.9 reduce_sum.66
  253.7 0.7 broadcast_in_dim.109
  254.4 4.2 %all-to-all-start.3 = ((bf16[8,64,96]{2,1,0:T(8,128)(2,1)}), bf16[8,64,96]{2,1,0:T(8,128)(2,1)S(1)}, u32[]{:S(2)}, u32[]{:S(2)}) async-start(bf16[8,64,96]{2,1,0:T(8,128)(2,1)} %broadcast_in_dim.109), calls=%async_computation.3 | async-start | bytes 262144 | tf_op jit(solution)/shard_map/all_to_all | solution.py:43
  258.6 1.9 fusion.4
  260.6 3.3 all-to-all-done.3
  264.8 2.2 fusion.31
  267.1 4.2 %all-to-all-start.4 = ((bf16[16,32,96]{2,1,0:T(8,128)(2,1)}), bf16[16,32,96]{2,1,0:T(8,128)(2,1)S(1)}, u32[]{:S(2)}, u32[]{:S(2)}) async-start(bf16[16,32,96]{2,1,0:T(8,128)(2,1)} %fusion.31), calls=%async_computation.4 | async-start | bytes 262144 | tf_op jit(solution)/shard_map/all_to_all | solution.py:43
  271.3 1.9 fusion.2
  273.2 4.2 %all-to-all-done.4 = bf16[16,32,96]{2,1,0:T(8,128)(2,1)S(1)} async-done(((bf16[16,32,96]{2,1,0:T(8,128)(2,1)}), bf16[16,32,96]{2,1,0:T(8,128)(2,1)S(1)}, u32[]{:S(2)}, u32[]{:S(2)}) %all-to-all-start.4) | async-done | bytes 98336 | tf_op jit(solution)/shard_map/all_to_all | solution.py:43
  277.5 0.7 broadcast_in_dim.112
  278.1 4.0 %all-to-all-start.5 = ((bf16[16,32,96]{2,1,0:T(8,128)(2,1)}), bf16[16,32,96]{2,1,0:T(8,128)(2,1)S(1)}, u32[]{:S(2)}, u32[]{:S(2)}) async-start(bf16[16,32,96]{2,1,0:T(8,128)(2,1)} %broadcast_in_dim.112), calls=%async_computation.5 | async-start | bytes 262144 | tf_op jit(solution)/shard_map/all_to_all | solution.py:43
  282.1 1.7 convolution_add_fusion.1
  283.9 4.5 %all-to-all-done.5 = bf16[16,32,96]{2,1,0:T(8,128)(2,1)S(1)} async-done(((bf16[16,32,96]{2,1,0:T(8,128)(2,1)}), bf16[16,32,96]{2,1,0:T(8,128)(2,1)S(1)}, u32[]{:S(2)}, u32[]{:S(2)}) %all-to-all-start.5) | async-done | bytes 98336 | tf_op jit(solution)/shard_map/all_to_all | solution.py:43
  289.3 2.1 fusion.18
  291.4 5.5 %all-to-all-start.6 = ((bf16[32,16,96]{2,1,0:T(8,128)(2,1)}), bf16[32,16,96]{2,1,0:T(8,128)(2,1)S(1)}, u32[]{:S(2)}, u32[]{:S(2)}) async-start(bf16[32,16,96]{2,1,0:T(8,128)(2,1)} %bitcast.61), calls=%async_computation.6 | async-start | bytes 262144 | tf_op jit(solution)/shard_map/all_to_all | solution.py:43
  296.9 2.1 convolution_bitcast_fusion.1
  298.9 5.6 %all-to-all-done.6 = bf16[32,16,96]{2,1,0:T(8,128)(2,1)S(1)} async-done(((bf16[32,16,96]{2,1,0:T(8,128)(2,1)}), bf16[32,16,96]{2,1,0:T(8,128)(2,1)S(1)}, u32[]{:S(2)}, u32[]{:S(2)}) %all-to-all-start.6) | async-done | bytes 98336 | tf_op jit(solution)/shard_map/all_to_all | solution.py:43
  304.6 0.7 broadcast_in_dim.115
  305.3 3.9 %all-to-all-start.7 = ((bf16[32,16,96]{2,1,0:T(8,128)(2,1)}), bf16[32,16,96]{2,1,0:T(8,128)(2,1)S(1)}, u32[]{:S(2)}, u32[]{:S(2)}) async-start(bf16[32,16,96]{2,1,0:T(8,128)(2,1)} %broadcast_in_dim.115), calls=%async_computation.7 | async-start | bytes 262144 | tf_op jit(solution)/shard_map/all_to_all | solution.py:43
  309.4 1.1 slice.259
  311.2 5.7 %all-to-all-done.7 = bf16[32,16,96]{2,1,0:T(8,128)(2,1)S(1)} async-done(((bf16[32,16,96]{2,1,0:T(8,128)(2,1)}), bf16[32,16,96]{2,1,0:T(8,128)(2,1)S(1)}, u32[]{:S(2)}, u32[]{:S(2)}) %all-to-all-start.7) | async-done | bytes 98336 | tf_op jit(solution)/shard_map/all_to_all | solution.py:43
  317.0 1.1 copy.60
  319.7 0.8 reshape.150
  320.5 8.2 %all-to-all-start.8 = ((bf16[16,2,720]{2,1,0:T(2,128)(2,1)}), bf16[16,2,720]{2,1,0:T(2,128)(2,1)S(1)}, u32[]{:S(2)}, u32[]{:S(2)}) async-start(bf16[16,2,720]{2,1,0:T(2,128)(2,1)} %reshape.150), calls=%async_computation.8 | async-start | bytes 98304 | tf_op jit(solution)/shard_map/all_to_all | solution.py:235
  329.1 11.2 %all-to-all-done.8 = bf16[16,2,720]{2,1,0:T(2,128)(2,1)S(1)} async-done(((bf16[16,2,720]{2,1,0:T(2,128)(2,1)}), bf16[16,2,720]{2,1,0:T(2,128)(2,1)S(1)}, u32[]{:S(2)}, u32[]{:S(2)}) %all-to-all-start.8) | async-done | bytes 46112 | tf_op jit(solution)/shard_map/all_to_all | solution.py:235
  340.8 1.1 copy.69
  (104 shorter events, 8.7 us)
Async XLA Ops:
  6.5 5.0 %copy-start.7 = (bf16[1,1,189,512]{3,2,1,0:T(8,128)(2,1)S(1)}, bf16[1,1,189,512]{3,2,1,0:T(8,128)(2,1)}, u32[]{:S(2)}) copy-start(bf16[1,1,189,512]{3,2,1,0:T(8,128)(2,1)} %param.9) | copy-start | bytes 580612
  6.5 113.9 %all-gather.6.cloned.1.call-start = ((), (), s32[]{:S(2)}) async-start(), calls=%async_computation.9 | async-start | bytes 7520256 | tf_op jit(solution)/shard_map/all_gather | solution.py:126
  8.4 225.2 %all-gather.8.cloned.1.call-start = ((), (), s32[]{:S(2)}) async-start(), calls=%async_computation.10 | async-start | bytes 8146944 | tf_op jit(solution)/shard_map/all_gather | solution.py:137
  8.5 42.7 %copy-start.10 = (s32[1,1,15]{2,1,0:T(1,128)S(1)}, s32[1,1,15]{2,1,0:T(1,128)}, u32[]{:S(2)}) copy-start(s32[1,1,15]{2,1,0:T(1,128)} %param.12) | copy-start | bytes 184
  8.5 42.7 %copy-start.12 = (s32[384]{0:T(512)S(1)}, s32[384]{0:T(512)}, u32[]{:S(2)}) copy-start(s32[384]{0:T(512)} %constant.31.clone) | copy-start | bytes 4612
  8.5 42.8 %copy-start.11 = (s32[480]{0:T(512)S(1)}, s32[480]{0:T(512)}, u32[]{:S(2)}) copy-start(s32[480]{0:T(512)} %constant.30.clone) | copy-start | bytes 5764
  8.5 42.9 %copy-start.13 = (s32[93]{0:T(128)S(1)}, s32[93]{0:T(128)}, u32[]{:S(2)}) copy-start(s32[93]{0:T(128)} %constant.27.clone) | copy-start | bytes 1120
  8.5 42.9 %copy-start.14 = (s32[93]{0:T(128)S(1)}, s32[93]{0:T(128)}, u32[]{:S(2)}) copy-start(s32[93]{0:T(128)} %constant.28.clone) | copy-start | bytes 1120
  8.5 42.9 %copy-start.15 = (s32[93]{0:T(128)S(1)}, s32[93]{0:T(128)}, u32[]{:S(2)}) copy-start(s32[93]{0:T(128)} %constant.29.clone) | copy-start | bytes 1120
  51.1 76.8 %copy-start.2 = (bf16[1536,256]{1,0:T(8,128)(2,1)}, bf16[1536,256]{1,0:T(8,128)(2,1)S(1)}, u32[]{:S(2)}) copy-start(bf16[1536,256]{1,0:T(8,128)(2,1)S(1)} %all_gather.24) | copy-start | bytes 2359300
  89.0 39.0 %copy-start.3 = (bf16[1536,256]{1,0:T(8,128)(2,1)}, bf16[1536,256]{1,0:T(8,128)(2,1)S(1)}, u32[]{:S(2)}) copy-start(bf16[1536,256]{1,0:T(8,128)(2,1)S(1)} %all_gather.25) | copy-start | bytes 2359300
  123.1 1.7 copy-start
  125.2 7.3 %collective-permute-start = (bf16[96,256]{1,0:T(8,128)(2,1)S(1)}, bf16[96,256]{1,0:T(8,128)(2,1)S(1)}, u32[]{:S(2)}, u32[]{:S(2)}) collective-permute-start(bf16[96,256]{1,0:T(8,128)(2,1)S(1)} %fusion.39), channel_id=1, source_target_pairs={{0,16},{16,0},{32,48},{48,32},{64,80},{80,64},{96,112},{112,96},{1... | collective-permute-start | bytes 147464 | tf_op jit(solution)/shard_map/ppermute | solution.py:33
  168.1 7.6 %collective-permute-start.1 = (bf16[1536,256]{1,0:T(8,128)(2,1)S(1)}, bf16[1536,256]{1,0:T(8,128)(2,1)S(1)}, u32[]{:S(2)}, u32[]{:S(2)}) collective-permute-start(bf16[1536,256]{1,0:T(8,128)(2,1)S(1)} %bitcast.220), channel_id=1, source_target_pairs={{0,16},{16,0},{32,48},{48,32},{64,80},{80,64},{96,112},{112,96},{1... | collective-permute-start | bytes 2359304 | tf_op jit(solution)/shard_map/ppermute | solution.py:33
  175.7 1.0 copy-start.4
  178.4 3.3 collective-permute-start.2
  208.2 27.6 %all-to-all-start.1 = ((bf16[4,16,16,96]{3,2,1,0:T(8,128)(2,1)}), bf16[4,16,16,96]{3,2,1,0:T(8,128)(2,1)S(1)}, u32[]{:S(2)}, u32[]{:S(2)}) async-start(bf16[4,16,16,96]{3,2,1,0:T(8,128)(2,1)} %broadcast_in_dim.102), calls=%async_computation.1 | async-start | bytes 524288 | tf_op jit(solution)/shard_map/all_to_all | solution.py:43
  236.1 11.3 %copy-start.1 = (bf16[1,1,189,1536]{3,2,1,0:T(8,128)(2,1)S(1)}, bf16[1,1,189,1536]{3,2,1,0:T(8,128)(2,1)}, u32[]{:S(2)}) copy-start(bf16[1,1,189,1536]{3,2,1,0:T(8,128)(2,1)} %inv_ref.1) | copy-start | bytes 1741828
  242.4 10.4 %all-to-all-start.2 = ((bf16[8,64,96]{2,1,0:T(8,128)(2,1)}), bf16[8,64,96]{2,1,0:T(8,128)(2,1)}, u32[]{:S(2)}, u32[]{:S(2)}) async-start(bf16[8,64,96]{2,1,0:T(8,128)(2,1)} %bitcast.51), calls=%async_computation.2 | async-start | bytes 262144 | tf_op jit(solution)/shard_map/all_to_all | solution.py:43
  254.4 9.5 %all-to-all-start.3 = ((bf16[8,64,96]{2,1,0:T(8,128)(2,1)}), bf16[8,64,96]{2,1,0:T(8,128)(2,1)S(1)}, u32[]{:S(2)}, u32[]{:S(2)}) async-start(bf16[8,64,96]{2,1,0:T(8,128)(2,1)} %broadcast_in_dim.109), calls=%async_computation.3 | async-start | bytes 262144 | tf_op jit(solution)/shard_map/all_to_all | solution.py:43
  267.1 10.4 %all-to-all-start.4 = ((bf16[16,32,96]{2,1,0:T(8,128)(2,1)}), bf16[16,32,96]{2,1,0:T(8,128)(2,1)S(1)}, u32[]{:S(2)}, u32[]{:S(2)}) async-start(bf16[16,32,96]{2,1,0:T(8,128)(2,1)} %fusion.31), calls=%async_computation.4 | async-start | bytes 262144 | tf_op jit(solution)/shard_map/all_to_all | solution.py:43
  277.5 11.8 %copy-start.6 = (bf16[16,32,96]{2,1,0:T(8,128)(2,1)S(1)}, bf16[16,32,96]{2,1,0:T(8,128)(2,1)}, u32[]{:S(2)}) copy-start(bf16[16,32,96]{2,1,0:T(8,128)(2,1)} %get-tuple-element.43) | copy-start | bytes 294916
  278.1 10.2 %all-to-all-start.5 = ((bf16[16,32,96]{2,1,0:T(8,128)(2,1)}), bf16[16,32,96]{2,1,0:T(8,128)(2,1)S(1)}, u32[]{:S(2)}, u32[]{:S(2)}) async-start(bf16[16,32,96]{2,1,0:T(8,128)(2,1)} %broadcast_in_dim.112), calls=%async_computation.5 | async-start | bytes 262144 | tf_op jit(solution)/shard_map/all_to_all | solution.py:43
  291.4 13.2 %all-to-all-start.6 = ((bf16[32,16,96]{2,1,0:T(8,128)(2,1)}), bf16[32,16,96]{2,1,0:T(8,128)(2,1)S(1)}, u32[]{:S(2)}, u32[]{:S(2)}) async-start(bf16[32,16,96]{2,1,0:T(8,128)(2,1)} %bitcast.61), calls=%async_computation.6 | async-start | bytes 262144 | tf_op jit(solution)/shard_map/all_to_all | solution.py:43
  305.3 11.7 %all-to-all-start.7 = ((bf16[32,16,96]{2,1,0:T(8,128)(2,1)}), bf16[32,16,96]{2,1,0:T(8,128)(2,1)S(1)}, u32[]{:S(2)}, u32[]{:S(2)}) async-start(bf16[32,16,96]{2,1,0:T(8,128)(2,1)} %broadcast_in_dim.115), calls=%async_computation.7 | async-start | bytes 262144 | tf_op jit(solution)/shard_map/all_to_all | solution.py:43
  318.1 10.7 %copy-start.5 = (bf16[1536,256]{1,0:T(8,128)(2,1)S(1)}, bf16[1536,256]{1,0:T(8,128)(2,1)}, u32[]{:S(2)}) copy-start(bf16[1536,256]{1,0:T(8,128)(2,1)} %copy-done.4) | copy-start | bytes 2359300
  318.4 10.6 %copy-start.8 = (f32[96,256]{1,0:T(8,128)S(1)}, f32[96,256]{1,0:T(8,128)}, u32[]{:S(2)}) copy-start(f32[96,256]{1,0:T(8,128)} %convolution_bitcast_fusion) | copy-start | bytes 294916
  318.4 10.6 %copy-start.9 = (f32[96,256]{1,0:T(8,128)S(1)}, f32[96,256]{1,0:T(8,128)}, u32[]{:S(2)}) copy-start(f32[96,256]{1,0:T(8,128)} %convolution_bitcast_fusion.1) | copy-start | bytes 294916
  320.5 19.8 %all-to-all-start.8 = ((bf16[16,2,720]{2,1,0:T(2,128)(2,1)}), bf16[16,2,720]{2,1,0:T(2,128)(2,1)S(1)}, u32[]{:S(2)}, u32[]{:S(2)}) async-start(bf16[16,2,720]{2,1,0:T(2,128)(2,1)} %reshape.150), calls=%async_computation.8 | async-start | bytes 98304 | tf_op jit(solution)/shard_map/all_to_all | solution.py:235
Sparse Core Ops, SparseCore 0:
  9.4 110.9 all-gather.5
  122.5 111.0 all-gather.7

commit v8 on v4

--- a/solution.py
+++ b/solution.py
@@ -147,16 +147,12 @@
     b_up = by_core(b_up, jnp.concatenate([b_up[:, half:], b_up[:, :half]], axis=1))
     placed = dot(spread, b_up)
 
-    z0_sent = by_core(z0_right, z0_left)
-    z0_kept = by_core(z0_left, z0_right)
+    z0 = jnp.concatenate([by_core(z0_left, z0_right), by_core(z0_right, z0_left)], axis=1)
     mask0, mask1 = lax.optimization_barrier((mask_rows(0), mask_rows(1)))
-    live1 = mask0[:strip]
-    yb_sent = dot(d_full0, z0_sent).astype(BF16)
-    sent = placed[:strip, half:] - dot(panel(1, 0), yb_sent) * live1
-    got = core_swap(sent.astype(BF16))
-    yb_kept = dot(d_full0, z0_kept).astype(BF16)
-    kept = placed[:strip, :half] - dot(panel(1, 0), yb_kept) * live1
-    yb0 = jnp.concatenate([yb_kept, yb_sent], axis=1)
+    yb0 = dot(d_full0, z0).astype(BF16)
+    part1 = placed[:strip] - dot(panel(1, 0), yb0) * mask0[:strip]
+    kept = part1[:, :half]
+    got = core_swap(part1[:, half:].astype(BF16))
     parts = [
         placed[strip * (m - 1) : strip * m] - dot(panel(m, 0), yb0) * mask0[strip * (m - 1) : strip * m]
         for m in range(2, levels + 1)
@@ -172,8 +168,7 @@
     yb1 = jnp.concatenate([y_kept1, y_sent1], axis=1).astype(BF16)
     yb1, parts = lax.optimization_barrier((yb1, parts))
     yb1 = lax.all_gather(yb1, "row", axis=0, tiled=True)
-    out0_kept = dot(d_own0, z0_kept)
-    out0_sent = dot(d_own0, z0_sent)
+    out0 = dot(d_own0, z0)
     part = jnp.concatenate(
         [
             parts[m - 2] - dot(panel(m, 1), yb1) * mask1[strip * (m - 2) : strip * (m - 1)]
@@ -190,15 +185,18 @@
     def turned_of(m):
         return turned[:, :, (m - 2) * strip : (m - 1) * strip]
 
-    def d_leaf(m):
-        rows = everyone[:, d_first[m] : d_first[m] + heights[m], :width]
-        return rows.reshape(rows_n * heights[m], width)
-
-    p_leaf = {}
+    p_first = {}
     at = 0
     for m, l in upper_pairs:
-        p_leaf[m, l] = everyone[:, :strip, at : at + (width >> l)]
+        p_first[m, l] = at
         at += width >> l
+
+    def d_leaf(m, block):
+        rows = block[:, d_first[m] : d_first[m] + heights[m], :width]
+        return rows.reshape(rows_n * heights[m], width)
+
+    def p_leaf(m, l, block):
+        return block[:, :strip, p_first[m, l] : p_first[m, l] + (width >> l)]
 
     def natural(z, m):
         z = z.reshape(rows_n, 2 * sub, 2**m, heights[m])
@@ -208,7 +206,9 @@
     sums = {}
     for m in range(2, levels + 1):
         if m == 2:
-            pieces = leaf_everyone(turned_of(2), 4).astype(F32)
+            pieces = jnp.broadcast_to(turned_of(2), (4, rows_n, sub, strip))
+            pieces, everyone = lax.optimization_barrier((pieces, everyone))
+            pieces = leaf_scatter(pieces).astype(F32)
             pieces = pieces.reshape(2, 2, rows_n, sub, strip).sum(axis=0).astype(BF16)
             z = pieces.transpose(1, 0, 2, 3).reshape(rows_n, 2 * sub, strip)
         else:
@@ -220,19 +220,19 @@
             v = v.reshape(size, rows_n * 2 * sub // size, strip)
             z = leaf_scatter(v).astype(F32).sum(axis=0).astype(BF16)
             z = leaf_everyone(z, size).reshape(rows_n, 2 * sub, strip)
-        y = dot_t(natural(z, m), d_leaf(m))
+        y = dot_t(natural(z, m), d_leaf(m, everyone))
         yb = y.astype(BF16)
         solved.append(yb.reshape(2 * sub, rows_n, heights[m]))
         for higher in range(m + 1, levels + 1):
-            term = dot_t(yb, p_leaf[higher, m]).transpose(1, 0, 2)
+            term = dot_t(yb, p_leaf(higher, m, everyone)).transpose(1, 0, 2)
             sums[higher] = term if m == 2 else sums[higher] + term
 
     d_rows = sum(heights[2:])
     done = jnp.concatenate(solved, axis=2).transpose(1, 0, 2)
     done = lax.all_to_all(done, "row", 0, 0, tiled=True)
     done = done.reshape(rows_n, 2, sub, d_rows).transpose(3, 1, 0, 2).reshape(d_rows, cols)
-    head_kept = jnp.concatenate([out0_kept, y_kept1], axis=0)
-    head_sent = jnp.concatenate([out0_sent, y_sent1], axis=0)
+    head_kept = jnp.concatenate([out0[:, :half], y_kept1], axis=0)
+    head_sent = jnp.concatenate([out0[:, half:], y_sent1], axis=0)
     head = by_core(
         jnp.concatenate([head_kept, head_sent], axis=1), jnp.concatenate([head_sent, head_kept], axis=1)
     )

time: 349 us -> 342 us (0.980)
  blocking collectives: 195 us -> 178 us
  waiting for transfers between devices: 35 us -> 49 us
  matrix products: 29 us -> 23.6 us
  starting transfers between devices: 49.1 us -> 53.4 us
    all_to_all x2 -> x1, blocking collectives: 25.1 us -> 13 us  [leaf_scatter(): lax.all_to_all(pieces, 'leaf', 0, 0, tiled=True, axis_index_groups=leaf_g...]
    all_gather x1, waiting for transfers between devices: 5.46 us -> 12.4 us  [shards(): d_full0 = lax.all_gather(d_own0, 'row', axis=0, tiled=True)]
    all_to_all x5 -> x6, waiting for transfers between devices: 17.2 us -> 23.5 us  [leaf_scatter(): lax.all_to_all(pieces, 'leaf', 0, 0, tiled=True, axis_index_groups=leaf_g...]
    dot_general x17 -> x14, matrix products: 16.5 us -> 10.5 us  [dot(): return jnp.dot(a, b, preferred_element_type=F32)]
    all_to_all x5 -> x6, starting transfers between devices: 23 us -> 29.1 us  [leaf_scatter(): lax.all_to_all(pieces, 'leaf', 0, 0, tiled=True, axis_index_groups=leaf_g...]
    all_gather x1, blocking collectives: 37.3 us -> 33.3 us  [shards(): z0_right = lax.all_gather(b0[:, half:], 'row', axis=0, tiled=True)]
  transfers between devices with their start and end apart: 11 -> 12, of which waited for: 8 -> 10; matrix products, arithmetic and copies ran while one was open for 9% -> 7% of each run, Pallas kernels for 1% -> 1%
where the time goes in v8:
time: 342 us; the launch traced here: 341 us
  blocking collectives  178 us (52%)
  starting transfers between devices  53.4 us (16%)
  waiting for transfers between devices  49 us (14%)
  matrix products  23.6 us (7%)
  local copies, waits for them, and re-layouts  18.6 us (5%)
  between operations  14.1 us (4%)
    all_gather x1, blocking collectives, shards(): z0_left = lax.all_gather(b0[:, :half], 'row', axis=0, tiled=True)  38.7 us
    all_gather x1, blocking collectives, shards(): yb1 = lax.all_gather(yb1, 'row', axis=0, tiled=True)  37.5 us
    all_gather x1, blocking collectives, shards(): z1 = lax.all_gather(z1, 'row', axis=0, tiled=False)  34.6 us
    all_gather x1, blocking collectives, shards(): z0_right = lax.all_gather(b0[:, half:], 'row', axis=0, tiled=True)  33.3 us
    all_to_all x6, starting transfers between devices, leaf_scatter(): lax.all_to_all(pieces, 'leaf', 0, 0, tiled=True, axis_index_groups=leaf_g...  29.1 us
    all_to_all x6, waiting for transfers between devices, leaf_scatter(): lax.all_to_all(pieces, 'leaf', 0, 0, tiled=True, axis_index_groups=leaf_g...  23.5 us
    all_to_all x1, blocking collectives, shards(): turned = lax.all_to_all(turned, 'row', 0, 0, tiled=True)  20.7 us
    ppermute x3, starting transfers between devices, core_swap(): return lax.ppermute(block, 'leaf', [(i, i ^ 1) for i in range(count)])  18.4 us
  transfers between devices with their start and end apart: 12, of which 10 were waited for; matrix products, arithmetic and copies ran while one was open for 7% of the time, Pallas kernels for 1%

profile of v8, /device:TPU:1, one launch (start us, length us, event | category | flops | bytes accessed | tf_op | source)
XLA Modules:
  0.0 340.5 jit_solution(3893350837429880883)
XLA Ops:
  6.5 1.7 slice.171
  8.4 3.0 pack_upper.1
  11.4 38.7 %all_gather.24 = bf16[1536,256]{1,0:T(8,128)(2,1)S(1)} all-gather(bf16[96,256]{1,0:T(8,128)(2,1)S(1)} %get-tuple-element.37), channel_id=1, replica_groups=mesh['leaf'=32,'row'=16] {'row'}, dimensions={0}, use_global_device_ids=true | all-gather | bytes 835584 | tf_op jit(solution)/shard_map/all_gather | solution.py:129
  50.6 0.3 fusion.54
  50.9 33.3 %all_gather.25 = bf16[1536,256]{1,0:T(8,128)(2,1)S(1)} all-gather(bf16[96,256]{1,0:T(8,128)(2,1)S(1)} %get-tuple-element.38), channel_id=1, replica_groups=mesh['leaf'=32,'row'=16] {'row'}, dimensions={0}, use_global_device_ids=true | all-gather | bytes 835584 | tf_op jit(solution)/shard_map/all_gather | solution.py:130
  84.4 12.4 %all-gather.6.cloned.1.call-done = bf16[1,1,1536,1536]{3,2,1,0:T(8,128)(2,1)} async-done(((bf16[1,1,96,1536]{3,2,1,0:T(8,128)(2,1)}), bf16[1,1,1536,1536]{3,2,1,0:T(8,128)(2,1)}) %all-gather.6.cloned.1.call-update) | async-done | bytes 4718608 | tf_op jit(solution)/shard_map/all_gather | solution.py:127
  96.8 5.1 %fusion.2 = bf16[512,1536]{1,0:T(8,128)(2,1)S(1)} fusion(bf16[1,1,1536,1536]{3,2,1,0:T(8,128)(2,1)} %all-gather.6.cloned.1.call-done, bf16[1536,256]{1,0:T(8,128)(2,1)S(1)} %get-tuple-element.28, bf16[1536,256]{1,0:T(8,128)(2,1)S(1)} %get-tuple-element.27), kind=kOutput, calls=%fused_computation.2 | convolution fusion | flops 2419851264 | bytes 7864320 | tf_op jit(solution)/shard_map/dot_general | solution.py:24
  102.0 0.6 fusion.31
  102.6 6.7 %collective-permute-start = (bf16[96,256]{1,0:T(8,128)(2,1)S(1)}, bf16[96,256]{1,0:T(8,128)(2,1)S(1)}, u32[]{:S(2)}, u32[]{:S(2)}) collective-permute-start(bf16[96,256]{1,0:T(8,128)(2,1)S(1)} %slice.328), channel_id=1, source_target_pairs={{0,16},{16,0},{32,48},{48,32},{64,80},{80,64},{96,112},{112,96},{1... | collective-permute-start | bytes 147464 | tf_op jit(solution)/shard_map/ppermute | solution.py:33
  109.3 0.6 fusion.33
  109.9 0.6 fusion.35
  110.6 34.6 %all-gather.1 = bf16[1536,256]{1,0:T(8,128)(2,1)S(1)} all-gather(bf16[96,256]{1,0:T(8,128)(2,1)S(1)} %fusion.65), channel_id=3, replica_groups=mesh['leaf'=32,'row'=16] {'row'}, dimensions={0}, use_global_device_ids=true | all-gather | bytes 835584 | tf_op jit(solution)/shard_map/all_gather | solution.py:163
  145.2 6.6 %collective-permute-start.1 = (bf16[1536,256]{1,0:T(8,128)(2,1)S(1)}, bf16[1536,256]{1,0:T(8,128)(2,1)S(1)}, u32[]{:S(2)}, u32[]{:S(2)}) collective-permute-start(bf16[1536,256]{1,0:T(8,128)(2,1)S(1)} %bitcast.208), channel_id=1, source_target_pairs={{0,16},{16,0},{32,48},{48,32},{64,80},{80,64},{96,112},{112,96},{1... | collective-permute-start | bytes 2359304 | tf_op jit(solution)/shard_map/ppermute | solution.py:33
  151.8 0.6 fusion.37
  152.5 0.6 fusion.39
  153.3 0.4 collective-permute-done.1
  154.0 37.5 %all_gather.29 = bf16[768,512]{1,0:T(8,128)(2,1)S(1)} all-gather(bf16[48,512]{1,0:T(8,128)(2,1)S(1)} %pad_maximum_fusion.4), channel_id=1, replica_groups=mesh['leaf'=32,'row'=16] {'row'}, dimensions={0}, use_global_device_ids=true | all-gather | bytes 835584 | tf_op jit(solution)/shard_map/all_gather | solution.py:170
  191.5 0.3 fusion.26
  191.8 0.3 fusion.27
  192.1 0.3 fusion.28
  192.3 0.3 fusion.29
  192.8 5.0 %collective-permute-start.2 = (bf16[384,256]{1,0:T(8,128)(2,1)S(1)}, bf16[384,256]{1,0:T(8,128)(2,1)S(1)}, u32[]{:S(2)}, u32[]{:S(2)}) collective-permute-start(bf16[384,256]{1,0:T(8,128)(2,1)S(1)} %slice.327), channel_id=1, source_target_pairs={{0,16},{16,0},{32,48},{48,32},{64,80},{80,64},{96,112},{112,96},{1... | collective-permute-start | bytes 589832 | tf_op jit(solution)/shard_map/ppermute | solution.py:33
  197.8 1.0 collective-permute-done.2
  199.1 20.7 %all_to_all.45 = bf16[16,16,384]{2,1,0:T(8,128)(2,1)S(1)} all-to-all(bf16[16,16,384]{2,1,0:T(8,128)(2,1)S(1)} %bitcast.216), channel_id=1, replica_groups=mesh['leaf'=32,'row'=16] {'row'}, dimensions={0} | all-to-all | bytes 393216 | tf_op jit(solution)/shard_map/all_to_all | solution.py:183
  219.9 0.7 broadcast_in_dim.102
  220.7 7.3 %all-to-all-start.1 = ((bf16[4,16,16,96]{3,2,1,0:T(8,128)(2,1)}), bf16[4,16,16,96]{3,2,1,0:T(8,128)(2,1)S(1)}, u32[]{:S(2)}, u32[]{:S(2)}) async-start(bf16[4,16,16,96]{3,2,1,0:T(8,128)(2,1)} %broadcast_in_dim.102), calls=%async_computation.1 | async-start | bytes 524288 | tf_op jit(solution)/shard_map/all_to_all | solution.py:43
  228.2 1.4 slice.209
  229.6 3.4 all-to-all-done.1
  233.3 0.6 copy.53
  233.9 0.7 reshape.113
  234.6 0.5 convolution_convert_fusion
  235.1 2.6 fusion.41
  237.7 5.6 %all-to-all-start.2 = ((bf16[8,64,96]{2,1,0:T(8,128)(2,1)}), bf16[8,64,96]{2,1,0:T(8,128)(2,1)S(1)}, u32[]{:S(2)}, u32[]{:S(2)}) async-start(bf16[8,64,96]{2,1,0:T(8,128)(2,1)} %bitcast.43), calls=%async_computation.2 | async-start | bytes 262144 | tf_op jit(solution)/shard_map/all_to_all | solution.py:43
  243.4 1.2 slice.212
  244.6 1.3 slice.216
  246.1 2.5 all-to-all-done.2
  248.6 0.7 broadcast_in_dim.109
  249.3 4.1 %all-to-all-start.3 = ((bf16[8,64,96]{2,1,0:T(8,128)(2,1)}), bf16[8,64,96]{2,1,0:T(8,128)(2,1)S(1)}, u32[]{:S(2)}, u32[]{:S(2)}) async-start(bf16[8,64,96]{2,1,0:T(8,128)(2,1)} %broadcast_in_dim.109), calls=%async_computation.3 | async-start | bytes 262144 | tf_op jit(solution)/shard_map/all_to_all | solution.py:43
  253.4 1.9 fusion.7
  255.4 3.3 all-to-all-done.3
  259.4 0.3 convolution_convert_fusion.1
  259.7 2.2 fusion.40
  261.9 4.2 %all-to-all-start.4 = ((bf16[16,32,96]{2,1,0:T(8,128)(2,1)}), bf16[16,32,96]{2,1,0:T(8,128)(2,1)S(1)}, u32[]{:S(2)}, u32[]{:S(2)}) async-start(bf16[16,32,96]{2,1,0:T(8,128)(2,1)} %fusion.40), calls=%async_computation.4 | async-start | bytes 262144 | tf_op jit(solution)/shard_map/all_to_all | solution.py:43
  266.1 1.9 fusion.5
  268.0 4.3 %all-to-all-done.4 = bf16[16,32,96]{2,1,0:T(8,128)(2,1)S(1)} async-done(((bf16[16,32,96]{2,1,0:T(8,128)(2,1)}), bf16[16,32,96]{2,1,0:T(8,128)(2,1)S(1)}, u32[]{:S(2)}, u32[]{:S(2)}) %all-to-all-start.4) | async-done | bytes 98336 | tf_op jit(solution)/shard_map/all_to_all | solution.py:43
  272.3 0.7 broadcast_in_dim.112
  273.0 4.0 %all-to-all-start.5 = ((bf16[16,32,96]{2,1,0:T(8,128)(2,1)}), bf16[16,32,96]{2,1,0:T(8,128)(2,1)S(1)}, u32[]{:S(2)}, u32[]{:S(2)}) async-start(bf16[16,32,96]{2,1,0:T(8,128)(2,1)} %broadcast_in_dim.112), calls=%async_computation.5 | async-start | bytes 262144 | tf_op jit(solution)/shard_map/all_to_all | solution.py:43
  277.0 1.7 convolution_add_fusion.1
  278.7 4.4 %all-to-all-done.5 = bf16[16,32,96]{2,1,0:T(8,128)(2,1)S(1)} async-done(((bf16[16,32,96]{2,1,0:T(8,128)(2,1)}), bf16[16,32,96]{2,1,0:T(8,128)(2,1)S(1)}, u32[]{:S(2)}, u32[]{:S(2)}) %all-to-all-start.5) | async-done | bytes 98336 | tf_op jit(solution)/shard_map/all_to_all | solution.py:43
  283.2 0.3 copy.57
  284.1 1.4 fusion.21
  285.6 13.0 %all_to_all.46 = bf16[32,16,96]{2,1,0:T(8,128)(2,1)S(1)} all-to-all(bf16[32,16,96]{2,1,0:T(8,128)(2,1)S(1)} %bitcast.217), channel_id=1, replica_groups={{0,16,32,48,64,80,96,112,128,144,160,176,192,208,224,240,256,272,288,30..., dimensions={0} | all-to-all | bytes 196608 | tf_op jit(solution)/shard_map/all_to_all | solution.py:43
  298.6 0.7 broadcast_in_dim.115
  299.3 3.9 %all-to-all-start.7 = ((bf16[32,16,96]{2,1,0:T(8,128)(2,1)}), bf16[32,16,96]{2,1,0:T(8,128)(2,1)S(1)}, u32[]{:S(2)}, u32[]{:S(2)}) async-start(bf16[32,16,96]{2,1,0:T(8,128)(2,1)} %broadcast_in_dim.115), calls=%async_computation.7 | async-start | bytes 262144 | tf_op jit(solution)/shard_map/all_to_all | solution.py:43
  303.2 0.4 convolution_bitcast_fusion
  303.6 1.1 slice.221
  305.4 5.6 %all-to-all-done.7 = bf16[32,16,96]{2,1,0:T(8,128)(2,1)S(1)} async-done(((bf16[32,16,96]{2,1,0:T(8,128)(2,1)}), bf16[32,16,96]{2,1,0:T(8,128)(2,1)S(1)}, u32[]{:S(2)}, u32[]{:S(2)}) %all-to-all-start.7) | async-done | bytes 98336 | tf_op jit(solution)/shard_map/all_to_all | solution.py:43
  311.0 1.1 copy.60
  312.1 0.3 reshape_reshape.11
  312.7 0.3 reshape.125
  313.7 0.8 reshape.140
  314.6 6.0 %all-to-all-start.8 = ((bf16[16,2,720]{2,1,0:T(2,128)(2,1)}), bf16[16,2,720]{2,1,0:T(2,128)(2,1)S(1)}, u32[]{:S(2)}, u32[]{:S(2)}) async-start(bf16[16,2,720]{2,1,0:T(2,128)(2,1)} %reshape.140), calls=%async_computation.8 | async-start | bytes 98304 | tf_op jit(solution)/shard_map/all_to_all | solution.py:232
  320.6 11.5 %all-to-all-done.8 = bf16[16,2,720]{2,1,0:T(2,128)(2,1)S(1)} async-done(((bf16[16,2,720]{2,1,0:T(2,128)(2,1)}), bf16[16,2,720]{2,1,0:T(2,128)(2,1)S(1)}, u32[]{:S(2)}, u32[]{:S(2)}) %all-to-all-start.8) | async-done | bytes 46112 | tf_op jit(solution)/shard_map/all_to_all | solution.py:232
  332.5 1.1 copy.69
  (91 shorter events, 5.9 us)
Async XLA Ops:
  6.5 4.9 %copy-start.6 = (bf16[1,1,189,512]{3,2,1,0:T(8,128)(2,1)S(1)}, bf16[1,1,189,512]{3,2,1,0:T(8,128)(2,1)}, u32[]{:S(2)}) copy-start(bf16[1,1,189,512]{3,2,1,0:T(8,128)(2,1)} %param.9) | copy-start | bytes 580612
  6.5 90.3 %all-gather.6.cloned.1.call-start = ((), (), s32[]{:S(2)}) async-start(), calls=%async_computation.9 | async-start | bytes 5013504 | tf_op jit(solution)/shard_map/all_gather | solution.py:127
  8.3 211.6 %all-gather.8.cloned.1.call-start = ((), (), s32[]{:S(2)}) async-start(), calls=%async_computation.10 | async-start | bytes 8146944 | tf_op jit(solution)/shard_map/all_gather | solution.py:138
  8.3 41.8 %copy-start.7 = (s32[1,1,15]{2,1,0:T(1,128)S(1)}, s32[1,1,15]{2,1,0:T(1,128)}, u32[]{:S(2)}) copy-start(s32[1,1,15]{2,1,0:T(1,128)} %param.12) | copy-start | bytes 184
  8.4 41.8 %copy-start.9 = (s32[384]{0:T(512)S(1)}, s32[384]{0:T(512)}, u32[]{:S(2)}) copy-start(s32[384]{0:T(512)} %constant.31.clone) | copy-start | bytes 4612
  8.4 41.9 %copy-start.8 = (s32[480]{0:T(512)S(1)}, s32[480]{0:T(512)}, u32[]{:S(2)}) copy-start(s32[480]{0:T(512)} %constant.30.clone) | copy-start | bytes 5764
  8.4 42.0 %copy-start.10 = (s32[93]{0:T(128)S(1)}, s32[93]{0:T(128)}, u32[]{:S(2)}) copy-start(s32[93]{0:T(128)} %constant.27.clone) | copy-start | bytes 1120
  8.4 42.0 %copy-start.11 = (s32[93]{0:T(128)S(1)}, s32[93]{0:T(128)}, u32[]{:S(2)}) copy-start(s32[93]{0:T(128)} %constant.28.clone) | copy-start | bytes 1120
  8.4 42.0 %copy-start.12 = (s32[93]{0:T(128)S(1)}, s32[93]{0:T(128)}, u32[]{:S(2)}) copy-start(s32[93]{0:T(128)} %constant.29.clone) | copy-start | bytes 1120
  84.3 17.6 %copy-start.2 = (bf16[1536,256]{1,0:T(8,128)(2,1)}, bf16[1536,256]{1,0:T(8,128)(2,1)S(1)}, u32[]{:S(2)}) copy-start(bf16[1536,256]{1,0:T(8,128)(2,1)S(1)} %get-tuple-element.27) | copy-start | bytes 2359300
  84.4 17.6 %copy-start.4 = (bf16[1536,256]{1,0:T(8,128)(2,1)}, bf16[1536,256]{1,0:T(8,128)(2,1)S(1)}, u32[]{:S(2)}) copy-start(bf16[1536,256]{1,0:T(8,128)(2,1)S(1)} %get-tuple-element.28) | copy-start | bytes 2359300
  96.8 5.2 %copy-start = (bf16[1,1,96,12384]{3,2,1,0:T(8,128)(2,1)S(1)}, bf16[1,1,96,12384]{3,2,1,0:T(8,128)(2,1)}, u32[]{:S(2)}) copy-start(bf16[1,1,96,12384]{3,2,1,0:T(8,128)(2,1)} %off_ref.1) | copy-start | bytes 7133188
  102.6 7.9 %collective-permute-start = (bf16[96,256]{1,0:T(8,128)(2,1)S(1)}, bf16[96,256]{1,0:T(8,128)(2,1)S(1)}, u32[]{:S(2)}, u32[]{:S(2)}) collective-permute-start(bf16[96,256]{1,0:T(8,128)(2,1)S(1)} %slice.328), channel_id=1, source_target_pairs={{0,16},{16,0},{32,48},{48,32},{64,80},{80,64},{96,112},{112,96},{1... | collective-permute-start | bytes 147464 | tf_op jit(solution)/shard_map/ppermute | solution.py:33
  145.2 7.9 %copy-start.1 = (bf16[1,1,189,1536]{3,2,1,0:T(8,128)(2,1)S(1)}, bf16[1,1,189,1536]{3,2,1,0:T(8,128)(2,1)}, u32[]{:S(2)}) copy-start(bf16[1,1,189,1536]{3,2,1,0:T(8,128)(2,1)} %inv_ref.1) | copy-start | bytes 1741828
  145.2 8.5 %collective-permute-start.1 = (bf16[1536,256]{1,0:T(8,128)(2,1)S(1)}, bf16[1536,256]{1,0:T(8,128)(2,1)S(1)}, u32[]{:S(2)}, u32[]{:S(2)}) collective-permute-start(bf16[1536,256]{1,0:T(8,128)(2,1)S(1)} %bitcast.208), channel_id=1, source_target_pairs={{0,16},{16,0},{32,48},{48,32},{64,80},{80,64},{96,112},{112,96},{1... | collective-permute-start | bytes 2359304 | tf_op jit(solution)/shard_map/ppermute | solution.py:33
  192.8 6.1 %collective-permute-start.2 = (bf16[384,256]{1,0:T(8,128)(2,1)S(1)}, bf16[384,256]{1,0:T(8,128)(2,1)S(1)}, u32[]{:S(2)}, u32[]{:S(2)}) collective-permute-start(bf16[384,256]{1,0:T(8,128)(2,1)S(1)} %slice.327), channel_id=1, source_target_pairs={{0,16},{16,0},{32,48},{48,32},{64,80},{80,64},{96,112},{112,96},{1... | collective-permute-start | bytes 589832 | tf_op jit(solution)/shard_map/ppermute | solution.py:33
  220.7 12.3 %all-to-all-start.1 = ((bf16[4,16,16,96]{3,2,1,0:T(8,128)(2,1)}), bf16[4,16,16,96]{3,2,1,0:T(8,128)(2,1)S(1)}, u32[]{:S(2)}, u32[]{:S(2)}) async-start(bf16[4,16,16,96]{3,2,1,0:T(8,128)(2,1)} %broadcast_in_dim.102), calls=%async_computation.1 | async-start | bytes 524288 | tf_op jit(solution)/shard_map/all_to_all | solution.py:43
  237.7 10.9 %all-to-all-start.2 = ((bf16[8,64,96]{2,1,0:T(8,128)(2,1)}), bf16[8,64,96]{2,1,0:T(8,128)(2,1)S(1)}, u32[]{:S(2)}, u32[]{:S(2)}) async-start(bf16[8,64,96]{2,1,0:T(8,128)(2,1)} %bitcast.43), calls=%async_computation.2 | async-start | bytes 262144 | tf_op jit(solution)/shard_map/all_to_all | solution.py:43
  249.3 9.4 %all-to-all-start.3 = ((bf16[8,64,96]{2,1,0:T(8,128)(2,1)}), bf16[8,64,96]{2,1,0:T(8,128)(2,1)S(1)}, u32[]{:S(2)}, u32[]{:S(2)}) async-start(bf16[8,64,96]{2,1,0:T(8,128)(2,1)} %broadcast_in_dim.109), calls=%async_computation.3 | async-start | bytes 262144 | tf_op jit(solution)/shard_map/all_to_all | solution.py:43
  261.9 10.4 %all-to-all-start.4 = ((bf16[16,32,96]{2,1,0:T(8,128)(2,1)}), bf16[16,32,96]{2,1,0:T(8,128)(2,1)S(1)}, u32[]{:S(2)}, u32[]{:S(2)}) async-start(bf16[16,32,96]{2,1,0:T(8,128)(2,1)} %fusion.40), calls=%async_computation.4 | async-start | bytes 262144 | tf_op jit(solution)/shard_map/all_to_all | solution.py:43
  273.0 10.2 %all-to-all-start.5 = ((bf16[16,32,96]{2,1,0:T(8,128)(2,1)}), bf16[16,32,96]{2,1,0:T(8,128)(2,1)S(1)}, u32[]{:S(2)}, u32[]{:S(2)}) async-start(bf16[16,32,96]{2,1,0:T(8,128)(2,1)} %broadcast_in_dim.112), calls=%async_computation.5 | async-start | bytes 262144 | tf_op jit(solution)/shard_map/all_to_all | solution.py:43
  278.7 24.5 %copy-start.3 = (bf16[1536,256]{1,0:T(8,128)(2,1)S(1)}, bf16[1536,256]{1,0:T(8,128)(2,1)}, u32[]{:S(2)}) copy-start(bf16[1536,256]{1,0:T(8,128)(2,1)} %copy-done.2) | copy-start | bytes 2359300
  283.9 19.4 %copy-start.5 = (bf16[1536,256]{1,0:T(8,128)(2,1)S(1)}, bf16[1536,256]{1,0:T(8,128)(2,1)}, u32[]{:S(2)}) copy-start(bf16[1536,256]{1,0:T(8,128)(2,1)} %copy-done.4) | copy-start | bytes 2359300
  299.3 11.7 %all-to-all-start.7 = ((bf16[32,16,96]{2,1,0:T(8,128)(2,1)}), bf16[32,16,96]{2,1,0:T(8,128)(2,1)S(1)}, u32[]{:S(2)}, u32[]{:S(2)}) async-start(bf16[32,16,96]{2,1,0:T(8,128)(2,1)} %broadcast_in_dim.115), calls=%async_computation.7 | async-start | bytes 262144 | tf_op jit(solution)/shard_map/all_to_all | solution.py:43
  314.6 17.5 %all-to-all-start.8 = ((bf16[16,2,720]{2,1,0:T(2,128)(2,1)}), bf16[16,2,720]{2,1,0:T(2,128)(2,1)S(1)}, u32[]{:S(2)}, u32[]{:S(2)}) async-start(bf16[16,2,720]{2,1,0:T(2,128)(2,1)} %reshape.140), calls=%async_computation.8 | async-start | bytes 98304 | tf_op jit(solution)/shard_map/all_to_all | solution.py:232
Sparse Core Ops, SparseCore 0:
  9.4 87.3 all-gather.5
  98.9 113.9 all-gather.7

commit v9 on v8

--- a/solution.py
+++ b/solution.py
@@ -224,7 +224,10 @@
         yb = y.astype(BF16)
         solved.append(yb.reshape(2 * sub, rows_n, heights[m]))
         for higher in range(m + 1, levels + 1):
-            term = dot_t(yb, p_leaf(higher, m, everyone)).transpose(1, 0, 2)
+            block = p_leaf(higher, m, everyone)
+            if higher == m + 1:
+                block = lax.optimization_barrier(block)
+            term = dot_t(yb, block).transpose(1, 0, 2)
             sums[higher] = term if m == 2 else sums[higher] + term
 
     d_rows = sum(heights[2:])

time: 342 us -> 347 us (1.015)
  local copies, waits for them, and re-layouts: 18.6 us -> 26.4 us
  waiting for transfers between devices: 49 us -> 41.7 us
    all_to_all x6, waiting for transfers between devices: 23.5 us -> 18.7 us  [leaf_scatter(): lax.all_to_all(pieces, 'leaf', 0, 0, tiled=True, axis_index_groups=leaf_g...]
    slice x0 -> x3, local copies, waits for them, and re-layouts: none -> 3.69 us  [p_leaf(): return block[:, :strip, p_first[m, l]:p_first[m, l] + (width >> l)]]
  transfers between devices with their start and end apart: 12 -> 12, of which waited for: 10 -> 8; matrix products, arithmetic and copies ran while one was open for 7% -> 9% of each run, Pallas kernels for 1% -> 1%
where the time goes in v9:
time: 347 us; the launch traced here: 345 us
  blocking collectives  179 us (52%)
  starting transfers between devices  54.4 us (16%)
  waiting for transfers between devices  41.7 us (12%)
  local copies, waits for them, and re-layouts  26.4 us (8%)
  matrix products  24.2 us (7%)
  between operations  14.1 us (4%)
    all_gather x1, blocking collectives, shards(): z0_left = lax.all_gather(b0[:, :half], 'row', axis=0, tiled=True)  38.7 us
    all_gather x1, blocking collectives, shards(): yb1 = lax.all_gather(yb1, 'row', axis=0, tiled=True)  37.5 us
    all_gather x1, blocking collectives, shards(): z1 = lax.all_gather(z1, 'row', axis=0, tiled=False)  35 us
    all_gather x1, blocking collectives, shards(): z0_right = lax.all_gather(b0[:, half:], 'row', axis=0, tiled=True)  34.2 us
    all_to_all x6, starting transfers between devices, leaf_scatter(): lax.all_to_all(pieces, 'leaf', 0, 0, tiled=True, axis_index_groups=leaf_g...  28.6 us
    all_to_all x1, blocking collectives, shards(): turned = lax.all_to_all(turned, 'row', 0, 0, tiled=True)  20.6 us
    ppermute x3, starting transfers between devices, core_swap(): return lax.ppermute(block, 'leaf', [(i, i ^ 1) for i in range(count)])  19.8 us
    all_to_all x6, waiting for transfers between devices, leaf_scatter(): lax.all_to_all(pieces, 'leaf', 0, 0, tiled=True, axis_index_groups=leaf_g...  18.7 us
  transfers between devices with their start and end apart: 12, of which 8 were waited for; matrix products, arithmetic and copies ran while one was open for 9% of the time, Pallas kernels for 1%

profile of v9, /device:TPU:1, one launch (start us, length us, event | category | flops | bytes accessed | tf_op | source)
XLA Modules:
  0.0 345.4 jit_solution(15484630223240939)
XLA Ops:
  6.5 1.7 slice.171
  8.4 3.0 pack_upper.1
  11.5 38.7 %all_gather.24 = bf16[1536,256]{1,0:T(8,128)(2,1)S(1)} all-gather(bf16[96,256]{1,0:T(8,128)(2,1)S(1)} %get-tuple-element.37), channel_id=1, replica_groups=mesh['leaf'=32,'row'=16] {'row'}, dimensions={0}, use_global_device_ids=true | all-gather | bytes 835584 | tf_op jit(solution)/shard_map/all_gather | solution.py:129
  50.9 34.2 %all_gather.25 = bf16[1536,256]{1,0:T(8,128)(2,1)S(1)} all-gather(bf16[96,256]{1,0:T(8,128)(2,1)S(1)} %get-tuple-element.38), channel_id=1, replica_groups=mesh['leaf'=32,'row'=16] {'row'}, dimensions={0}, use_global_device_ids=true | all-gather | bytes 835584 | tf_op jit(solution)/shard_map/all_gather | solution.py:130
  85.3 10.4 %all-gather.6.cloned.1.call-done = bf16[1,1,1536,1536]{3,2,1,0:T(8,128)(2,1)} async-done(((bf16[1,1,96,1536]{3,2,1,0:T(8,128)(2,1)}), bf16[1,1,1536,1536]{3,2,1,0:T(8,128)(2,1)}) %all-gather.6.cloned.1.call-update) | async-done | bytes 4718608 | tf_op jit(solution)/shard_map/all_gather | solution.py:127
  95.7 5.1 %fusion.2 = bf16[512,1536]{1,0:T(8,128)(2,1)S(1)} fusion(bf16[1,1,1536,1536]{3,2,1,0:T(8,128)(2,1)} %all-gather.6.cloned.1.call-done, bf16[1536,256]{1,0:T(8,128)(2,1)S(1)} %get-tuple-element.28, bf16[1536,256]{1,0:T(8,128)(2,1)S(1)} %get-tuple-element.27), kind=kOutput, calls=%fused_computation.2 | convolution fusion | flops 2419851264 | bytes 7864320 | tf_op jit(solution)/shard_map/dot_general | solution.py:24
  100.9 0.6 fusion.24
  101.5 8.0 %collective-permute-start = (bf16[96,256]{1,0:T(8,128)(2,1)S(1)}, bf16[96,256]{1,0:T(8,128)(2,1)S(1)}, u32[]{:S(2)}, u32[]{:S(2)}) collective-permute-start(bf16[96,256]{1,0:T(8,128)(2,1)S(1)} %slice.316), channel_id=1, source_target_pairs={{0,16},{16,0},{32,48},{48,32},{64,80},{80,64},{96,112},{112,96},{1... | collective-permute-start | bytes 147464 | tf_op jit(solution)/shard_map/ppermute | solution.py:33
  109.5 0.6 fusion.26
  110.2 0.6 fusion.28
  110.8 35.0 %all-gather.1 = bf16[1536,256]{1,0:T(8,128)(2,1)S(1)} all-gather(bf16[96,256]{1,0:T(8,128)(2,1)S(1)} %fusion.54), channel_id=3, replica_groups=mesh['leaf'=32,'row'=16] {'row'}, dimensions={0}, use_global_device_ids=true | all-gather | bytes 835584 | tf_op jit(solution)/shard_map/all_gather | solution.py:163
  145.8 6.6 %collective-permute-start.1 = (bf16[1536,256]{1,0:T(8,128)(2,1)S(1)}, bf16[1536,256]{1,0:T(8,128)(2,1)S(1)}, u32[]{:S(2)}, u32[]{:S(2)}) collective-permute-start(bf16[1536,256]{1,0:T(8,128)(2,1)S(1)} %bitcast.211), channel_id=1, source_target_pairs={{0,16},{16,0},{32,48},{48,32},{64,80},{80,64},{96,112},{112,96},{1... | collective-permute-start | bytes 2359304 | tf_op jit(solution)/shard_map/ppermute | solution.py:33
  152.4 0.6 fusion.30
  153.0 0.6 fusion.32
  153.6 0.9 fusion.73
  154.5 0.9 fusion.72
  155.4 37.5 %all_gather.29 = bf16[768,512]{1,0:T(8,128)(2,1)S(1)} all-gather(bf16[48,512]{1,0:T(8,128)(2,1)S(1)} %pad_maximum_fusion.4), channel_id=1, replica_groups=mesh['leaf'=32,'row'=16] {'row'}, dimensions={0}, use_global_device_ids=true | all-gather | bytes 835584 | tf_op jit(solution)/shard_map/all_gather | solution.py:170
  194.1 5.2 %collective-permute-start.2 = (bf16[384,256]{1,0:T(8,128)(2,1)S(1)}, bf16[384,256]{1,0:T(8,128)(2,1)S(1)}, u32[]{:S(2)}, u32[]{:S(2)}) collective-permute-start(bf16[384,256]{1,0:T(8,128)(2,1)S(1)} %slice.315), channel_id=1, source_target_pairs={{0,16},{16,0},{32,48},{48,32},{64,80},{80,64},{96,112},{112,96},{1... | collective-permute-start | bytes 589832 | tf_op jit(solution)/shard_map/ppermute | solution.py:33
  199.3 1.0 collective-permute-done.2
  200.6 20.6 %all_to_all.45 = bf16[16,16,384]{2,1,0:T(8,128)(2,1)S(1)} all-to-all(bf16[16,16,384]{2,1,0:T(8,128)(2,1)S(1)} %bitcast.219), channel_id=1, replica_groups=mesh['leaf'=32,'row'=16] {'row'}, dimensions={0} | all-to-all | bytes 393216 | tf_op jit(solution)/shard_map/all_to_all | solution.py:183
  221.3 0.7 broadcast_in_dim.102
  222.1 6.4 %all-to-all-start.1 = ((bf16[4,16,16,96]{3,2,1,0:T(8,128)(2,1)}), bf16[4,16,16,96]{3,2,1,0:T(8,128)(2,1)S(1)}, u32[]{:S(2)}, u32[]{:S(2)}) async-start(bf16[4,16,16,96]{3,2,1,0:T(8,128)(2,1)} %broadcast_in_dim.102), calls=%async_computation.1 | async-start | bytes 524288 | tf_op jit(solution)/shard_map/all_to_all | solution.py:43
  228.6 0.9 bitcast_select_fusion.1
  229.5 1.4 slice.209
  230.8 1.4 slice.211
  232.3 1.2 all-to-all-done.1
  233.5 0.7 copy.52
  234.2 1.1 reshape_reshape.9
  235.4 1.5 copy.53
  236.8 1.7 reshape.113
  238.5 0.5 convolution_convert_fusion
  239.0 2.3 fusion.34
  241.2 5.0 %all-to-all-start.2 = ((bf16[8,64,96]{2,1,0:T(8,128)(2,1)}), bf16[8,64,96]{2,1,0:T(8,128)(2,1)}, u32[]{:S(2)}, u32[]{:S(2)}) async-start(bf16[8,64,96]{2,1,0:T(8,128)(2,1)} %bitcast.43), calls=%async_computation.2 | async-start | bytes 262144 | tf_op jit(solution)/shard_map/all_to_all | solution.py:43
  246.2 1.2 slice.212
  247.4 1.2 slice.215
  248.6 1.3 slice.216
  249.9 1.1 slice.220
  251.1 0.8 reshape.122
  251.9 0.9 reduce_sum.66
  252.9 0.7 broadcast_in_dim.109
  253.5 4.8 %all-to-all-start.3 = ((bf16[8,64,96]{2,1,0:T(8,128)(2,1)}), bf16[8,64,96]{2,1,0:T(8,128)(2,1)S(1)}, u32[]{:S(2)}, u32[]{:S(2)}) async-start(bf16[8,64,96]{2,1,0:T(8,128)(2,1)} %broadcast_in_dim.109), calls=%async_computation.3 | async-start | bytes 262144 | tf_op jit(solution)/shard_map/all_to_all | solution.py:43
  258.3 2.0 fusion.7
  260.3 3.3 all-to-all-done.3
  264.6 2.0 fusion.33
  266.5 4.6 %all-to-all-start.4 = ((bf16[16,32,96]{2,1,0:T(8,128)(2,1)}), bf16[16,32,96]{2,1,0:T(8,128)(2,1)S(1)}, u32[]{:S(2)}, u32[]{:S(2)}) async-start(bf16[16,32,96]{2,1,0:T(8,128)(2,1)} %fusion.33), calls=%async_computation.4 | async-start | bytes 262144 | tf_op jit(solution)/shard_map/all_to_all | solution.py:43
  271.1 1.9 fusion.5
  273.1 4.2 %all-to-all-done.4 = bf16[16,32,96]{2,1,0:T(8,128)(2,1)S(1)} async-done(((bf16[16,32,96]{2,1,0:T(8,128)(2,1)}), bf16[16,32,96]{2,1,0:T(8,128)(2,1)S(1)}, u32[]{:S(2)}, u32[]{:S(2)}) %all-to-all-start.4) | async-done | bytes 98336 | tf_op jit(solution)/shard_map/all_to_all | solution.py:43
  277.3 0.7 broadcast_in_dim.112
  277.9 4.0 %all-to-all-start.5 = ((bf16[16,32,96]{2,1,0:T(8,128)(2,1)}), bf16[16,32,96]{2,1,0:T(8,128)(2,1)S(1)}, u32[]{:S(2)}, u32[]{:S(2)}) async-start(bf16[16,32,96]{2,1,0:T(8,128)(2,1)} %broadcast_in_dim.112), calls=%async_computation.5 | async-start | bytes 262144 | tf_op jit(solution)/shard_map/all_to_all | solution.py:43
  281.9 1.7 convolution_add_fusion.1
  283.7 4.4 %all-to-all-done.5 = bf16[16,32,96]{2,1,0:T(8,128)(2,1)S(1)} async-done(((bf16[16,32,96]{2,1,0:T(8,128)(2,1)}), bf16[16,32,96]{2,1,0:T(8,128)(2,1)S(1)}, u32[]{:S(2)}, u32[]{:S(2)}) %all-to-all-start.5) | async-done | bytes 98336 | tf_op jit(solution)/shard_map/all_to_all | solution.py:43
  289.1 1.3 fusion.14
  290.4 13.0 %all_to_all.46 = bf16[32,16,96]{2,1,0:T(8,128)(2,1)S(1)} all-to-all(bf16[32,16,96]{2,1,0:T(8,128)(2,1)S(1)} %bitcast.220), channel_id=1, replica_groups={{0,16,32,48,64,80,96,112,128,144,160,176,192,208,224,240,256,272,288,30..., dimensions={0} | all-to-all | bytes 196608 | tf_op jit(solution)/shard_map/all_to_all | solution.py:43
  303.4 0.7 broadcast_in_dim.115
  304.1 3.9 %all-to-all-start.7 = ((bf16[32,16,96]{2,1,0:T(8,128)(2,1)}), bf16[32,16,96]{2,1,0:T(8,128)(2,1)S(1)}, u32[]{:S(2)}, u32[]{:S(2)}) async-start(bf16[32,16,96]{2,1,0:T(8,128)(2,1)} %broadcast_in_dim.115), calls=%async_computation.7 | async-start | bytes 262144 | tf_op jit(solution)/shard_map/all_to_all | solution.py:43
  308.0 0.4 convolution_bitcast_fusion.1
  308.4 1.1 slice.221
  310.2 5.6 %all-to-all-done.7 = bf16[32,16,96]{2,1,0:T(8,128)(2,1)S(1)} async-done(((bf16[32,16,96]{2,1,0:T(8,128)(2,1)}), bf16[32,16,96]{2,1,0:T(8,128)(2,1)S(1)}, u32[]{:S(2)}, u32[]{:S(2)}) %all-to-all-start.7) | async-done | bytes 98336 | tf_op jit(solution)/shard_map/all_to_all | solution.py:43
  315.8 1.1 copy.60
  316.9 0.3 reshape_reshape.11
  318.6 0.8 reshape.140
  319.4 6.0 %all-to-all-start.8 = ((bf16[16,2,720]{2,1,0:T(2,128)(2,1)}), bf16[16,2,720]{2,1,0:T(2,128)(2,1)S(1)}, u32[]{:S(2)}, u32[]{:S(2)}) async-start(bf16[16,2,720]{2,1,0:T(2,128)(2,1)} %reshape.140), calls=%async_computation.8 | async-start | bytes 98304 | tf_op jit(solution)/shard_map/all_to_all | solution.py:235
  325.5 11.5 %all-to-all-done.8 = bf16[16,2,720]{2,1,0:T(2,128)(2,1)S(1)} async-done(((bf16[16,2,720]{2,1,0:T(2,128)(2,1)}), bf16[16,2,720]{2,1,0:T(2,128)(2,1)S(1)}, u32[]{:S(2)}, u32[]{:S(2)}) %all-to-all-start.8) | async-done | bytes 46112 | tf_op jit(solution)/shard_map/all_to_all | solution.py:235
  337.4 1.1 copy.69
  (104 shorter events, 7.3 us)
Async XLA Ops:
  6.5 4.9 %copy-start.9 = (bf16[1,1,189,512]{3,2,1,0:T(8,128)(2,1)S(1)}, bf16[1,1,189,512]{3,2,1,0:T(8,128)(2,1)}, u32[]{:S(2)}) copy-start(bf16[1,1,189,512]{3,2,1,0:T(8,128)(2,1)} %param.9) | copy-start | bytes 580612
  6.5 89.2 %all-gather.6.cloned.1.call-start = ((), (), s32[]{:S(2)}) async-start(), calls=%async_computation.9 | async-start | bytes 5013504 | tf_op jit(solution)/shard_map/all_gather | solution.py:127
  8.3 213.0 %all-gather.8.cloned.1.call-start = ((), (), s32[]{:S(2)}) async-start(), calls=%async_computation.10 | async-start | bytes 8146944 | tf_op jit(solution)/shard_map/all_gather | solution.py:138
  8.3 41.8 %copy-start.12 = (s32[1,1,15]{2,1,0:T(1,128)S(1)}, s32[1,1,15]{2,1,0:T(1,128)}, u32[]{:S(2)}) copy-start(s32[1,1,15]{2,1,0:T(1,128)} %param.12) | copy-start | bytes 184
  8.4 41.8 %copy-start.14 = (s32[384]{0:T(512)S(1)}, s32[384]{0:T(512)}, u32[]{:S(2)}) copy-start(s32[384]{0:T(512)} %constant.31.clone) | copy-start | bytes 4612
  8.4 41.9 %copy-start.13 = (s32[480]{0:T(512)S(1)}, s32[480]{0:T(512)}, u32[]{:S(2)}) copy-start(s32[480]{0:T(512)} %constant.30.clone) | copy-start | bytes 5764
  8.4 42.0 %copy-start.15 = (s32[93]{0:T(128)S(1)}, s32[93]{0:T(128)}, u32[]{:S(2)}) copy-start(s32[93]{0:T(128)} %constant.27.clone) | copy-start | bytes 1120
  8.4 42.0 %copy-start.16 = (s32[93]{0:T(128)S(1)}, s32[93]{0:T(128)}, u32[]{:S(2)}) copy-start(s32[93]{0:T(128)} %constant.28.clone) | copy-start | bytes 1120
  8.4 42.0 %copy-start.17 = (s32[93]{0:T(128)S(1)}, s32[93]{0:T(128)}, u32[]{:S(2)}) copy-start(s32[93]{0:T(128)} %constant.29.clone) | copy-start | bytes 1120
  85.3 15.6 %copy-start.3 = (bf16[1536,256]{1,0:T(8,128)(2,1)}, bf16[1536,256]{1,0:T(8,128)(2,1)S(1)}, u32[]{:S(2)}) copy-start(bf16[1536,256]{1,0:T(8,128)(2,1)S(1)} %get-tuple-element.27) | copy-start | bytes 2359300
  85.3 15.6 %copy-start.5 = (bf16[1536,256]{1,0:T(8,128)(2,1)}, bf16[1536,256]{1,0:T(8,128)(2,1)S(1)}, u32[]{:S(2)}) copy-start(bf16[1536,256]{1,0:T(8,128)(2,1)S(1)} %get-tuple-element.28) | copy-start | bytes 2359300
  95.7 5.2 %copy-start = (bf16[1,1,96,12384]{3,2,1,0:T(8,128)(2,1)S(1)}, bf16[1,1,96,12384]{3,2,1,0:T(8,128)(2,1)}, u32[]{:S(2)}) copy-start(bf16[1,1,96,12384]{3,2,1,0:T(8,128)(2,1)} %off_ref.1) | copy-start | bytes 7133188
  101.5 9.2 %collective-permute-start = (bf16[96,256]{1,0:T(8,128)(2,1)S(1)}, bf16[96,256]{1,0:T(8,128)(2,1)S(1)}, u32[]{:S(2)}, u32[]{:S(2)}) collective-permute-start(bf16[96,256]{1,0:T(8,128)(2,1)S(1)} %slice.316), channel_id=1, source_target_pairs={{0,16},{16,0},{32,48},{48,32},{64,80},{80,64},{96,112},{112,96},{1... | collective-permute-start | bytes 147464 | tf_op jit(solution)/shard_map/ppermute | solution.py:33
  145.8 7.8 %copy-start.1 = (bf16[1,1,189,1536]{3,2,1,0:T(8,128)(2,1)S(1)}, bf16[1,1,189,1536]{3,2,1,0:T(8,128)(2,1)}, u32[]{:S(2)}) copy-start(bf16[1,1,189,1536]{3,2,1,0:T(8,128)(2,1)} %inv_ref.1) | copy-start | bytes 1741828
  145.8 8.7 %collective-permute-start.1 = (bf16[1536,256]{1,0:T(8,128)(2,1)S(1)}, bf16[1536,256]{1,0:T(8,128)(2,1)S(1)}, u32[]{:S(2)}, u32[]{:S(2)}) collective-permute-start(bf16[1536,256]{1,0:T(8,128)(2,1)S(1)} %bitcast.211), channel_id=1, source_target_pairs={{0,16},{16,0},{32,48},{48,32},{64,80},{80,64},{96,112},{112,96},{1... | collective-permute-start | bytes 2359304 | tf_op jit(solution)/shard_map/ppermute | solution.py:33
  194.1 6.3 %collective-permute-start.2 = (bf16[384,256]{1,0:T(8,128)(2,1)S(1)}, bf16[384,256]{1,0:T(8,128)(2,1)S(1)}, u32[]{:S(2)}, u32[]{:S(2)}) collective-permute-start(bf16[384,256]{1,0:T(8,128)(2,1)S(1)} %slice.315), channel_id=1, source_target_pairs={{0,16},{16,0},{32,48},{48,32},{64,80},{80,64},{96,112},{112,96},{1... | collective-permute-start | bytes 589832 | tf_op jit(solution)/shard_map/ppermute | solution.py:33
  222.1 11.4 %all-to-all-start.1 = ((bf16[4,16,16,96]{3,2,1,0:T(8,128)(2,1)}), bf16[4,16,16,96]{3,2,1,0:T(8,128)(2,1)S(1)}, u32[]{:S(2)}, u32[]{:S(2)}) async-start(bf16[4,16,16,96]{3,2,1,0:T(8,128)(2,1)} %broadcast_in_dim.102), calls=%async_computation.1 | async-start | bytes 524288 | tf_op jit(solution)/shard_map/all_to_all | solution.py:43
  239.0 2.3 copy-start.7
  241.2 10.7 %all-to-all-start.2 = ((bf16[8,64,96]{2,1,0:T(8,128)(2,1)}), bf16[8,64,96]{2,1,0:T(8,128)(2,1)}, u32[]{:S(2)}, u32[]{:S(2)}) async-start(bf16[8,64,96]{2,1,0:T(8,128)(2,1)} %bitcast.43), calls=%async_computation.2 | async-start | bytes 262144 | tf_op jit(solution)/shard_map/all_to_all | solution.py:43
  253.5 10.0 %all-to-all-start.3 = ((bf16[8,64,96]{2,1,0:T(8,128)(2,1)}), bf16[8,64,96]{2,1,0:T(8,128)(2,1)S(1)}, u32[]{:S(2)}, u32[]{:S(2)}) async-start(bf16[8,64,96]{2,1,0:T(8,128)(2,1)} %broadcast_in_dim.109), calls=%async_computation.3 | async-start | bytes 262144 | tf_op jit(solution)/shard_map/all_to_all | solution.py:43
  264.3 6.9 %copy-start.8 = (bf16[32,384]{1,0:T(8,128)(2,1)S(1)}, bf16[32,384]{1,0:T(8,128)(2,1)}, u32[]{:S(2)}) copy-start(bf16[32,384]{1,0:T(8,128)(2,1)} %copy-done.7) | copy-start | bytes 73732
  266.5 10.7 %all-to-all-start.4 = ((bf16[16,32,96]{2,1,0:T(8,128)(2,1)}), bf16[16,32,96]{2,1,0:T(8,128)(2,1)S(1)}, u32[]{:S(2)}, u32[]{:S(2)}) async-start(bf16[16,32,96]{2,1,0:T(8,128)(2,1)} %fusion.33), calls=%async_computation.4 | async-start | bytes 262144 | tf_op jit(solution)/shard_map/all_to_all | solution.py:43
  273.1 15.7 %copy-start.2 = (bf16[96,1536]{1,0:T(8,128)(2,1)S(1)}, bf16[96,1536]{1,0:T(8,128)(2,1)}, u32[]{:S(2)}) copy-start(bf16[96,1536]{1,0:T(8,128)(2,1)} %reshape.122) | copy-start | bytes 884740
  277.9 10.2 %all-to-all-start.5 = ((bf16[16,32,96]{2,1,0:T(8,128)(2,1)}), bf16[16,32,96]{2,1,0:T(8,128)(2,1)S(1)}, u32[]{:S(2)}, u32[]{:S(2)}) async-start(bf16[16,32,96]{2,1,0:T(8,128)(2,1)} %broadcast_in_dim.112), calls=%async_computation.5 | async-start | bytes 262144 | tf_op jit(solution)/shard_map/all_to_all | solution.py:43
  283.6 24.4 %copy-start.4 = (bf16[1536,256]{1,0:T(8,128)(2,1)S(1)}, bf16[1536,256]{1,0:T(8,128)(2,1)}, u32[]{:S(2)}) copy-start(bf16[1536,256]{1,0:T(8,128)(2,1)} %copy-done.3) | copy-start | bytes 2359300
  288.8 19.2 %copy-start.6 = (bf16[1536,256]{1,0:T(8,128)(2,1)S(1)}, bf16[1536,256]{1,0:T(8,128)(2,1)}, u32[]{:S(2)}) copy-start(bf16[1536,256]{1,0:T(8,128)(2,1)} %copy-done.5) | copy-start | bytes 2359300
  304.1 11.7 %all-to-all-start.7 = ((bf16[32,16,96]{2,1,0:T(8,128)(2,1)}), bf16[32,16,96]{2,1,0:T(8,128)(2,1)S(1)}, u32[]{:S(2)}, u32[]{:S(2)}) async-start(bf16[32,16,96]{2,1,0:T(8,128)(2,1)} %broadcast_in_dim.115), calls=%async_computation.7 | async-start | bytes 262144 | tf_op jit(solution)/shard_map/all_to_all | solution.py:43
  316.9 8.5 %copy-start.10 = (f32[48,256]{1,0:T(8,128)S(1)}, f32[48,256]{1,0:T(8,128)}, u32[]{:S(2)}) copy-start(f32[48,256]{1,0:T(8,128)} %get-tuple-element.54) | copy-start | bytes 147460
  316.9 8.5 %copy-start.11 = (f32[48,256]{1,0:T(8,128)S(1)}, f32[48,256]{1,0:T(8,128)}, u32[]{:S(2)}) copy-start(f32[48,256]{1,0:T(8,128)} %get-tuple-element.52) | copy-start | bytes 147460
  319.4 17.6 %all-to-all-start.8 = ((bf16[16,2,720]{2,1,0:T(2,128)(2,1)}), bf16[16,2,720]{2,1,0:T(2,128)(2,1)S(1)}, u32[]{:S(2)}, u32[]{:S(2)}) async-start(bf16[16,2,720]{2,1,0:T(2,128)(2,1)} %reshape.140), calls=%async_computation.8 | async-start | bytes 98304 | tf_op jit(solution)/shard_map/all_to_all | solution.py:235
Sparse Core Ops, SparseCore 0:
  9.4 86.2 all-gather.5
  97.8 114.6 all-gather.7

commit v10 on v8

--- a/solution.py
+++ b/solution.py
@@ -47,21 +47,18 @@
     return leaf_scatter(jnp.broadcast_to(block, (size, *block.shape)))
 
 
-def pack_upper(off_diag, inv_diag, live, pairs, d_start):
-    strip, width = off_diag.shape[2], inv_diag.shape[3]
-    d_rows = inv_diag.shape[2] - d_start
+def pack_upper(off_diag, inverse, live, pairs):
+    strip = off_diag.shape[2]
+    d_rows, width = inverse.shape
     first = min(column_start(m, l, width) for m, l in pairs) // 128 * 128
     span = off_diag.shape[3] - first
     total = sum(width >> l for _, l in pairs)
 
-    def body(live_ref, off_ref, inv_ref, out_ref, p_ref, d_ref, sems):
+    def body(live_ref, off_ref, inv_ref, out_ref, p_ref, sems):
         p_copy = pltpu.make_async_copy(off_ref.at[0, 0, :, pl.ds(first, span)], p_ref, sems.at[0])
-        d_copy = pltpu.make_async_copy(inv_ref.at[0, 0, pl.ds(d_start, d_rows), :], d_ref, sems.at[1])
         p_copy.start()
-        d_copy.start()
-        d_copy.wait()
         out_ref[strip:, :] = jnp.zeros((out_ref.shape[0] - strip, total), BF16)
-        out_ref[strip : strip + d_rows, :width] = d_ref[...]
+        out_ref[strip : strip + d_rows, :width] = inv_ref[...]
         p_copy.wait()
         at = 0
         for m, l in pairs:
@@ -79,16 +76,15 @@
         in_specs=[
             pl.BlockSpec(memory_space=pltpu.SMEM),
             pl.BlockSpec(memory_space=pl.ANY),
-            pl.BlockSpec(memory_space=pl.ANY),
+            pl.BlockSpec(memory_space=pltpu.VMEM),
         ],
         out_specs=pl.BlockSpec(memory_space=pltpu.VMEM),
         scratch_shapes=[
             pltpu.VMEM((strip, span), BF16),
-            pltpu.VMEM((d_rows, width), BF16),
-            pltpu.SemaphoreType.DMA((2,)),
+            pltpu.SemaphoreType.DMA((1,)),
         ],
         name="pack_upper",
-    )(live, off_diag, inv_diag)
+    )(live, off_diag, inverse)
 
 
 def shards(rhs, inv_diag, off_diag, pair_mask):
@@ -133,8 +129,19 @@
         ((m, l) for l in range(2, levels) for m in range(l + 1, levels + 1)), key=lambda p: (p[1], p[0])
     )
     d_first = {m: strip + starts[m] - starts[2] for m in range(2, levels + 1)}
-    packed = pack_upper(off_diag, inv_diag, live, upper_pairs, starts[2])
-    packed, z0_left = lax.optimization_barrier((packed, z0_left))
+    turned_levels = (2, levels)
+    tail, live_up, z0_right = lax.optimization_barrier((d_all[starts[2] :], live, z0_right))
+
+    def in_order(m):
+        rows = tail[starts[m] - starts[2] : starts[m] - starts[2] + heights[m]]
+        if m not in turned_levels:
+            return rows
+        rows = rows.reshape(heights[m], 2**m, rows_n, heights[m])
+        return rows.transpose(0, 2, 1, 3).reshape(heights[m], width)
+
+    inverse_up = jnp.concatenate([in_order(m) for m in range(2, levels + 1)], axis=0)
+    packed = pack_upper(off_diag, inverse_up, live_up, upper_pairs)
+    packed, z0_right = lax.optimization_barrier((packed, z0_right))
     everyone = lax.all_gather(packed, "row", axis=0, tiled=False)
 
     tall = strip * levels
@@ -199,6 +206,8 @@
         return block[:, :strip, p_first[m, l] : p_first[m, l] + (width >> l)]
 
     def natural(z, m):
+        if m in turned_levels:
+            return z.transpose(1, 0, 2).reshape(2 * sub, width)
         z = z.reshape(rows_n, 2 * sub, 2**m, heights[m])
         return z.transpose(1, 2, 0, 3).reshape(2 * sub, width)
 

time: 342 us -> 339 us (level)
  waiting for transfers between devices: 49 us -> 41.2 us
    all_gather x1, waiting for transfers between devices: 12.4 us -> 5.45 us  [shards(): d_full0 = lax.all_gather(d_own0, 'row', axis=0, tiled=True)]
    all_gather x1, blocking collectives: 38.7 us -> 33.7 us  [shards(): z0_left = lax.all_gather(b0[:, :half], 'row', axis=0, tiled=True)]
    all_gather x1, blocking collectives: 33.3 us -> 37.7 us  [shards(): z0_right = lax.all_gather(b0[:, half:], 'row', axis=0, tiled=True)]
  transfers between devices with their start and end apart: 12 -> 12, of which waited for: 10 -> 10; matrix products, arithmetic and copies ran while one was open for 7% -> 9% of each run, Pallas kernels for 1% -> 1%
where the time goes in v10:
time: 339 us; the launch traced here: 338 us
  blocking collectives  175 us (52%)
  starting transfers between devices  56.6 us (17%)
  waiting for transfers between devices  41.2 us (12%)
  matrix products  24.1 us (7%)
  local copies, waits for them, and re-layouts  20 us (6%)
  between operations  14.1 us (4%)
  other arithmetic  3.39 us (1%)
    all_gather x1, blocking collectives, shards(): yb1 = lax.all_gather(yb1, 'row', axis=0, tiled=True)  38 us
    all_gather x1, blocking collectives, shards(): z0_right = lax.all_gather(b0[:, half:], 'row', axis=0, tiled=True)  37.7 us
    all_gather x1, blocking collectives, shards(): z1 = lax.all_gather(z1, 'row', axis=0, tiled=False)  33.8 us
    all_gather x1, blocking collectives, shards(): z0_left = lax.all_gather(b0[:, :half], 'row', axis=0, tiled=True)  33.7 us
    all_to_all x6, starting transfers between devices, leaf_scatter(): lax.all_to_all(pieces, 'leaf', 0, 0, tiled=True, axis_index_groups=leaf_g...  29.1 us
    all_to_all x6, waiting for transfers between devices, leaf_scatter(): lax.all_to_all(pieces, 'leaf', 0, 0, tiled=True, axis_index_groups=leaf_g...  22.7 us
    ppermute x3, starting transfers between devices, core_swap(): return lax.ppermute(block, 'leaf', [(i, i ^ 1) for i in range(count)])  21.6 us
    all_to_all x1, blocking collectives, shards(): turned = lax.all_to_all(turned, 'row', 0, 0, tiled=True)  18.7 us
  transfers between devices with their start and end apart: 12, of which 10 were waited for; matrix products, arithmetic and copies ran while one was open for 9% of the time, Pallas kernels for 1%

profile of v10, /device:TPU:1, one launch (start us, length us, event | category | flops | bytes accessed | tf_op | source)
XLA Modules:
  0.0 337.8 jit_solution(4875632754971433544)
XLA Ops:
  6.5 1.7 slice.193
  8.3 0.9 slice_bitcast_fusion.2
  9.2 37.7 %all_gather.25 = bf16[1536,256]{1,0:T(8,128)(2,1)S(1)} all-gather(bf16[96,256]{1,0:T(8,128)(2,1)S(1)} %get-tuple-element.44), channel_id=1, replica_groups=mesh['leaf'=32,'row'=16] {'row'}, dimensions={0}, use_global_device_ids=true | all-gather | bytes 835584 | tf_op jit(solution)/shard_map/all_gather | solution.py:126
  46.9 0.9 slice_bitcast_fusion
  47.9 0.6 reshape.127
  48.7 0.5 reshape.128
  49.2 0.7 reshape.129
  50.1 0.5 reshape.130
  50.7 0.7 pad_maximum_fusion.4.inv_ref
  51.3 3.1 pack_upper.1
  55.2 33.7 %all_gather.24 = bf16[1536,256]{1,0:T(8,128)(2,1)S(1)} all-gather(bf16[96,256]{1,0:T(8,128)(2,1)S(1)} %get-tuple-element.43), channel_id=1, replica_groups=mesh['leaf'=32,'row'=16] {'row'}, dimensions={0}, use_global_device_ids=true | all-gather | bytes 835584 | tf_op jit(solution)/shard_map/all_gather | solution.py:125
  89.1 5.5 %all-gather.6.cloned.1.call-done = bf16[1,1,1536,1536]{3,2,1,0:T(8,128)(2,1)} async-done(((bf16[1,1,96,1536]{3,2,1,0:T(8,128)(2,1)}), bf16[1,1,1536,1536]{3,2,1,0:T(8,128)(2,1)}) %all-gather.6.cloned.1.call-update) | async-done | bytes 4718608 | tf_op jit(solution)/shard_map/all_gather | solution.py:123
  94.6 5.1 %fusion.2 = bf16[512,1536]{1,0:T(8,128)(2,1)S(1)} fusion(bf16[1,1,1536,1536]{3,2,1,0:T(8,128)(2,1)} %all-gather.6.cloned.1.call-done, bf16[1536,256]{1,0:T(8,128)(2,1)S(1)} %get-tuple-element.34, bf16[1536,256]{1,0:T(8,128)(2,1)S(1)} %get-tuple-element.33), kind=kOutput, calls=%fused_computation.2 | convolution fusion | flops 2419851264 | bytes 7864320 | tf_op jit(solution)/shard_map/dot_general | solution.py:24
  99.7 0.6 fusion.31
  100.4 8.3 %collective-permute-start = (bf16[96,256]{1,0:T(8,128)(2,1)S(1)}, bf16[96,256]{1,0:T(8,128)(2,1)S(1)}, u32[]{:S(2)}, u32[]{:S(2)}) collective-permute-start(bf16[96,256]{1,0:T(8,128)(2,1)S(1)} %slice.351), channel_id=1, source_target_pairs={{0,16},{16,0},{32,48},{48,32},{64,80},{80,64},{96,112},{112,96},{1... | collective-permute-start | bytes 147464 | tf_op jit(solution)/shard_map/ppermute | solution.py:33
  108.7 0.6 fusion.33
  109.3 0.6 fusion.35
  110.0 33.8 %all-gather.1 = bf16[1536,256]{1,0:T(8,128)(2,1)S(1)} all-gather(bf16[96,256]{1,0:T(8,128)(2,1)S(1)} %fusion.65), channel_id=3, replica_groups=mesh['leaf'=32,'row'=16] {'row'}, dimensions={0}, use_global_device_ids=true | all-gather | bytes 835584 | tf_op jit(solution)/shard_map/all_gather | solution.py:170
  143.9 6.2 %collective-permute-start.1 = (bf16[1536,256]{1,0:T(8,128)(2,1)S(1)}, bf16[1536,256]{1,0:T(8,128)(2,1)S(1)}, u32[]{:S(2)}, u32[]{:S(2)}) collective-permute-start(bf16[1536,256]{1,0:T(8,128)(2,1)S(1)} %bitcast.210), channel_id=1, source_target_pairs={{0,16},{16,0},{32,48},{48,32},{64,80},{80,64},{96,112},{112,96},{1... | collective-permute-start | bytes 2359304 | tf_op jit(solution)/shard_map/ppermute | solution.py:33
  150.1 0.6 fusion.37
  150.7 0.6 fusion.39
  151.6 0.4 collective-permute-done.1
  151.9 0.9 fusion.83
  152.8 38.0 %all_gather.29 = bf16[768,512]{1,0:T(8,128)(2,1)S(1)} all-gather(bf16[48,512]{1,0:T(8,128)(2,1)S(1)} %pad_maximum_fusion.5), channel_id=1, replica_groups=mesh['leaf'=32,'row'=16] {'row'}, dimensions={0}, use_global_device_ids=true | all-gather | bytes 835584 | tf_op jit(solution)/shard_map/all_gather | solution.py:177
  191.6 0.3 fusion.29
  192.0 7.1 %collective-permute-start.2 = (bf16[384,256]{1,0:T(8,128)(2,1)S(1)}, bf16[384,256]{1,0:T(8,128)(2,1)S(1)}, u32[]{:S(2)}, u32[]{:S(2)}) collective-permute-start(bf16[384,256]{1,0:T(8,128)(2,1)S(1)} %slice.350), channel_id=1, source_target_pairs={{0,16},{16,0},{32,48},{48,32},{64,80},{80,64},{96,112},{112,96},{1... | collective-permute-start | bytes 589832 | tf_op jit(solution)/shard_map/ppermute | solution.py:33
  199.1 1.0 collective-permute-done.2
  200.4 18.7 %all_to_all.45 = bf16[16,16,384]{2,1,0:T(8,128)(2,1)S(1)} all-to-all(bf16[16,16,384]{2,1,0:T(8,128)(2,1)S(1)} %bitcast.218), channel_id=1, replica_groups=mesh['leaf'=32,'row'=16] {'row'}, dimensions={0} | all-to-all | bytes 393216 | tf_op jit(solution)/shard_map/all_to_all | solution.py:190
  219.3 0.7 broadcast_in_dim.102
  220.0 7.5 %all-to-all-start.1 = ((bf16[4,16,16,96]{3,2,1,0:T(8,128)(2,1)}), bf16[4,16,16,96]{3,2,1,0:T(8,128)(2,1)S(1)}, u32[]{:S(2)}, u32[]{:S(2)}) async-start(bf16[4,16,16,96]{3,2,1,0:T(8,128)(2,1)} %broadcast_in_dim.102), calls=%async_computation.1 | async-start | bytes 524288 | tf_op jit(solution)/shard_map/all_to_all | solution.py:43
  227.7 0.8 bitcast_select_fusion.1
  228.5 1.4 slice.231
  229.9 2.6 all-to-all-done.1
  232.8 0.5 convolution_convert_fusion
  233.2 2.6 fusion.41
  235.9 5.2 %all-to-all-start.2 = ((bf16[8,64,96]{2,1,0:T(8,128)(2,1)}), bf16[8,64,96]{2,1,0:T(8,128)(2,1)}, u32[]{:S(2)}, u32[]{:S(2)}) async-start(bf16[8,64,96]{2,1,0:T(8,128)(2,1)} %bitcast.47), calls=%async_computation.2 | async-start | bytes 262144 | tf_op jit(solution)/shard_map/all_to_all | solution.py:43
  241.1 1.2 slice.234
  242.3 1.3 slice.238
  243.8 2.6 all-to-all-done.2
  246.4 0.9 reduce_sum.66
  247.3 0.7 broadcast_in_dim.109
  248.0 4.1 %all-to-all-start.3 = ((bf16[8,64,96]{2,1,0:T(8,128)(2,1)}), bf16[8,64,96]{2,1,0:T(8,128)(2,1)S(1)}, u32[]{:S(2)}, u32[]{:S(2)}) async-start(bf16[8,64,96]{2,1,0:T(8,128)(2,1)} %broadcast_in_dim.109), calls=%async_computation.3 | async-start | bytes 262144 | tf_op jit(solution)/shard_map/all_to_all | solution.py:43
  252.2 1.9 fusion.7
  254.1 3.3 all-to-all-done.3
  258.4 2.2 fusion.40
  260.6 4.4 %all-to-all-start.4 = ((bf16[16,32,96]{2,1,0:T(8,128)(2,1)}), bf16[16,32,96]{2,1,0:T(8,128)(2,1)S(1)}, u32[]{:S(2)}, u32[]{:S(2)}) async-start(bf16[16,32,96]{2,1,0:T(8,128)(2,1)} %fusion.40), calls=%async_computation.4 | async-start | bytes 262144 | tf_op jit(solution)/shard_map/all_to_all | solution.py:43
  265.0 1.9 fusion.5
  266.9 4.2 %all-to-all-done.4 = bf16[16,32,96]{2,1,0:T(8,128)(2,1)S(1)} async-done(((bf16[16,32,96]{2,1,0:T(8,128)(2,1)}), bf16[16,32,96]{2,1,0:T(8,128)(2,1)S(1)}, u32[]{:S(2)}, u32[]{:S(2)}) %all-to-all-start.4) | async-done | bytes 98336 | tf_op jit(solution)/shard_map/all_to_all | solution.py:43
  271.2 0.7 broadcast_in_dim.112
  271.8 4.0 %all-to-all-start.5 = ((bf16[16,32,96]{2,1,0:T(8,128)(2,1)}), bf16[16,32,96]{2,1,0:T(8,128)(2,1)S(1)}, u32[]{:S(2)}, u32[]{:S(2)}) async-start(bf16[16,32,96]{2,1,0:T(8,128)(2,1)} %broadcast_in_dim.112), calls=%async_computation.5 | async-start | bytes 262144 | tf_op jit(solution)/shard_map/all_to_all | solution.py:43
  275.8 1.7 convolution_add_fusion.1
  277.5 4.5 %all-to-all-done.5 = bf16[16,32,96]{2,1,0:T(8,128)(2,1)S(1)} async-done(((bf16[16,32,96]{2,1,0:T(8,128)(2,1)}), bf16[16,32,96]{2,1,0:T(8,128)(2,1)S(1)}, u32[]{:S(2)}, u32[]{:S(2)}) %all-to-all-start.5) | async-done | bytes 98336 | tf_op jit(solution)/shard_map/all_to_all | solution.py:43
  282.0 0.3 copy.81
  283.0 1.4 fusion.21
  284.4 13.5 %all_to_all.46 = bf16[32,16,96]{2,1,0:T(8,128)(2,1)S(1)} all-to-all(bf16[32,16,96]{2,1,0:T(8,128)(2,1)S(1)} %bitcast.219), channel_id=1, replica_groups={{0,16,32,48,64,80,96,112,128,144,160,176,192,208,224,240,256,272,288,30..., dimensions={0} | all-to-all | bytes 196608 | tf_op jit(solution)/shard_map/all_to_all | solution.py:43
  297.9 0.7 broadcast_in_dim.115
  298.6 3.9 %all-to-all-start.7 = ((bf16[32,16,96]{2,1,0:T(8,128)(2,1)}), bf16[32,16,96]{2,1,0:T(8,128)(2,1)S(1)}, u32[]{:S(2)}, u32[]{:S(2)}) async-start(bf16[32,16,96]{2,1,0:T(8,128)(2,1)} %broadcast_in_dim.115), calls=%async_computation.7 | async-start | bytes 262144 | tf_op jit(solution)/shard_map/all_to_all | solution.py:43
  302.5 0.4 convolution_bitcast_fusion
  302.9 1.1 slice.243
  304.7 5.6 %all-to-all-done.7 = bf16[32,16,96]{2,1,0:T(8,128)(2,1)S(1)} async-done(((bf16[32,16,96]{2,1,0:T(8,128)(2,1)}), bf16[32,16,96]{2,1,0:T(8,128)(2,1)S(1)}, u32[]{:S(2)}, u32[]{:S(2)}) %all-to-all-start.7) | async-done | bytes 98336 | tf_op jit(solution)/shard_map/all_to_all | solution.py:43
  311.1 0.8 reshape.165
  311.9 5.9 %all-to-all-start.8 = ((bf16[16,2,720]{2,1,0:T(2,128)(2,1)}), bf16[16,2,720]{2,1,0:T(2,128)(2,1)S(1)}, u32[]{:S(2)}, u32[]{:S(2)}) async-start(bf16[16,2,720]{2,1,0:T(2,128)(2,1)} %reshape.165), calls=%async_computation.8 | async-start | bytes 98304 | tf_op jit(solution)/shard_map/all_to_all | solution.py:241
  317.9 11.5 %all-to-all-done.8 = bf16[16,2,720]{2,1,0:T(2,128)(2,1)S(1)} async-done(((bf16[16,2,720]{2,1,0:T(2,128)(2,1)}), bf16[16,2,720]{2,1,0:T(2,128)(2,1)S(1)}, u32[]{:S(2)}, u32[]{:S(2)}) %all-to-all-start.8) | async-done | bytes 46112 | tf_op jit(solution)/shard_map/all_to_all | solution.py:241
  329.8 1.1 copy.92
  (99 shorter events, 7.1 us)
Async XLA Ops:
  6.5 88.0 %all-gather.6.cloned.1.call-start = ((), (), s32[]{:S(2)}) async-start(), calls=%async_computation.9 | async-start | bytes 5013504 | tf_op jit(solution)/shard_map/all_gather | solution.py:123
  8.3 211.0 %all-gather.8.cloned.1.call-start = ((), (), s32[]{:S(2)}) async-start(), calls=%async_computation.10 | async-start | bytes 8146944 | tf_op jit(solution)/shard_map/all_gather | solution.py:145
  49.9 4.6 %copy-start.7 = (s32[1,1,15]{2,1,0:T(1,128)S(1)}, s32[1,1,15]{2,1,0:T(1,128)}, u32[]{:S(2)}) copy-start(s32[1,1,15]{2,1,0:T(1,128)} %param.12) | copy-start | bytes 184
  49.9 4.6 %copy-start.9 = (s32[384]{0:T(512)S(1)}, s32[384]{0:T(512)}, u32[]{:S(2)}) copy-start(s32[384]{0:T(512)} %constant.31.clone) | copy-start | bytes 4612
  49.9 4.7 %copy-start.8 = (s32[480]{0:T(512)S(1)}, s32[480]{0:T(512)}, u32[]{:S(2)}) copy-start(s32[480]{0:T(512)} %constant.30.clone) | copy-start | bytes 5764
  50.0 4.8 %copy-start.10 = (s32[93]{0:T(128)S(1)}, s32[93]{0:T(128)}, u32[]{:S(2)}) copy-start(s32[93]{0:T(128)} %constant.27.clone) | copy-start | bytes 1120
  50.0 4.8 %copy-start.11 = (s32[93]{0:T(128)S(1)}, s32[93]{0:T(128)}, u32[]{:S(2)}) copy-start(s32[93]{0:T(128)} %constant.28.clone) | copy-start | bytes 1120
  50.0 4.8 %copy-start.12 = (s32[93]{0:T(128)S(1)}, s32[93]{0:T(128)}, u32[]{:S(2)}) copy-start(s32[93]{0:T(128)} %constant.29.clone) | copy-start | bytes 1120
  50.0 4.9 %copy-start.5 = (bf16[1,1,189,512]{3,2,1,0:T(8,128)(2,1)S(1)}, bf16[1,1,189,512]{3,2,1,0:T(8,128)(2,1)}, u32[]{:S(2)}) copy-start(bf16[1,1,189,512]{3,2,1,0:T(8,128)(2,1)} %param.9) | copy-start | bytes 580612
  89.1 10.6 %copy-start.2 = (bf16[1536,256]{1,0:T(8,128)(2,1)}, bf16[1536,256]{1,0:T(8,128)(2,1)S(1)}, u32[]{:S(2)}) copy-start(bf16[1536,256]{1,0:T(8,128)(2,1)S(1)} %get-tuple-element.34) | copy-start | bytes 2359300
  94.6 5.2 %copy-start = (bf16[1,1,96,12384]{3,2,1,0:T(8,128)(2,1)S(1)}, bf16[1,1,96,12384]{3,2,1,0:T(8,128)(2,1)}, u32[]{:S(2)}) copy-start(bf16[1,1,96,12384]{3,2,1,0:T(8,128)(2,1)} %off_ref.1) | copy-start | bytes 7133188
  100.4 9.6 %collective-permute-start = (bf16[96,256]{1,0:T(8,128)(2,1)S(1)}, bf16[96,256]{1,0:T(8,128)(2,1)S(1)}, u32[]{:S(2)}, u32[]{:S(2)}) collective-permute-start(bf16[96,256]{1,0:T(8,128)(2,1)S(1)} %slice.351), channel_id=1, source_target_pairs={{0,16},{16,0},{32,48},{48,32},{64,80},{80,64},{96,112},{112,96},{1... | collective-permute-start | bytes 147464 | tf_op jit(solution)/shard_map/ppermute | solution.py:33
  143.9 7.4 %copy-start.1 = (bf16[1,1,189,1536]{3,2,1,0:T(8,128)(2,1)S(1)}, bf16[1,1,189,1536]{3,2,1,0:T(8,128)(2,1)}, u32[]{:S(2)}) copy-start(bf16[1,1,189,1536]{3,2,1,0:T(8,128)(2,1)} %param.10) | copy-start | bytes 1741828
  143.9 8.1 %collective-permute-start.1 = (bf16[1536,256]{1,0:T(8,128)(2,1)S(1)}, bf16[1536,256]{1,0:T(8,128)(2,1)S(1)}, u32[]{:S(2)}, u32[]{:S(2)}) collective-permute-start(bf16[1536,256]{1,0:T(8,128)(2,1)S(1)} %bitcast.210), channel_id=1, source_target_pairs={{0,16},{16,0},{32,48},{48,32},{64,80},{80,64},{96,112},{112,96},{1... | collective-permute-start | bytes 2359304 | tf_op jit(solution)/shard_map/ppermute | solution.py:33
  192.0 8.1 %collective-permute-start.2 = (bf16[384,256]{1,0:T(8,128)(2,1)S(1)}, bf16[384,256]{1,0:T(8,128)(2,1)S(1)}, u32[]{:S(2)}, u32[]{:S(2)}) collective-permute-start(bf16[384,256]{1,0:T(8,128)(2,1)S(1)} %slice.350), channel_id=1, source_target_pairs={{0,16},{16,0},{32,48},{48,32},{64,80},{80,64},{96,112},{112,96},{1... | collective-permute-start | bytes 589832 | tf_op jit(solution)/shard_map/ppermute | solution.py:33
  220.0 12.5 %all-to-all-start.1 = ((bf16[4,16,16,96]{3,2,1,0:T(8,128)(2,1)}), bf16[4,16,16,96]{3,2,1,0:T(8,128)(2,1)S(1)}, u32[]{:S(2)}, u32[]{:S(2)}) async-start(bf16[4,16,16,96]{3,2,1,0:T(8,128)(2,1)} %broadcast_in_dim.102), calls=%async_computation.1 | async-start | bytes 524288 | tf_op jit(solution)/shard_map/all_to_all | solution.py:43
  235.9 10.5 %all-to-all-start.2 = ((bf16[8,64,96]{2,1,0:T(8,128)(2,1)}), bf16[8,64,96]{2,1,0:T(8,128)(2,1)}, u32[]{:S(2)}, u32[]{:S(2)}) async-start(bf16[8,64,96]{2,1,0:T(8,128)(2,1)} %bitcast.47), calls=%async_computation.2 | async-start | bytes 262144 | tf_op jit(solution)/shard_map/all_to_all | solution.py:43
  248.0 9.4 %all-to-all-start.3 = ((bf16[8,64,96]{2,1,0:T(8,128)(2,1)}), bf16[8,64,96]{2,1,0:T(8,128)(2,1)S(1)}, u32[]{:S(2)}, u32[]{:S(2)}) async-start(bf16[8,64,96]{2,1,0:T(8,128)(2,1)} %broadcast_in_dim.109), calls=%async_computation.3 | async-start | bytes 262144 | tf_op jit(solution)/shard_map/all_to_all | solution.py:43
  260.6 10.5 %all-to-all-start.4 = ((bf16[16,32,96]{2,1,0:T(8,128)(2,1)}), bf16[16,32,96]{2,1,0:T(8,128)(2,1)S(1)}, u32[]{:S(2)}, u32[]{:S(2)}) async-start(bf16[16,32,96]{2,1,0:T(8,128)(2,1)} %fusion.40), calls=%async_computation.4 | async-start | bytes 262144 | tf_op jit(solution)/shard_map/all_to_all | solution.py:43
  271.1 11.8 %copy-start.4 = (bf16[16,32,96]{2,1,0:T(8,128)(2,1)S(1)}, bf16[16,32,96]{2,1,0:T(8,128)(2,1)}, u32[]{:S(2)}) copy-start(bf16[16,32,96]{2,1,0:T(8,128)(2,1)} %get-tuple-element.55) | copy-start | bytes 294916
  271.8 10.2 %all-to-all-start.5 = ((bf16[16,32,96]{2,1,0:T(8,128)(2,1)}), bf16[16,32,96]{2,1,0:T(8,128)(2,1)S(1)}, u32[]{:S(2)}, u32[]{:S(2)}) async-start(bf16[16,32,96]{2,1,0:T(8,128)(2,1)} %broadcast_in_dim.112), calls=%async_computation.5 | async-start | bytes 262144 | tf_op jit(solution)/shard_map/all_to_all | solution.py:43
  282.7 19.8 %copy-start.3 = (bf16[1536,256]{1,0:T(8,128)(2,1)S(1)}, bf16[1536,256]{1,0:T(8,128)(2,1)}, u32[]{:S(2)}) copy-start(bf16[1536,256]{1,0:T(8,128)(2,1)} %copy-done.2) | copy-start | bytes 2359300
  298.6 11.7 %all-to-all-start.7 = ((bf16[32,16,96]{2,1,0:T(8,128)(2,1)}), bf16[32,16,96]{2,1,0:T(8,128)(2,1)S(1)}, u32[]{:S(2)}, u32[]{:S(2)}) async-start(bf16[32,16,96]{2,1,0:T(8,128)(2,1)} %broadcast_in_dim.115), calls=%async_computation.7 | async-start | bytes 262144 | tf_op jit(solution)/shard_map/all_to_all | solution.py:43
  302.9 14.9 %copy-start.6 = (f32[48,256]{1,0:T(8,128)S(1)}, f32[48,256]{1,0:T(8,128)}, u32[]{:S(2)}) copy-start(f32[48,256]{1,0:T(8,128)} %get-tuple-element.58) | copy-start | bytes 147460
  311.9 17.4 %all-to-all-start.8 = ((bf16[16,2,720]{2,1,0:T(2,128)(2,1)}), bf16[16,2,720]{2,1,0:T(2,128)(2,1)S(1)}, u32[]{:S(2)}, u32[]{:S(2)}) async-start(bf16[16,2,720]{2,1,0:T(2,128)(2,1)} %reshape.165), calls=%async_computation.8 | async-start | bytes 98304 | tf_op jit(solution)/shard_map/all_to_all | solution.py:241
Sparse Core Ops, SparseCore 0:
  9.4 85.1 all-gather.5
  96.6 117.9 all-gather.7
